TPU v7x, 512 devices: a whole 4x4x16 slice. The times are simulated.
512 devices in a mesh: band: 16 (over x, y), lon: 32 (over z, core).
Axes of the slice: x: 4, y: 4, z: 16, core: 2. Of those that a mesh axis runs over, the one named last changes fastest.
Arguments:
- back_height: float32 [1024, 8640], P('band', 'lon'), may hold values from -6 to 6
- back_east: float32 [1024, 8640], P('band', 'lon'), may hold values from -6 to 6
- back_north: float32 [1024, 8640], P('band', 'lon'), may hold values from -6 to 6
- obs_values: float32 [65536, 256], P(('band', 'lon')), may hold values from -6 to 6
- obs_owner: int32 [65536, 1], P(('band', 'lon')), may hold values from 0 to 31; in each aligned block of 128 rows (0 to 127, 128 to 255, ...) at most 12 rows name the same one
- obs_row: int32 [65536], P(('band', 'lon')), may hold values from 0 to 63
- obs_count: int32 [65536], P(('band', 'lon')), may hold values from 1 to 256
- polar_mask: int32 [1024], P('band'), may hold values from 0 to 1, as said below
- keep_share: float32 [1024], P('band'), may hold values from 0.05 to 0.9
- depth_level: int32 [1024, 8640], P('band', 'lon'), may hold values from 0 to 50
Outputs:
- grad_height: float32 [1024, 8640], P('band', 'lon')
- grad_east: float32 [1024, 8640], P('band', 'lon')
- grad_north: float32 [1024, 8640], P('band', 'lon')
Inputs may be any that keep to these rules, and one draw needn't show every extreme that they name: `obs_owner`: among the rows of one device at most 12 name the same tile, a bound that some block reaches. `polar_mask`: among the 64 rows of one band at most 32 are 1, and some band has exactly 32.
All inputs are finite; a program needn't handle non-finite values.
Results may differ from a plain program's by a relative error of at most 0.00005.
Values sent between devices are 32-bit elements; how exact they have to be, the bound alone decides.
No kernel may reach another device: no remote copies, remote signals or barrier semaphores. Data moves between devices by JAX's collectives and lax.ppermute only.
A program may use at most 64 MiB of HBM per device.

v0:
```python
import math

import jax
import jax.numpy as jnp
from jax import lax
from jax.sharding import PartitionSpec as P

MODES = 128
LEVELS = 50


COURANT = 0.25
ROTATION = 0.4
LIMIT = 1.3089969389957472
OUTER_COUNT = 64


def with_halo(cells, sides, width, closed):
    for axis, dim in sides:
        count = lax.axis_size(axis)
        ends = count if closed else count - 1
        head = lax.slice_in_dim(cells, 0, width, axis=dim)
        tail = lax.slice_in_dim(cells, cells.shape[dim] - width, cells.shape[dim], axis=dim)
        cells = jnp.concatenate(
            [
                lax.ppermute(tail, axis, [(i, (i + 1) % count) for i in range(ends)]),
                cells,
                lax.ppermute(head, axis, [((i + 1) % count, i) for i in range(ends)]),
            ],
            axis=dim,
        )
    return cells


def latitude_terms(first_row, count_rows, total_rows):
    global_rows = first_row + jnp.arange(count_rows, dtype=jnp.int32)
    centre = (global_rows.astype(jnp.float32) + 0.5) / total_rows
    angle = (2.0 * centre - 1.0) * LIMIT
    return (1.0 / jnp.cos(angle), ROTATION * jnp.sin(angle))


def spectral_tables(length, modes):
    inner_count = length // OUTER_COUNT
    outer_pos = jnp.arange(OUTER_COUNT, dtype=jnp.int32)
    outer_phase = outer_pos[:, None] * outer_pos[None, :] % OUTER_COUNT
    outer_angle = outer_phase.astype(jnp.float32) * (2.0 * math.pi / OUTER_COUNT)
    number = jnp.arange(modes, dtype=jnp.int32)
    inner_pos = jnp.arange(inner_count, dtype=jnp.int32)
    inner_phase = number[:, None] * inner_pos[None, :] % length
    inner_angle = inner_phase.astype(jnp.float32) * (2.0 * math.pi / length)
    grouping = (number[:, None] % OUTER_COUNT == outer_pos[None, :]).astype(jnp.float32)
    mode_weights = jnp.where(number == 0, 1.0 / length, 2.0 / length).astype(jnp.float32)
    return (
        jnp.cos(outer_angle),
        jnp.sin(outer_angle),
        jnp.cos(inner_angle),
        jnp.sin(inner_angle),
        grouping,
        mode_weights,
    )


def project_rows(pieces, tables):
    cos_outer, sin_outer, cos_inner, sin_inner, grouping, mode_weights = tables
    fields, rows, length = pieces.shape
    inner_count = length // OUTER_COUNT
    highest = lax.Precision.HIGHEST
    split = pieces.reshape(fields, rows, OUTER_COUNT, inner_count)
    real_part = jnp.einsum("fnab,ar->fnrb", split, cos_outer, precision=highest)
    imag_part = -jnp.einsum("fnab,ar->fnrb", split, sin_outer, precision=highest)
    real_mode = jnp.einsum("fnrb,mr->fnmb", real_part, grouping, precision=highest)
    imag_mode = jnp.einsum("fnrb,mr->fnmb", imag_part, grouping, precision=highest)
    coeff_real = jnp.sum(real_mode * cos_inner + imag_mode * sin_inner, axis=3) * mode_weights
    coeff_imag = jnp.sum(imag_mode * cos_inner - real_mode * sin_inner, axis=3) * mode_weights
    back_real = coeff_real[..., None] * cos_inner - coeff_imag[..., None] * sin_inner
    back_imag = coeff_real[..., None] * sin_inner + coeff_imag[..., None] * cos_inner
    group_real = jnp.einsum("fnmb,mr->fnrb", back_real, grouping, precision=highest)
    group_imag = jnp.einsum("fnmb,mr->fnrb", back_imag, grouping, precision=highest)
    result = jnp.einsum("fnrb,ar->fnab", group_real, cos_outer, precision=highest) - jnp.einsum(
        "fnrb,ar->fnab", group_imag, sin_outer, precision=highest
    )
    return result.reshape(fields, rows, length)


def extend(stacked, width):
    wider = with_halo(stacked, (("lon", 2),), width, True)
    return with_halo(wider, (("band", 1),), width, False)


def polar_filter(stacked, weight, tables):
    smooth = project_rows(
        lax.all_to_all(stacked, "lon", split_axis=1, concat_axis=2, tiled=True), tables
    )
    projected = lax.all_to_all(smooth, "lon", split_axis=2, concat_axis=1, tiled=True)
    return stacked + weight[None, :, None] * (projected - stacked)


def adjoint_step(state, weight, tables, wet_cells, depth_share, metric, rotation):
    stacked = jnp.stack([state[0], wet_cells * state[1], wet_cells * state[2]])
    kept = polar_filter(stacked, weight, tables)
    height_kept = kept[0]
    east_kept = kept[1]
    north_kept = kept[2]
    wider = extend(kept[1:], 1)
    middle = height_kept + COURANT * (
        metric[:, None] * (wider[0, 1:-1, 2:] - wider[0, 1:-1, :-2]) * 0.5
        + (wider[1, 2:, 1:-1] - wider[1, :-2, 1:-1]) * 0.5
    )
    beside_all = extend(middle[None], 1)[0]
    new_east = (
        east_kept
        - rotation[:, None] * north_kept
        + COURANT
        * depth_share
        * (metric[:, None] * (beside_all[1:-1, 2:] - beside_all[1:-1, :-2]) * 0.5)
    )
    new_north = (
        north_kept
        + rotation[:, None] * east_kept
        + COURANT * depth_share * ((beside_all[2:, 1:-1] - beside_all[:-2, 1:-1]) * 0.5)
    )
    return (middle, new_east, new_north)


def place_observations(
    obs_values, obs_owner, obs_row, obs_count, lon_count, count_rows, count_cols
):
    sample_rows, sample_width = obs_values.shape
    capacity = 3 * sample_rows // lon_count
    owner_ids = obs_owner[:, 0]
    owner_hits = (owner_ids[:, None] == jnp.arange(lon_count, dtype=jnp.int32)[None, :]).astype(
        jnp.int32
    )
    arrival = jnp.sum((jnp.cumsum(owner_hits, axis=0) - 1) * owner_hits, axis=1)
    target = owner_ids * capacity + arrival
    outgoing = (
        jnp.zeros((lon_count * capacity, sample_width), jnp.float32).at[target].set(obs_values)
    )
    labels = (
        jnp.zeros((lon_count * capacity, 2), jnp.int32)
        .at[target]
        .set(jnp.stack([obs_row, obs_count], axis=1))
    )
    incoming, tagged = (
        lax.all_to_all(
            outgoing.reshape(lon_count, capacity, sample_width),
            "lon",
            split_axis=0,
            concat_axis=0,
            tiled=True,
        ),
        lax.all_to_all(
            labels.reshape(lon_count, capacity, 2), "lon", split_axis=0, concat_axis=0, tiled=True
        ),
    )
    flat_values = incoming.reshape(lon_count * capacity, sample_width)
    flat_labels = tagged.reshape(lon_count * capacity, 2)
    alive_cells = jnp.arange(sample_width, dtype=jnp.int32)[None, :] < flat_labels[:, 1:2]
    summed = jax.ops.segment_sum(
        jnp.where(alive_cells, flat_values, 0.0), flat_labels[:, 0], num_segments=count_rows
    )
    return jnp.pad(summed, ((0, 0), (0, count_cols - sample_width)))


def on_device(
    back_height,
    back_east,
    back_north,
    obs_values,
    obs_owner,
    obs_row,
    obs_count,
    polar_mask,
    keep_share,
    depth_level,
):
    count_rows, count_cols = back_height.shape
    band_count = lax.axis_size("band")
    lon_count = lax.axis_size("lon")
    total_rows = count_rows * band_count
    first_row = lax.axis_index("band") * count_rows
    metric, rotation = latitude_terms(first_row, count_rows, total_rows)
    wet_cells = (depth_level > 0).astype(jnp.float32)
    depth_share = depth_level.astype(jnp.float32) / LEVELS
    weight = polar_mask.astype(jnp.float32) * (1.0 - keep_share)
    tables = spectral_tables(count_cols * lon_count, MODES)
    placed = place_observations(
        obs_values, obs_owner, obs_row, obs_count, lon_count, count_rows, count_cols
    )
    state = (back_height, back_east, back_north)
    state = adjoint_step(state, weight, tables, wet_cells, depth_share, metric, rotation)
    state = (state[0] + placed, state[1], state[2])
    state = adjoint_step(state, weight, tables, wet_cells, depth_share, metric, rotation)
    return (state[0], state[1], state[2])


def solution(mesh):
    placed = (
        P("band", "lon"),
        P("band", "lon"),
        P("band", "lon"),
        P(("band", "lon"), None),
        P(("band", "lon"), None),
        P(("band", "lon")),
        P(("band", "lon")),
        P("band"),
        P("band"),
        P("band", "lon"),
    )
    return jax.shard_map(
        on_device,
        mesh=mesh,
        in_specs=placed,
        out_specs=(P("band", "lon"), P("band", "lon"), P("band", "lon")),
        check_vma=False,
    )
```

profile of v0, /device:TPU:24, one launch (start us, length us, event | category | flops | bytes accessed | tf_op | source)
XLA Modules:
  0.0 317.1 jit_solution(5938740981193499104)
XLA Ops:
  3.5 15.5 %all-to-all-start = ((f32[3,64,270]{2,0,1:T(4,128)}), f32[3,64,270]{2,0,1:T(4,128)S(1)}, u32[]{:S(2)}, u32[]{:S(2)}) async-start(f32[3,64,270]{2,0,1:T(4,128)} %copy.81), calls=%async_computation | async-start | bytes 786432 | tf_op jit(solution)/shard_map/all_to_all | solution.py:92
  24.3 22.9 %all-to-all-done = f32[3,64,270]{2,0,1:T(4,128)S(1)} async-done(((f32[3,64,270]{2,0,1:T(4,128)}), f32[3,64,270]{2,0,1:T(4,128)S(1)}, u32[]{:S(2)}, u32[]{:S(2)}) %all-to-all-start) | async-done | bytes 207392 | tf_op jit(solution)/shard_map/all_to_all | solution.py:92
  47.2 3.9 %all-to-all-start.2 = ((s32[32,12,2]{1,2,0:T(2,128)}), s32[32,12,2]{1,2,0:T(2,128)S(1)}, u32[]{:S(2)}, u32[]{:S(2)}) async-start(s32[32,12,2]{1,2,0:T(2,128)} %copy.89), calls=%async_computation.2 | async-start | bytes 65536 | tf_op jit(solution)/shard_map/all_to_all | solution.py:152
  56.3 11.0 %copy.106 = f32[3,2,64,135]{0,1,3,2:T(2,128)} copy(f32[3,2,64,135]{3,2,1,0:T(8,128)S(1)} %fusion.2) | data formatting | bytes 414720 | tf_op jit(solution)/shard_map/reshape | solution.py:82
  67.3 11.7 %reshape.177 = f32[32,1,1620]{2,1,0:T(1,128)} reshape(f32[8640,2,3]{2,1,0:T(2,128)} %bitcast.184) | data formatting | bytes 414720
  79.0 12.2 %all-to-all-start.1 = ((f32[32,1,1620]{2,1,0:T(1,128)}), f32[32,1,1620]{2,1,0:T(1,128)S(1)}, u32[]{:S(2)}, u32[]{:S(2)}) async-start(f32[32,1,1620]{2,1,0:T(1,128)} %reshape.177), calls=%async_computation.1 | async-start | bytes 425984 | tf_op jit(solution)/shard_map/all_to_all | solution.py:94
  93.5 18.3 %all-to-all-done.1 = f32[32,1,1620]{2,1,0:T(1,128)S(1)} async-done(((f32[32,1,1620]{2,1,0:T(1,128)}), f32[32,1,1620]{2,1,0:T(1,128)S(1)}, u32[]{:S(2)}, u32[]{:S(2)}) %all-to-all-start.1) | async-done | bytes 207392 | tf_op jit(solution)/shard_map/all_to_all | solution.py:94
  111.9 4.1 %all-to-all-start.3 = ((f32[32,12,256]{2,1,0:T(8,128)}), f32[32,12,256]{2,1,0:T(8,128)S(1)}, u32[]{:S(2)}, u32[]{:S(2)}) async-start(f32[32,12,256]{2,1,0:T(8,128)} %reshape.134), calls=%async_computation.3 | async-start | bytes 1048576 | tf_op jit(solution)/shard_map/all_to_all | solution.py:145
  117.6 8.1 %reshape.178 = f32[8640,2,3]{2,1,0:T(2,128)} reshape(f32[32,1620]{1,0:T(8,128)S(1)} %reduce.8) | data formatting | bytes 414720
  125.7 11.2 %copy.86 = f32[3,2,32,270]{3,1,2,0:T(2,128)S(1)} copy(f32[3,2,32,270]{0,1,3,2:T(2,128)} %bitcast.185) | data formatting | bytes 414720 | tf_op jit(solution)/shard_map/all_to_all | solution.py:94
  141.9 3.1 collective-permute-done.1
  147.8 5.3 %collective-permute-start.3 = (f32[2,1,272]{2,1,0:T(1,128)S(1)}, f32[2,1,272]{2,1,0:T(1,128)S(1)}, u32[]{:S(2)}, u32[]{:S(2)}) collective-permute-start(f32[2,1,272]{2,1,0:T(1,128)S(1)} %get-tuple-element.22), channel_id=1, source_target_pairs={{0,32},{32,64},{64,96},{96,128},{128,160},{160,192},{192,224},{224... | collective-permute-start | bytes 6536 | tf_op jit(solution)/shard_map/ppermute | solution.py:26
  161.0 4.7 %collective-permute-start.6 = (f32[1,1,272]{2,1,0:T(1,128)S(1)}, f32[1,1,272]{2,1,0:T(1,128)S(1)}, u32[]{:S(2)}, u32[]{:S(2)}) collective-permute-start(f32[1,1,272]{2,1,0:T(1,128)S(1)} %get-tuple-element.30), channel_id=1, source_target_pairs={{0,32},{32,64},{64,96},{96,128},{128,160},{160,192},{192,224},{224... | collective-permute-start | bytes 3272 | tf_op jit(solution)/shard_map/ppermute | solution.py:26
  167.7 5.6 %collective-permute-done.7 = f32[1,1,272]{2,1,0:T(1,128)S(1)} collective-permute-done((f32[1,1,272]{2,1,0:T(1,128)S(1)}, f32[1,1,272]{2,1,0:T(1,128)S(1)}, u32[]{:S(2)}, u32[]{:S(2)}) %collective-permute-start.7) | collective-permute-done | bytes 1120 | tf_op jit(solution)/shard_map/ppermute | solution.py:28
  173.8 37.5 %all_to_all.76 = f32[3,64,270]{2,0,1:T(4,128)S(1)} all-to-all(f32[3,64,270]{2,0,1:T(4,128)S(1)} %copy.91), channel_id=1, replica_groups=mesh['band'=16,'lon'=32] {'lon'}, dimensions={1} | all-to-all | bytes 414720 | tf_op jit(solution)/shard_map/all_to_all | solution.py:92
  216.5 11.0 %copy.109 = f32[3,2,64,135]{0,1,3,2:T(2,128)} copy(f32[3,2,64,135]{3,2,1,0:T(8,128)S(1)} %fusion) | data formatting | bytes 414720 | tf_op jit(solution)/shard_map/reshape | solution.py:82
  227.5 11.1 %reshape.179 = f32[32,1,1620]{2,1,0:T(1,128)S(1)} reshape(f32[8640,2,3]{2,1,0:T(2,128)} %bitcast.186) | data formatting | bytes 414720
  238.6 23.7 %all_to_all.77 = f32[32,1,1620]{2,1,0:T(1,128)S(1)} all-to-all(f32[32,1,1620]{2,1,0:T(1,128)S(1)} %reshape.179), channel_id=1, replica_groups=mesh['band'=16,'lon'=32] {'lon'}, dimensions={0} | all-to-all | bytes 414720 | tf_op jit(solution)/shard_map/all_to_all | solution.py:94
  263.4 8.1 %reshape.180 = f32[8640,2,3]{2,1,0:T(2,128)} reshape(f32[32,1620]{1,0:T(8,128)S(1)} %reduce.9) | data formatting | bytes 414720
  271.5 11.1 %copy.96 = f32[3,2,32,270]{3,1,2,0:T(2,128)S(1)} copy(f32[3,2,32,270]{0,1,3,2:T(2,128)} %bitcast.187) | data formatting | bytes 414720 | tf_op jit(solution)/shard_map/all_to_all | solution.py:94
  285.0 3.0 collective-permute-done.9
  290.0 6.0 %collective-permute-start.11 = (f32[2,1,272]{2,1,0:T(1,128)S(1)}, f32[2,1,272]{2,1,0:T(1,128)S(1)}, u32[]{:S(2)}, u32[]{:S(2)}) collective-permute-start(f32[2,1,272]{2,1,0:T(1,128)S(1)} %get-tuple-element.20), channel_id=1, source_target_pairs={{0,32},{32,64},{64,96},{96,128},{128,160},{160,192},{192,224},{224... | collective-permute-start | bytes 6536 | tf_op jit(solution)/shard_map/ppermute | solution.py:26
  302.2 6.3 %collective-permute-start.14 = (f32[1,1,272]{2,1,0:T(1,128)S(1)}, f32[1,1,272]{2,1,0:T(1,128)S(1)}, u32[]{:S(2)}, u32[]{:S(2)}) collective-permute-start(f32[1,1,272]{2,1,0:T(1,128)S(1)} %get-tuple-element.28), channel_id=1, source_target_pairs={{0,32},{32,64},{64,96},{96,128},{128,160},{160,192},{192,224},{224... | collective-permute-start | bytes 3272 | tf_op jit(solution)/shard_map/ppermute | solution.py:26
  310.5 5.6 %collective-permute-done.15 = f32[1,1,272]{2,1,0:T(1,128)S(1)} collective-permute-done((f32[1,1,272]{2,1,0:T(1,128)S(1)}, f32[1,1,272]{2,1,0:T(1,128)S(1)}, u32[]{:S(2)}, u32[]{:S(2)}) %collective-permute-start.15) | collective-permute-done | bytes 1120 | tf_op jit(solution)/shard_map/ppermute | solution.py:28
  (108 shorter events, 55.0 us)
Async XLA Ops:
  3.5 43.7 %all-to-all-start = ((f32[3,64,270]{2,0,1:T(4,128)}), f32[3,64,270]{2,0,1:T(4,128)S(1)}, u32[]{:S(2)}, u32[]{:S(2)}) async-start(f32[3,64,270]{2,0,1:T(4,128)} %copy.81), calls=%async_computation | async-start | bytes 786432 | tf_op jit(solution)/shard_map/all_to_all | solution.py:92
  47.2 31.8 %all-to-all-start.2 = ((s32[32,12,2]{1,2,0:T(2,128)}), s32[32,12,2]{1,2,0:T(2,128)S(1)}, u32[]{:S(2)}, u32[]{:S(2)}) async-start(s32[32,12,2]{1,2,0:T(2,128)} %copy.89), calls=%async_computation.2 | async-start | bytes 65536 | tf_op jit(solution)/shard_map/all_to_all | solution.py:152
  56.3 59.6 %copy-start.2 = (f32[64]{0:T(128)S(1)}, f32[64]{0:T(128)}, u32[]{:S(2)}) copy-start(f32[64]{0:T(128)} %param.18) | copy-start | bytes 772
  56.3 59.6 %copy-start.3 = (s32[64]{0:T(128)S(1)}, s32[64]{0:T(128)}, u32[]{:S(2)}) copy-start(s32[64]{0:T(128)} %param.17) | copy-start | bytes 772
  79.0 32.8 %all-to-all-start.1 = ((f32[32,1,1620]{2,1,0:T(1,128)}), f32[32,1,1620]{2,1,0:T(1,128)S(1)}, u32[]{:S(2)}, u32[]{:S(2)}) async-start(f32[32,1,1620]{2,1,0:T(1,128)} %reshape.177), calls=%async_computation.1 | async-start | bytes 425984 | tf_op jit(solution)/shard_map/all_to_all | solution.py:94
  111.9 41.3 %all-to-all-start.3 = ((f32[32,12,256]{2,1,0:T(8,128)}), f32[32,12,256]{2,1,0:T(8,128)S(1)}, u32[]{:S(2)}, u32[]{:S(2)}) async-start(f32[32,12,256]{2,1,0:T(8,128)} %reshape.134), calls=%async_computation.3 | async-start | bytes 1048576 | tf_op jit(solution)/shard_map/all_to_all | solution.py:145
  117.6 19.5 %copy-start.1 = (f32[64,270]{1,0:T(8,128)S(1)}, f32[64,270]{1,0:T(8,128)}, u32[]{:S(2)}) copy-start(f32[64,270]{1,0:T(8,128)} %param.10) | copy-start | bytes 207364
  125.7 47.6 %copy-start = (s32[64,270]{1,0:T(8,128)S(1)}, s32[64,270]{1,0:T(8,128)}, u32[]{:S(2)}) copy-start(s32[64,270]{1,0:T(8,128)} %param.19) | copy-start | bytes 207364
  137.3 4.6 %collective-permute-start = (f32[2,64,1]{2,1,0:T(8,128)S(1)}, f32[2,64,1]{2,1,0:T(8,128)S(1)}, u32[]{:S(2)}, u32[]{:S(2)}) collective-permute-start(f32[2,64,1]{2,1,0:T(8,128)S(1)} %get-tuple-element.26), channel_id=1, source_target_pairs={{1,0},{2,1},{3,2},{4,3},{5,4},{6,5},{7,6},{8,7},{9,8},{10,9},{11,1... | collective-permute-start | bytes 1544 | tf_op jit(solution)/shard_map/ppermute | solution.py:28
  140.0 5.0 %collective-permute-start.1 = (f32[2,64,1]{2,1,0:T(8,128)S(1)}, f32[2,64,1]{2,1,0:T(8,128)S(1)}, u32[]{:S(2)}, u32[]{:S(2)}) collective-permute-start(f32[2,64,1]{2,1,0:T(8,128)S(1)} %get-tuple-element.27), channel_id=1, source_target_pairs={{0,1},{1,2},{2,3},{3,4},{4,5},{5,6},{6,7},{7,8},{8,9},{9,10},{10,1... | collective-permute-start | bytes 1544 | tf_op jit(solution)/shard_map/ppermute | solution.py:26
  145.1 10.8 %collective-permute-start.2 = (f32[2,1,272]{2,1,0:T(1,128)S(1)}, f32[2,1,272]{2,1,0:T(1,128)S(1)}, u32[]{:S(2)}, u32[]{:S(2)}) collective-permute-start(f32[2,1,272]{2,1,0:T(1,128)S(1)} %get-tuple-element.21), channel_id=1, source_target_pairs={{32,0},{64,32},{96,64},{128,96},{160,128},{192,160},{224,192},{256... | collective-permute-start | bytes 6536 | tf_op jit(solution)/shard_map/ppermute | solution.py:28
  147.8 8.2 %collective-permute-start.3 = (f32[2,1,272]{2,1,0:T(1,128)S(1)}, f32[2,1,272]{2,1,0:T(1,128)S(1)}, u32[]{:S(2)}, u32[]{:S(2)}) collective-permute-start(f32[2,1,272]{2,1,0:T(1,128)S(1)} %get-tuple-element.22), channel_id=1, source_target_pairs={{0,32},{32,64},{64,96},{96,128},{128,160},{160,192},{192,224},{224... | collective-permute-start | bytes 6536 | tf_op jit(solution)/shard_map/ppermute | solution.py:26
  156.3 4.6 %collective-permute-start.4 = (f32[1,64,1]{2,1,0:T(8,128)S(1)}, f32[1,64,1]{2,1,0:T(8,128)S(1)}, u32[]{:S(2)}, u32[]{:S(2)}) collective-permute-start(f32[1,64,1]{2,1,0:T(8,128)S(1)} %get-tuple-element.34), channel_id=1, source_target_pairs={{0,1},{1,2},{2,3},{3,4},{4,5},{5,6},{6,7},{7,8},{8,9},{9,10},{10,1... | collective-permute-start | bytes 776 | tf_op jit(solution)/shard_map/ppermute | solution.py:26
  156.3 4.6 %collective-permute-start.5 = (f32[1,64,1]{2,1,0:T(8,128)S(1)}, f32[1,64,1]{2,1,0:T(8,128)S(1)}, u32[]{:S(2)}, u32[]{:S(2)}) collective-permute-start(f32[1,64,1]{2,1,0:T(8,128)S(1)} %get-tuple-element.35), channel_id=1, source_target_pairs={{1,0},{2,1},{3,2},{4,3},{5,4},{6,5},{7,6},{8,7},{9,8},{10,9},{11,1... | collective-permute-start | bytes 776 | tf_op jit(solution)/shard_map/ppermute | solution.py:28
  161.0 6.7 %collective-permute-start.6 = (f32[1,1,272]{2,1,0:T(1,128)S(1)}, f32[1,1,272]{2,1,0:T(1,128)S(1)}, u32[]{:S(2)}, u32[]{:S(2)}) collective-permute-start(f32[1,1,272]{2,1,0:T(1,128)S(1)} %get-tuple-element.30), channel_id=1, source_target_pairs={{0,32},{32,64},{64,96},{96,128},{128,160},{160,192},{192,224},{224... | collective-permute-start | bytes 3272 | tf_op jit(solution)/shard_map/ppermute | solution.py:26
  165.7 7.6 %collective-permute-start.7 = (f32[1,1,272]{2,1,0:T(1,128)S(1)}, f32[1,1,272]{2,1,0:T(1,128)S(1)}, u32[]{:S(2)}, u32[]{:S(2)}) collective-permute-start(f32[1,1,272]{2,1,0:T(1,128)S(1)} %get-tuple-element.31), channel_id=1, source_target_pairs={{32,0},{64,32},{96,64},{128,96},{160,128},{192,160},{224,192},{256... | collective-permute-start | bytes 3272 | tf_op jit(solution)/shard_map/ppermute | solution.py:28
  283.1 1.9 collective-permute-start.8
  283.1 4.9 %collective-permute-start.9 = (f32[2,64,1]{2,1,0:T(8,128)S(1)}, f32[2,64,1]{2,1,0:T(8,128)S(1)}, u32[]{:S(2)}, u32[]{:S(2)}) collective-permute-start(f32[2,64,1]{2,1,0:T(8,128)S(1)} %get-tuple-element.25), channel_id=1, source_target_pairs={{0,1},{1,2},{2,3},{3,4},{4,5},{5,6},{6,7},{7,8},{8,9},{9,10},{10,1... | collective-permute-start | bytes 1544 | tf_op jit(solution)/shard_map/ppermute | solution.py:26
  288.1 8.0 %collective-permute-start.10 = (f32[2,1,272]{2,1,0:T(1,128)S(1)}, f32[2,1,272]{2,1,0:T(1,128)S(1)}, u32[]{:S(2)}, u32[]{:S(2)}) collective-permute-start(f32[2,1,272]{2,1,0:T(1,128)S(1)} %get-tuple-element.19), channel_id=1, source_target_pairs={{32,0},{64,32},{96,64},{128,96},{160,128},{192,160},{224,192},{256... | collective-permute-start | bytes 6536 | tf_op jit(solution)/shard_map/ppermute | solution.py:28
  290.0 7.3 %collective-permute-start.11 = (f32[2,1,272]{2,1,0:T(1,128)S(1)}, f32[2,1,272]{2,1,0:T(1,128)S(1)}, u32[]{:S(2)}, u32[]{:S(2)}) collective-permute-start(f32[2,1,272]{2,1,0:T(1,128)S(1)} %get-tuple-element.20), channel_id=1, source_target_pairs={{0,32},{32,64},{64,96},{96,128},{128,160},{160,192},{192,224},{224... | collective-permute-start | bytes 6536 | tf_op jit(solution)/shard_map/ppermute | solution.py:26
  297.6 4.6 %collective-permute-start.12 = (f32[1,64,1]{2,1,0:T(8,128)S(1)}, f32[1,64,1]{2,1,0:T(8,128)S(1)}, u32[]{:S(2)}, u32[]{:S(2)}) collective-permute-start(f32[1,64,1]{2,1,0:T(8,128)S(1)} %get-tuple-element.32), channel_id=1, source_target_pairs={{0,1},{1,2},{2,3},{3,4},{4,5},{5,6},{6,7},{7,8},{8,9},{9,10},{10,1... | collective-permute-start | bytes 776 | tf_op jit(solution)/shard_map/ppermute | solution.py:26
  297.6 4.6 %collective-permute-start.13 = (f32[1,64,1]{2,1,0:T(8,128)S(1)}, f32[1,64,1]{2,1,0:T(8,128)S(1)}, u32[]{:S(2)}, u32[]{:S(2)}) collective-permute-start(f32[1,64,1]{2,1,0:T(8,128)S(1)} %get-tuple-element.33), channel_id=1, source_target_pairs={{1,0},{2,1},{3,2},{4,3},{5,4},{6,5},{7,6},{8,7},{9,8},{10,9},{11,1... | collective-permute-start | bytes 776 | tf_op jit(solution)/shard_map/ppermute | solution.py:28
  302.2 8.2 %collective-permute-start.14 = (f32[1,1,272]{2,1,0:T(1,128)S(1)}, f32[1,1,272]{2,1,0:T(1,128)S(1)}, u32[]{:S(2)}, u32[]{:S(2)}) collective-permute-start(f32[1,1,272]{2,1,0:T(1,128)S(1)} %get-tuple-element.28), channel_id=1, source_target_pairs={{0,32},{32,64},{64,96},{96,128},{128,160},{160,192},{192,224},{224... | collective-permute-start | bytes 3272 | tf_op jit(solution)/shard_map/ppermute | solution.py:26
  308.5 7.6 %collective-permute-start.15 = (f32[1,1,272]{2,1,0:T(1,128)S(1)}, f32[1,1,272]{2,1,0:T(1,128)S(1)}, u32[]{:S(2)}, u32[]{:S(2)}) collective-permute-start(f32[1,1,272]{2,1,0:T(1,128)S(1)} %get-tuple-element.29), channel_id=1, source_target_pairs={{32,0},{64,32},{96,64},{128,96},{160,128},{192,160},{224,192},{256... | collective-permute-start | bytes 3272 | tf_op jit(solution)/shard_map/ppermute | solution.py:28
where the time goes:
time: 318 us; the launch traced here: 317 us
  local copies, waits for them, and re-layouts  90.5 us (28%)
  starting transfers between devices  75.4 us (24%)
  waiting for transfers between devices  66.2 us (21%)
  blocking collectives  61.2 us (19%)
  other arithmetic  12.7 us (4%)
  matrix products  9.91 us (3%)
    unnamed x12, local copies, waits for them, and re-layouts  39 us
    all_to_all x1, blocking collectives, polar_filter(): lax.all_to_all(stacked, 'lon', split_axis=1, concat_axis=2, tiled=True)  37.5 us
    all_to_all x1, blocking collectives, polar_filter(): lax.all_to_all(smooth, 'lon', split_axis=2, concat_axis=1, tiled=True)  23.7 us
    all_to_all x5, local copies, waits for them, and re-layouts, polar_filter(): lax.all_to_all(smooth, 'lon', split_axis=2, concat_axis=1, tiled=True)  23.3 us
    all_to_all x1, waiting for transfers between devices, polar_filter(): lax.all_to_all(stacked, 'lon', split_axis=1, concat_axis=2, tiled=True)  22.9 us
    ppermute x8, starting transfers between devices, with_halo(): lax.ppermute(tail, axis, [(i, (i + 1) % count) for i in range(ends)])  22.8 us
    reshape x2, local copies, waits for them, and re-layouts, project_rows(): return result.reshape(fields, rows, length)  22 us
    all_to_all x1, waiting for transfers between devices, polar_filter(): lax.all_to_all(smooth, 'lon', split_axis=2, concat_axis=1, tiled=True)  18.3 us
  transfers between devices with their start and end apart: 20, of which 11 were waited for; matrix products, arithmetic and copies ran while one was open for 19% of the time, Pallas kernels for 0%

commit v1 on v0

v1 whole, which is shorter than its diff:
```python
import math

import jax
import jax.numpy as jnp
import numpy as np
from jax import lax
from jax.experimental import pallas as pl
from jax.experimental.pallas import tpu as pltpu
from jax.sharding import PartitionSpec as P

MODES = 128
LEVELS = 50
COURANT = 0.25
ROTATION = 0.4
LIMIT = 1.3089969389957472
CAP = 12
LANES = 384
GRID = 512
HALO = 4
F32 = jnp.float32


def hdot(left, right):
    return jnp.dot(left, right, precision=lax.Precision.HIGHEST, preferred_element_type=F32)


def iota(shape, dim):
    return lax.broadcasted_iota(jnp.int32, shape, dim)


def to_col(row):
    size = row.shape[1]
    same = iota((size, size), 0) == iota((size, size), 1)
    return jnp.sum(jnp.where(same, row, jnp.zeros_like(row)), axis=1, keepdims=True)


def to_row(col):
    size = col.shape[0]
    same = iota((size, size), 0) == iota((size, size), 1)
    return jnp.sum(jnp.where(same, col, jnp.zeros_like(col)), axis=0, keepdims=True)


def lon_diff(field):
    width = field.shape[1]
    return 0.5 * (pltpu.roll(field, width - 1, 1) - pltpu.roll(field, 1, 1))


def lat_diff(field):
    rows = field.shape[0]
    return 0.5 * (pltpu.roll(field, rows - 1, 0) - pltpu.roll(field, 1, 0))


def rank_in_row(mask_row):
    size = mask_row.shape[1]
    before = iota((size, size), 0) < iota((size, size), 1)
    return jnp.sum(jnp.where(before, to_col(mask_row), 0), axis=0, keepdims=True)


def slot_rows(mask_row, core, devices):
    rows = mask_row.shape[1]
    half = devices // 2
    line = iota((devices, rows), 0)
    near = (line < half).astype(jnp.int32)
    place = jnp.where(line < half, line, line - half)
    slot = 2 * place + near * core + (1 - near) * (1 - core)
    hit = (slot == rank_in_row(mask_row)) & (mask_row == 1)
    return hit.astype(F32)


def pack_lon(h_ref, e_ref, n_ref, d_ref, fields_ref, west_ref, east_ref):
    cols = h_ref.shape[1]
    level = d_ref[...].astype(F32)
    wet = (level > 0).astype(F32)
    values = (h_ref[...], wet * e_ref[...], wet * n_ref[...], level)
    lane = iota((h_ref.shape[0], 128), 1)
    west = jnp.zeros(lane.shape, F32)
    east = jnp.zeros(lane.shape, F32)
    last = cols - HALO - 256
    fields_ref[...] = jnp.zeros(fields_ref.shape, F32)
    for f, value in enumerate(values):
        fields_ref[f, :, 0:cols] = value
        inside = (lane >= HALO * f) & (lane < HALO * f + HALO)
        head = fields_ref[f, :, 0:128]
        tail = fields_ref[f, :, 256:384]
        if f:
            head = pltpu.roll(head, HALO * f, 1)
        west = jnp.where(inside, head, west)
        east = jnp.where(inside, pltpu.roll(tail, (HALO * f - last) % 128, 1), east)
    west_ref[...] = west
    east_ref[...] = east


def third_tile(tail, left, right, f, cols):
    lane = iota(tail.shape, 1)
    first = cols - 256
    shifted = pltpu.roll(right, (first - HALO * f) % 128, 1)
    tail = jnp.where((lane >= first) & (lane < first + HALO), shifted, tail)
    shifted = pltpu.roll(left, (128 - HALO - HALO * f) % 128, 1)
    return jnp.where(lane >= 128 - HALO, shifted, tail)


WEIGHT_LANE = 300 - 256


def pack_lat(cols, fields_ref, left_ref, right_ref, mask_ref, keep_ref, north_ref, south_ref):
    rows = fields_ref.shape[1]
    weight = to_col(mask_ref[...].astype(F32) * (1.0 - keep_ref[...]))
    for f in range(4):
        for out_ref, at in ((north_ref, 0), (south_ref, rows - HALO)):
            span = slice(at, at + HALO)
            tail = third_tile(
                fields_ref[f, span, 256:384], left_ref[span, :], right_ref[span, :], f, cols
            )
            if f == 3:
                tail = jnp.where(iota(tail.shape, 1) == WEIGHT_LANE, weight[span, :], tail)
            out_ref[HALO * f : HALO * f + HALO, 0:256] = fields_ref[f, span, 0:256]
            out_ref[HALO * f : HALO * f + HALO, 256:384] = tail


def row_terms(terms, band):
    lane = iota(terms.shape, 1)
    return [
        jnp.sum(jnp.where(lane == band + 16 * i, terms, 0.0), axis=1, keepdims=True)
        for i in range(3)
    ]


def partial_sums(
    cols,
    place_ref,
    fields_ref,
    left_ref,
    right_ref,
    above_ref,
    below_ref,
    mask_ref,
    keep_ref,
    terms_ref,
    cos_ref,
    sin_ref,
    table_ref,
    kernel_ref,
    placed_ref,
    ext_ref,
    weight_ref,
    mine_ref,
    other_ref,
    stack_ref,
    cells_ref,
):
    rows = fields_ref.shape[1]
    ext = rows + 2 * HALO
    devices = cos_ref.shape[0]
    half = devices // 2
    band, lon = place_ref[0], place_ref[1]
    core = lon % 2
    for f in range(4):
        ext_ref[f, 0:rows, 0:256] = fields_ref[f, :, 0:256]
        ext_ref[f, 0:rows, 256:384] = third_tile(
            fields_ref[f, :, 256:384], left_ref[...], right_ref[...], f, cols
        )
        ext_ref[f, rows : rows + HALO, :] = below_ref[HALO * f : HALO * f + HALO, :]
        ext_ref[f, rows + HALO : ext, :] = above_ref[HALO * f : HALO * f + HALO, :]
    edge = ext_ref[3, rows:ext, 256:384]
    marked = iota(edge.shape, 1) == WEIGHT_LANE
    mask = mask_ref[...]
    weight_ref[0:rows, :] = jnp.broadcast_to(
        to_col(mask.astype(F32) * (1.0 - keep_ref[...])), (rows, 128)
    )
    weight_ref[rows:ext, :] = jnp.broadcast_to(
        jnp.sum(jnp.where(marked, edge, 0.0), axis=1, keepdims=True), (2 * HALO, 128)
    )
    ext_ref[3, rows:ext, 256:384] = jnp.where(marked, 0.0, edge)
    weight = weight_ref[:, 0:1]
    rest = 1.0 - weight
    metric, rotation, valid = row_terms(terms_ref[...], band)
    metric = metric * valid
    height, east, north = ext_ref[0], ext_ref[1], ext_ref[2]
    share = ext_ref[3] / LEVELS
    low_height = weight * height + COURANT * (
        metric * lon_diff(weight * east) + lat_diff(weight * north)
    )
    low_height = valid * low_height
    east_rest, north_rest = rest * east, rest * north
    middle = valid * (
        rest * height + COURANT * (metric * lon_diff(east_rest) + lat_diff(north_rest))
    )
    new_east = east_rest - rotation * north_rest + COURANT * share * metric * lon_diff(middle)
    new_north = north_rest + rotation * east_rest + COURANT * share * lat_diff(middle)
    chosen = slot_rows(mask, core, devices)
    sources = (height, east, north, low_height, lat_diff(low_height), middle, new_east, new_north)
    for v, field in enumerate(sources):
        stack_ref[devices * v : devices * v + devices, :] = hdot(chosen, field[0:rows, :])
    level = ext_ref[3, 0:rows, :]
    cells_ref[0:devices, :] = hdot(chosen, (level > 0).astype(F32))
    cells_ref[devices : 2 * devices, :] = hdot(chosen, share[0:rows, :])
    sums = hdot(stack_ref[...], table_ref[...])
    turn_cos, turn_sin = cos_ref[pl.ds(lon, 1), :], sin_ref[pl.ds(lon, 1), :]
    for v in range(len(sources)):
        lines = slice(devices * v, devices * v + devices)
        on_cos, on_sin = sums[lines, 0:128], sums[lines, 128:256]
        all_cos = on_cos * turn_cos - on_sin * turn_sin
        all_sin = on_sin * turn_cos + on_cos * turn_sin
        if v == 5:
            all_cos = all_cos + placed_ref[:, 0:128]
            all_sin = all_sin + placed_ref[:, 128:256]
        for i, value in enumerate((all_cos, all_sin)):
            mine_ref[:, 2 * v + i, :] = value[0:half]
            other_ref[:, 2 * v + i, :] = value[half:devices]
    spread = pltpu.roll(hdot(cells_ref[...], kernel_ref[...]), lon * (GRID // devices), 1)
    for c in range(2):
        for i in range(4):
            part = spread[devices * c : devices * c + devices, 128 * i : 128 * i + 128]
            at = 16 + 4 * c + i
            mine_ref[:, at, :] = part[0:half]
            other_ref[:, at, :] = part[half:devices]


def pack_observations(
    place_ref,
    values_ref,
    owner_ref,
    row_ref,
    count_ref,
    mask_ref,
    cos_ref,
    sin_ref,
    table_ref,
    out_ref,
    placed_ref,
):
    number, width = values_ref.shape
    devices = cos_ref.shape[0]
    core = place_ref[1] % 2
    values = jnp.where(
        iota((number, width), 1) < to_col(count_ref[...]), values_ref[...], 0.0
    )
    owner_col = owner_ref[...]
    owner_row = to_row(owner_col)
    same = owner_col == owner_row
    before = same & (iota((number, number), 0) < iota((number, number), 1))
    arrival_row = jnp.sum(before.astype(jnp.int32), axis=0, keepdims=True)
    after = same & (iota((number, number), 0) > iota((number, number), 1))
    arrival_col = jnp.sum(after.astype(jnp.int32), axis=1, keepdims=True)
    target = owner_row * 16 + arrival_row
    sent = (iota((16 * devices, number), 0) == target).astype(F32)
    out_ref[...] = hdot(sent, values).reshape(devices, 16, width)
    named = (iota((devices, number), 0) == owner_row).astype(F32) * row_ref[...].astype(F32)
    lines = hdot(named, (iota((number, width), 1) == arrival_col).astype(F32))
    out_ref[:, CAP, :] = lines
    sums = hdot(values, table_ref[0:width, :])
    whose = (iota((number, devices), 1) == owner_col).astype(F32)
    turn_cos, turn_sin = hdot(whose, cos_ref[...]), hdot(whose, sin_ref[...])
    on_cos, on_sin = sums[:, 0:128], sums[:, 128:256]
    all_cos = on_cos * turn_cos - on_sin * turn_sin
    all_sin = on_sin * turn_cos + on_cos * turn_sin
    mask = mask_ref[...]
    rows = mask.shape[1]
    in_row = (iota((rows, number), 0) == row_ref[...]).astype(F32)
    chosen = hdot(slot_rows(mask, core, devices), in_row)
    placed_ref[:, 0:128] = hdot(chosen, all_cos)
    placed_ref[:, 128:256] = hdot(chosen, all_sin)


def unpack_observations(in_ref, dep_ref, edge_ref):
    devices, lines, width = in_ref.shape
    rows = dep_ref.shape[0]
    total = devices * lines
    labels = in_ref[:, CAP, 0:128]
    across = hdot(labels, (iota((128, total), 1) % lines == iota((128, total), 0)).astype(F32))
    own = iota((devices, total), 1) // lines == iota((devices, total), 0)
    label_row = jnp.sum(jnp.where(own, across, 0.0), axis=0, keepdims=True)
    line = iota((rows, total), 1) % lines
    hit = (iota((rows, total), 0).astype(F32) == label_row) & (line < CAP)
    summed = hdot(hit.astype(F32), in_ref[...].reshape(total, width))
    dep_ref[:, 0:256] = summed
    dep_ref[:, 256:384] = jnp.zeros((rows, 128), F32)
    edge_ref[...] = pltpu.roll(summed[:, 0:128], 14, 1)


def own_row(
    place_ref,
    in_ref,
    mask_ref,
    keep_ref,
    lines_ref,
    slope_ref,
    to_grid_ref,
    from_grid_ref,
    out_ref,
    left_ref,
    grid_ref,
    res_ref,
):
    band, lon = place_ref[0], place_ref[1]
    sums = in_ref[0]
    for i in range(1, in_ref.shape[0]):
        sums = sums + in_ref[i]
    mask = mask_ref[...]
    chosen = ((rank_in_row(mask) == lon) & (mask == 1)).astype(F32)

    def pick(row):
        return jnp.sum(chosen * row, axis=1, keepdims=True)

    rows = mask.shape[1]
    weight = pick(1.0 - keep_ref[...])
    both = lines_ref[pl.ds(band, 1), :]
    metric = pick(both[:, 0:rows])
    rotation = pick(both[:, 128 : 128 + rows])

    def line(i):
        return sums[i : i + 1, :]

    slope = slope_ref[0:1, :]
    left_ref[...] = jnp.zeros(left_ref.shape, F32)
    pairs = (
        (weight * (line(2) - rotation * line(4)), weight * (line(3) - rotation * line(5))),
        (metric * slope * line(7), -metric * slope * line(6)),
        (weight * (line(4) + rotation * line(2)), weight * (line(5) + rotation * line(3))),
        (line(8), line(9)),
    )
    for i, (on_cos, on_sin) in enumerate(pairs):
        left_ref[i : i + 1, 0:128] = on_cos
        left_ref[i : i + 1, 128:256] = on_sin
    at = hdot(left_ref[...], to_grid_ref[...])
    wet = jnp.concatenate([line(16), line(17), line(18), line(19)], axis=1)
    share = COURANT * jnp.concatenate([line(20), line(21), line(22), line(23)], axis=1)
    grid_ref[...] = jnp.zeros(grid_ref.shape, F32)
    grid_ref[0:1, :] = wet * at[0:1] + share * at[1:2]
    grid_ref[1:2, :] = wet * at[2:3] + share * at[3:4]
    back = hdot(grid_ref[...], from_grid_ref[...])
    res_ref[...] = jnp.zeros(res_ref.shape, F32)
    res_ref[0:6, :] = sums[0:6]
    res_ref[6:8, :] = sums[10:12] + sums[6:8]
    for i in range(2):
        res_ref[8 + 2 * i : 9 + 2 * i, :] = line(12 + 2 * i) + back[i : i + 1, 0:128]
        res_ref[9 + 2 * i : 10 + 2 * i, :] = line(13 + 2 * i) + back[i : i + 1, 128:256]
    out_ref[...] = jnp.broadcast_to(res_ref[...][None], out_ref.shape)


def band_edges(cols, all_ref, dep_ref, edge_ref, mask_ref, coef_ref, depx_ref, north_ref, south_ref):
    devices = all_ref.shape[0]
    rows = dep_ref.shape[0]
    mask = mask_ref[...]
    rank = to_col(rank_in_row(mask))
    chosen = ((iota((rows, devices), 1) == rank) & (to_col(mask) == 1)).astype(F32)
    first = cols - 256
    lane = iota((rows, 128), 1)
    depx_ref[:, 0:256] = dep_ref[:, 0:256]
    depx_ref[:, 256:384] = jnp.where((lane == first) | (lane == first + 1), edge_ref[...], 0.0)
    for v in range(12):
        own = hdot(chosen, all_ref[:, v, :])
        coef_ref[v] = own
        north_ref[4 * v : 4 * v + 4, :] = own[0:4]
        south_ref[4 * v : 4 * v + 4, :] = own[rows - 4 : rows]
    for out_ref, at in ((north_ref, 0), (south_ref, rows - 2)):
        for r in range(2):
            for t in range(3):
                out_ref[48 + 3 * r + t : 49 + 3 * r + t, :] = depx_ref[
                    at + r : at + r + 1, 128 * t : 128 * t + 128
                ]
        out_ref[54:56, :] = jnp.zeros((2, 128), F32)


def last_stage(
    place_ref,
    ext_ref,
    weight_ref,
    coef_ref,
    depx_ref,
    above_ref,
    below_ref,
    terms_ref,
    cos_ref,
    sin_ref,
    table_ref,
    h_ref,
    e_ref,
    n_ref,
    stack_ref,
    dep_ref,
):
    ext = ext_ref.shape[1]
    rows, cols = h_ref.shape
    band, lon = place_ref[0], place_ref[1]
    turn_cos, turn_sin = cos_ref[pl.ds(lon, 1), :], sin_ref[pl.ds(lon, 1), :]
    for f in range(6):
        for lines, on_cos, on_sin in (
            (slice(ext * f, ext * f + rows), coef_ref[2 * f], coef_ref[2 * f + 1]),
            (
                slice(ext * f + rows, ext * f + rows + 4),
                below_ref[8 * f : 8 * f + 4, :],
                below_ref[8 * f + 4 : 8 * f + 8, :],
            ),
            (
                slice(ext * f + rows + 4, ext * f + ext),
                above_ref[8 * f : 8 * f + 4, :],
                above_ref[8 * f + 4 : 8 * f + 8, :],
            ),
        ):
            stack_ref[lines, 0:128] = on_cos * turn_cos + on_sin * turn_sin
            stack_ref[lines, 128:256] = on_sin * turn_cos - on_cos * turn_sin
    low = hdot(stack_ref[...], table_ref[...])
    dep_ref[0:rows, :] = depx_ref[...]
    dep_ref[rows:ext, :] = jnp.zeros((ext - rows, LANES), F32)
    for in_ref, at in ((below_ref, rows), (above_ref, ext - 2)):
        for r in range(2):
            for t in range(3):
                dep_ref[at + r : at + r + 1, 128 * t : 128 * t + 128] = in_ref[
                    48 + 3 * r + t : 49 + 3 * r + t, :
                ]
    weight = weight_ref[:, 0:1]
    metric, rotation, valid = row_terms(terms_ref[...], band)
    level = ext_ref[3]
    wet = (level > 0).astype(F32)
    share = COURANT * (level / LEVELS)

    def step(height, east, north, f):
        height = height + weight * (low[ext * f : ext * f + ext] - height)
        east = east + weight * (low[ext * f + ext : ext * f + 2 * ext] - east)
        north = north + weight * (low[ext * f + 2 * ext : ext * f + 3 * ext] - north)
        middle = valid * (height + COURANT * (metric * lon_diff(east) + lat_diff(north)))
        new_east = east - rotation * north + share * (metric * lon_diff(middle))
        new_north = north + rotation * east + share * lat_diff(middle)
        return middle, new_east, new_north

    middle, east, north = step(ext_ref[0], ext_ref[1], ext_ref[2], 0)
    middle, east, north = step(middle + dep_ref[...], wet * east, wet * north, 3)
    h_ref[...] = middle[0:rows, 0:cols]
    e_ref[...] = east[0:rows, 0:cols]
    n_ref[...] = north[0:rows, 0:cols]


def tables(length, cols, devices, rows, bands):
    mode = np.arange(MODES)
    norm = np.where(mode == 0, 1.0 / length, 2.0 / length)
    lane = np.arange(LANES)

    def angle(at, number):
        phase = (at[:, None].astype(np.int64) * number[None, :]) % length
        return phase * (2.0 * math.pi / length)

    ahead = angle(lane, mode)
    inside = (lane < cols)[:, None]
    analyse = np.concatenate([np.cos(ahead) * norm, np.sin(ahead) * norm], axis=1) * inside
    place = np.where(lane < LANES - HALO, lane, lane - LANES)
    shown = ((lane < cols + HALO) | (lane >= LANES - HALO))[:, None]
    around = angle(place, mode)
    evaluate = (np.concatenate([np.cos(around), np.sin(around)], axis=1) * shown).T
    wide = np.arange(1, 2 * MODES - 1)
    spot = np.arange(GRID) * (length / GRID)
    gap = spot[None, :] - lane[:, None]
    kernel = np.full((LANES, GRID), 1.0 / length)
    for k in wide:
        kernel += (2.0 / length) * np.cos(2.0 * math.pi / length * k * gap)
    kernel *= inside
    coarse = (np.arange(GRID)[:, None] * mode[None, :]) % GRID * (2.0 * math.pi / GRID)
    to_grid = np.concatenate([np.cos(coarse), np.sin(coarse)], axis=1).T
    part = np.where(mode == 0, 1.0 / GRID, 2.0 / GRID)
    from_grid = np.concatenate([np.cos(coarse) * part, np.sin(coarse) * part], axis=1)
    turn = (np.arange(devices)[:, None] * mode[None, :]) % devices * (2.0 * math.pi / devices)
    slope = np.tile(np.sin(2.0 * math.pi / length * mode)[None, :], (8, 1))
    total = rows * bands
    index = np.arange(rows + 2 * HALO)
    local = np.where(index < rows + HALO, index, index - (rows + 2 * HALO))
    terms = np.zeros((rows + 2 * HALO, 128))
    lines = np.zeros((bands, 256))
    for b in range(bands):
        g = b * rows + local
        phi = (2.0 * ((g + 0.5) / total) - 1.0) * LIMIT
        terms[:, b] = 1.0 / np.cos(phi)
        terms[:, 16 + b] = ROTATION * np.sin(phi)
        terms[:, 32 + b] = (g >= 0) & (g < total)
        lines[b, 0:rows] = terms[0:rows, b]
        lines[b, 128 : 128 + rows] = terms[0:rows, 16 + b]
    made = dict(
        analyse=analyse,
        evaluate=evaluate,
        kernel=kernel,
        to_grid=to_grid,
        from_grid=from_grid,
        cos=np.cos(turn),
        sin=np.sin(turn),
        slope=slope,
        terms=terms,
        lines=lines,
    )
    return {name: value.astype(np.float32) for name, value in made.items()}


VMEM = pl.BlockSpec(memory_space=pltpu.VMEM)
SMEM = pl.BlockSpec(memory_space=pltpu.SMEM)


def call(kernel, name, outs, args, scratch=(), scalars=False):
    shapes = [jax.ShapeDtypeStruct(shape, F32) for shape in outs]
    specs = [SMEM if scalars and i == 0 else VMEM for i in range(len(args))]
    return pl.pallas_call(
        kernel,
        name=name,
        out_shape=shapes,
        in_specs=specs,
        out_specs=[VMEM] * len(shapes),
        scratch_shapes=[pltpu.VMEM(shape, F32) for shape in scratch],
        compiler_params=pltpu.CompilerParams(vmem_limit_bytes=40 * 2**20),
    )(*args)


def on_device(
    back_height,
    back_east,
    back_north,
    obs_values,
    obs_owner,
    obs_row,
    obs_count,
    polar_mask,
    keep_share,
    depth_level,
):
    rows, cols = back_height.shape
    bands, devices = lax.axis_size("band"), lax.axis_size("lon")
    half = devices // 2
    number, width = obs_values.shape
    ext = rows + 2 * HALO
    made = tables(cols * devices, cols, devices, rows, bands)
    place = jnp.stack([lax.axis_index("band"), lax.axis_index("lon")]).astype(jnp.int32)
    mask = polar_mask.reshape(1, rows)
    keep = keep_share.reshape(1, rows)

    def send(value, axis, shift, closed):
        count = lax.axis_size(axis)
        pairs = [(i, (i + shift) % count) for i in range(count) if closed or 0 <= i + shift < count]
        return lax.ppermute(value, axis, pairs)

    fields, west, east = call(
        pack_lon,
        "pack_lon",
        [(4, rows, LANES), (rows, 128), (rows, 128)],
        (back_height, back_east, back_north, depth_level),
    )
    right, left = send(west, "lon", -1, True), send(east, "lon", 1, True)
    outgoing, placed = call(
        pack_observations,
        "pack_observations",
        [(devices, 16, width), (devices, 256)],
        (
            place,
            obs_values,
            obs_owner,
            obs_row.reshape(1, number),
            obs_count.reshape(1, number),
            mask,
            made["cos"],
            made["sin"],
            made["analyse"],
        ),
        scalars=True,
    )
    north, south = call(
        lambda *refs: pack_lat(cols, *refs),
        "pack_lat",
        [(4 * HALO, LANES)] * 2,
        (fields, left, right, mask, keep),
    )
    below, above = send(north, "band", -1, False), send(south, "band", 1, False)
    ext_fields, weight, mine, other = call(
        lambda *refs: partial_sums(cols, *refs),
        "partial_sums",
        [(4, ext, LANES), (ext, 128), (half, 24, 128), (half, 24, 128)],
        (
            place,
            fields,
            left,
            right,
            above,
            below,
            mask,
            keep,
            made["terms"],
            made["cos"],
            made["sin"],
            made["analyse"],
            made["kernel"],
            placed,
        ),
        scratch=[(8 * devices, LANES), (2 * devices, LANES)],
        scalars=True,
    )
    swapped = lax.ppermute(other, "lon", [(i, i ^ 1) for i in range(devices)])
    groups = [[2 * i + c for i in range(half)] for c in range(2)]
    owned = lax.all_to_all(
        mine + swapped, "lon", split_axis=0, concat_axis=0, axis_index_groups=groups, tiled=True
    )
    (spread,) = call(
        own_row,
        "own_row",
        [(devices, 16, 128)],
        (
            place,
            owned,
            mask,
            keep,
            made["lines"],
            made["slope"],
            made["to_grid"],
            made["from_grid"],
        ),
        scratch=[(8, 256), (8, GRID), (16, 128)],
        scalars=True,
    )
    everyone = lax.all_to_all(spread, "lon", split_axis=0, concat_axis=0, tiled=True)
    incoming = lax.all_to_all(outgoing, "lon", split_axis=0, concat_axis=0, tiled=True)
    dep, edge = call(
        unpack_observations, "unpack_observations", [(rows, LANES), (rows, 128)], (incoming,)
    )
    dep_right = send(edge, "lon", -1, True)
    coef, depx, north, south = call(
        lambda *refs: band_edges(cols, *refs),
        "band_edges",
        [(12, rows, 128), (rows, LANES), (56, 128), (56, 128)],
        (everyone, dep, dep_right, mask),
    )
    below, above = send(north, "band", -1, False), send(south, "band", 1, False)
    return tuple(
        call(
            last_stage,
            "last_stage",
            [(rows, cols)] * 3,
            (
                place,
                ext_fields,
                weight,
                coef,
                depx,
                above,
                below,
                made["terms"],
                made["cos"],
                made["sin"],
                made["evaluate"],
            ),
            scratch=[(6 * ext, 256), (ext, LANES)],
            scalars=True,
        )
    )


def solution(mesh):
    placed = (
        P("band", "lon"),
        P("band", "lon"),
        P("band", "lon"),
        P(("band", "lon"), None),
        P(("band", "lon"), None),
        P(("band", "lon")),
        P(("band", "lon")),
        P("band"),
        P("band"),
        P("band", "lon"),
    )
    return jax.shard_map(
        on_device,
        mesh=mesh,
        in_specs=placed,
        out_specs=(P("band", "lon"), P("band", "lon"), P("band", "lon")),
        check_vma=False,
    )
```

time: 318 us -> 144 us (0.45)
  local copies, waits for them, and re-layouts: 90.5 us -> 9.28 us
  starting transfers between devices: 75.4 us -> 37 us
  blocking collectives: 61.2 us -> 24.8 us
  other arithmetic: 12.7 us -> 0.11 us
  Pallas kernels: 0 us -> 11.8 us
  matrix products: 9.91 us -> 0 us
  waiting for transfers between devices: 66.2 us -> 59.5 us
    all_to_all x2 -> x1, blocking collectives: 61.2 us -> 24.8 us  [on_device(): lax.all_to_all(mine + swapped, 'lon', split_axis=0, concat_axis=0, axis_i...]
    unnamed x12 -> x45, local copies, waits for them, and re-layouts: 39 us -> 9.28 us
    all_to_all x4 -> x2, starting transfers between devices: 35.6 us -> 10.3 us  [the longest x1 6.43 us: on_device(): lax.all_to_all(outgoing, 'lon', split_axis=0, concat_axis=0, tiled=True)]
    reshape x9 -> x0, local copies, waits for them, and re-layouts: 24 us -> none  [the longest x2 22 us: project_rows(): return result.reshape(fields, rows, length)]
    all_to_all x8 -> x0, local copies, waits for them, and re-layouts: 23.4 us -> none  [the longest x5 23.3 us: polar_filter(): lax.all_to_all(smooth, 'lon', split_axis=2, concat_axis=1, tiled=True)]
    ppermute x16 -> x8, waiting for transfers between devices: 25 us -> 8.95 us  [the longest x7 7.54 us: send(): return lax.ppermute(value, axis, pairs)]
    ppermute x16 -> x8, starting transfers between devices: 39.8 us -> 26.7 us  [the longest x7 24.7 us: send(): return lax.ppermute(value, axis, pairs)]
    pallas_call x0 -> x8, Pallas kernels: none -> 11.8 us  [call(): pl.pallas_call(kernel, name=name, out_shape=shapes, in_specs=specs, out_s...]
  transfers between devices with their start and end apart: 20 -> 10, of which waited for: 11 -> 5; matrix products, arithmetic and copies ran while one was open for 19% -> 1% of each run, Pallas kernels for 0% -> 4%
where the time goes in v1:
time: 144 us; the launch traced here: 143 us
  waiting for transfers between devices  59.5 us (41%)
  starting transfers between devices  37 us (26%)
  blocking collectives  24.8 us (17%)
  Pallas kernels  11.8 us (8%)
  local copies, waits for them, and re-layouts  9.28 us (6%)
    all_to_all x1, waiting for transfers between devices, on_device(): lax.all_to_all(outgoing, 'lon', split_axis=0, concat_axis=0, tiled=True)  31.2 us
    all_to_all x1, blocking collectives, on_device(): lax.all_to_all(mine + swapped, 'lon', split_axis=0, concat_axis=0, axis_i...  24.8 us
    ppermute x7, starting transfers between devices, send(): return lax.ppermute(value, axis, pairs)  24.7 us
    all_to_all x1, waiting for transfers between devices, on_device(): lax.all_to_all(spread, 'lon', split_axis=0, concat_axis=0, tiled=True)  19.3 us
    pallas_call x8, Pallas kernels, call(): pl.pallas_call(kernel, name=name, out_shape=shapes, in_specs=specs, out_s...  11.8 us
    unnamed x45, local copies, waits for them, and re-layouts  9.28 us
    ppermute x7, waiting for transfers between devices, send(): return lax.ppermute(value, axis, pairs)  7.54 us
    all_to_all x1, starting transfers between devices, on_device(): lax.all_to_all(outgoing, 'lon', split_axis=0, concat_axis=0, tiled=True)  6.43 us
  transfers between devices with their start and end apart: 10, of which 5 were waited for; matrix products, arithmetic and copies ran while one was open for 1% of the time, Pallas kernels for 4%

profile of v1, /device:TPU:24, one launch (start us, length us, event | category | flops | bytes accessed | tf_op | source)
XLA Modules:
  0.0 143.3 jit_solution(7895688103702959886)
XLA Ops:
  0.7 1.0 copy-done.9
  1.7 0.9 copy-done.10
  2.6 0.9 copy-done.11
  3.5 0.9 copy-done.12
  4.5 8.9 %collective-permute-start.1 = (f32[64,128]{1,0:T(8,128)S(1)}, f32[64,128]{1,0:T(8,128)S(1)}, u32[]{:S(2)}, u32[]{:S(2)}) collective-permute-start(f32[64,128]{1,0:T(8,128)S(1)} %get-tuple-element.22), channel_id=1, source_target_pairs={{0,31},{1,0},{2,1},{3,2},{4,3},{5,4},{6,5},{7,6},{8,7},{9,8},{10,9... | collective-permute-start | bytes 98312 | tf_op jit(solution)/shard_map/ppermute | solution.py:534
  13.5 1.6 %collective-permute-done.refs_1_.refs_2_ = f32[64,128]{1,0:T(8,128)S(1)} collective-permute-done((f32[64,128]{1,0:T(8,128)S(1)}, f32[64,128]{1,0:T(8,128)S(1)}, u32[]{:S(2)}, u32[]{:S(2)}) %collective-permute-start) | collective-permute-done | bytes 32800 | tf_op jit(solution)/shard_map/ppermute | solution.py:534
  16.5 3.1 %collective-permute-start.2 = (f32[16,384]{1,0:T(8,128)S(1)}, f32[16,384]{1,0:T(8,128)S(1)}, u32[]{:S(2)}, u32[]{:S(2)}) collective-permute-start(f32[16,384]{1,0:T(8,128)S(1)} %get-tuple-element.23), channel_id=1, source_target_pairs={{0,32},{32,64},{64,96},{96,128},{128,160},{160,192},{192,224},{224... | collective-permute-start | bytes 73736 | tf_op jit(solution)/shard_map/ppermute | solution.py:534
  19.5 2.8 %collective-permute-start.3 = (f32[16,384]{1,0:T(8,128)S(1)}, f32[16,384]{1,0:T(8,128)S(1)}, u32[]{:S(2)}, u32[]{:S(2)}) collective-permute-start(f32[16,384]{1,0:T(8,128)S(1)} %get-tuple-element.24), channel_id=1, source_target_pairs={{32,0},{64,32},{96,64},{128,96},{160,128},{192,160},{224,192},{256... | collective-permute-start | bytes 73736 | tf_op jit(solution)/shard_map/ppermute | solution.py:534
  23.2 0.9 copy-done.8
  26.1 2.4 %pack_observations.1 = (f32[32,16,256]{2,1,0:T(8,128)}, f32[32,256]{1,0:T(8,128)S(1)}) custom-call(s32[2]{0:T(128)S(1)} %pad_add_fusion.place_ref.refs_0_, f32[128,256]{1,0:T(8,128)S(1)} %copy-done.8, s32[128,1]{1,0:T(8,128)S(1)} %copy.23.owner_ref, s32[1,128]{1,0:T(1,128)S(1)} %bitcast.14, s32[1,128]{1,0:T(1,128)S(1)} %bitcast.15, s32[1,64]{1,0:T(1,128)S(1)} %bitcast.7, ...), custom_call_target="tpu_custom_call" | custom-call | tf_op jit(solution)/shard_map/pack_observations/pallas_call | solution.py:498
  29.2 2.9 %partial_sums.1 = (f32[4,72,384]{2,1,0:T(8,128)S(1)}, f32[72,128]{1,0:T(8,128)S(1)}, f32[16,24,128]{2,1,0:T(8,128)S(1)}, f32[16,24,128]{2,1,0:T(8,128)S(1)}) custom-call(s32[2]{0:T(128)S(1)} %pad_add_fusion.place_ref.refs_0_, f32[4,64,384]{2,1,0:T(8,128)S(1)} %get-tuple-element.20.refs_0_.refs_1_, f32[64,128]{1,0:T(8,128)S(1)} %collective-permute-done.refs_1_.refs_2_, ...), custom_call_target="tpu_custom_call" | custom-call | tf_op jit(solution)/shard_map/partial_sums/pallas_call | solution.py:498
  32.1 1.9 %collective-permute-start.4 = (f32[16,24,128]{2,1,0:T(8,128)S(1)}, f32[16,24,128]{2,1,0:T(8,128)S(1)}, u32[]{:S(2)}, u32[]{:S(2)}) collective-permute-start(f32[16,24,128]{2,1,0:T(8,128)S(1)} %get-tuple-element.29), channel_id=1, source_target_pairs={{0,1},{1,0},{2,3},{3,2},{4,5},{5,4},{6,7},{7,6},{8,9},{9,8},{10,11... | collective-permute-start | bytes 589832 | tf_op jit(solution)/shard_map/ppermute | solution.py:590
  34.0 1.4 collective-permute-done.4
  35.5 24.8 %all_to_all.15.in_ref = f32[16,24,128]{2,1,0:T(8,128)S(1)} all-to-all(f32[16,24,128]{2,1,0:T(8,128)S(1)} %add.3), channel_id=1, replica_groups={{0,2,4,6,8,10,12,14,16,18,20,22,24,26,28,30},{1,3,5,7,9,11,13,15,17,19,..., dimensions={0} | all-to-all | bytes 393216 | tf_op jit(solution)/shard_map/all_to_all | solution.py:592
  60.2 6.4 %all-to-all-start.2 = ((f32[32,16,256]{2,1,0:T(8,128)}), f32[32,16,256]{2,1,0:T(8,128)S(1)}, u32[]{:S(2)}, u32[]{:S(2)}) async-start(f32[32,16,256]{2,1,0:T(8,128)} %get-tuple-element.30), calls=%async_computation.2 | async-start | bytes 1048576 | tf_op jit(solution)/shard_map/all_to_all | solution.py:613
  66.7 2.5 %own_row.1 = f32[32,16,128]{2,1,0:T(8,128)} custom-call(s32[2]{0:T(128)S(1)} %pad_add_fusion.place_ref.refs_0_, f32[16,24,128]{2,1,0:T(8,128)S(1)} %all_to_all.15.in_ref, s32[1,64]{1,0:T(1,128)S(1)} %bitcast.9, f32[1,64]{1,0:T(1,128)S(1)} %bitcast.13, f32[16,256]{1,0:T(8,128)S(1)} %copy-done.13, f32[8,128]{1,0:T(8,128)S(1)} %copy-done.19, ...), custom_call_target="tpu_custom_call" | custom-call | tf_op jit(solution)/shard_map/own_row/pallas_call | solution.py:498
  69.2 31.2 %all-to-all-done.2.in_ref = f32[32,16,256]{2,1,0:T(8,128)S(1)} async-done(((f32[32,16,256]{2,1,0:T(8,128)}), f32[32,16,256]{2,1,0:T(8,128)S(1)}, u32[]{:S(2)}, u32[]{:S(2)}) %all-to-all-start.2) | async-done | bytes 524320 | tf_op jit(solution)/shard_map/all_to_all | solution.py:613
  100.4 3.9 %all-to-all-start.1 = ((f32[32,16,128]{2,1,0:T(8,128)}), f32[32,16,128]{2,1,0:T(8,128)S(1)}, u32[]{:S(2)}, u32[]{:S(2)}) async-start(f32[32,16,128]{2,1,0:T(8,128)} %own_row.1), calls=%async_computation.1 | async-start | bytes 524288 | tf_op jit(solution)/shard_map/all_to_all | solution.py:612
  104.9 2.8 %collective-permute-start.5 = (f32[64,128]{1,0:T(8,128)S(1)}, f32[64,128]{1,0:T(8,128)S(1)}, u32[]{:S(2)}, u32[]{:S(2)}) collective-permute-start(f32[64,128]{1,0:T(8,128)S(1)} %get-tuple-element.32), channel_id=1, source_target_pairs={{0,31},{1,0},{2,1},{3,2},{4,3},{5,4},{6,5},{7,6},{8,7},{9,8},{10,9... | collective-permute-start | bytes 98312 | tf_op jit(solution)/shard_map/ppermute | solution.py:534
  107.8 19.3 %all-to-all-done.1.refs_0_ = f32[32,16,128]{2,1,0:T(8,128)S(1)} async-done(((f32[32,16,128]{2,1,0:T(8,128)}), f32[32,16,128]{2,1,0:T(8,128)S(1)}, u32[]{:S(2)}, u32[]{:S(2)}) %all-to-all-start.1) | async-done | bytes 262176 | tf_op jit(solution)/shard_map/all_to_all | solution.py:612
  127.7 5.2 %collective-permute-start.6 = (f32[56,128]{1,0:T(8,128)S(1)}, f32[56,128]{1,0:T(8,128)S(1)}, u32[]{:S(2)}, u32[]{:S(2)}) collective-permute-start(f32[56,128]{1,0:T(8,128)S(1)} %get-tuple-element.35), channel_id=1, source_target_pairs={{0,32},{32,64},{64,96},{96,128},{128,160},{160,192},{192,224},{224... | collective-permute-start | bytes 86024 | tf_op jit(solution)/shard_map/ppermute | solution.py:534
  132.9 1.9 %collective-permute-start.7 = (f32[56,128]{1,0:T(8,128)S(1)}, f32[56,128]{1,0:T(8,128)S(1)}, u32[]{:S(2)}, u32[]{:S(2)}) collective-permute-start(f32[56,128]{1,0:T(8,128)S(1)} %get-tuple-element.36), channel_id=1, source_target_pairs={{32,0},{64,32},{96,64},{128,96},{160,128},{192,160},{224,192},{256... | collective-permute-start | bytes 86024 | tf_op jit(solution)/shard_map/ppermute | solution.py:534
  134.8 5.9 %collective-permute-done.7.below_ref = f32[56,128]{1,0:T(8,128)S(1)} collective-permute-done((f32[56,128]{1,0:T(8,128)S(1)}, f32[56,128]{1,0:T(8,128)S(1)}, u32[]{:S(2)}, u32[]{:S(2)}) %collective-permute-start.7) | collective-permute-done | bytes 28704 | tf_op jit(solution)/shard_map/ppermute | solution.py:534
  140.8 2.5 %last_stage.1 = (f32[64,270]{1,0:T(8,128)}, f32[64,270]{1,0:T(8,128)}, f32[64,270]{1,0:T(8,128)}) custom-call(s32[2]{0:T(128)S(1)} %pad_add_fusion.place_ref.refs_0_, f32[4,72,384]{2,1,0:T(8,128)S(1)} %get-tuple-element.26.ext_ref, f32[72,128]{1,0:T(8,128)S(1)} %get-tuple-element.27.weight_ref, f32[12,64,128]{2,1,0:T(8,128)S(1)} %get-tuple-element.33.coef_ref, ...), custom_call_target="tpu_custom_call" | custom-call | tf_op jit(solution)/shard_map/last_stage/pallas_call | solution.py:498
  (52 shorter events, 6.4 us)
Async XLA Ops:
  0.6 22.5 %copy-start.5 = (f32[32,128]{1,0:T(8,128)S(1)}, f32[32,128]{1,0:T(8,128)}, u32[]{:S(2)}) copy-start(f32[32,128]{1,0:T(8,128)} %constant.30.clone.sin_ref.refs_10_) | copy-start | bytes 49156
  0.6 22.5 %copy-start.6 = (f32[32,128]{1,0:T(8,128)S(1)}, f32[32,128]{1,0:T(8,128)}, u32[]{:S(2)}) copy-start(f32[32,128]{1,0:T(8,128)} %constant.29.clone.cos_ref.refs_9_) | copy-start | bytes 49156
  0.7 22.5 %copy-start = (f32[384,256]{1,0:T(8,128)S(1)}, f32[384,256]{1,0:T(8,128)}, u32[]{:S(2)}) copy-start(f32[384,256]{1,0:T(8,128)} %constant.31.clone.table_ref.refs_11_) | copy-start | bytes 1179652
  0.7 27.8 %copy-start.1 = (f32[384,512]{1,0:T(8,128)S(1)}, f32[384,512]{1,0:T(8,128)}, u32[]{:S(2)}) copy-start(f32[384,512]{1,0:T(8,128)} %constant.33.clone.refs_12_) | copy-start | bytes 2359300
  0.7 1.0 copy-start.9
  2.6 0.9 copy-start.11
  4.5 10.5 %collective-permute-start = (f32[64,128]{1,0:T(8,128)S(1)}, f32[64,128]{1,0:T(8,128)S(1)}, u32[]{:S(2)}, u32[]{:S(2)}) collective-permute-start(f32[64,128]{1,0:T(8,128)S(1)} %get-tuple-element.21), channel_id=1, source_target_pairs={{0,1},{1,2},{2,3},{3,4},{4,5},{5,6},{6,7},{7,8},{8,9},{9,10},{10,1... | collective-permute-start | bytes 98312 | tf_op jit(solution)/shard_map/ppermute | solution.py:534
  4.5 10.5 %collective-permute-start.1 = (f32[64,128]{1,0:T(8,128)S(1)}, f32[64,128]{1,0:T(8,128)S(1)}, u32[]{:S(2)}, u32[]{:S(2)}) collective-permute-start(f32[64,128]{1,0:T(8,128)S(1)} %get-tuple-element.22), channel_id=1, source_target_pairs={{0,31},{1,0},{2,1},{3,2},{4,3},{5,4},{6,5},{7,6},{8,7},{9,8},{10,9... | collective-permute-start | bytes 98312 | tf_op jit(solution)/shard_map/ppermute | solution.py:534
  16.5 12.0 %collective-permute-start.2 = (f32[16,384]{1,0:T(8,128)S(1)}, f32[16,384]{1,0:T(8,128)S(1)}, u32[]{:S(2)}, u32[]{:S(2)}) collective-permute-start(f32[16,384]{1,0:T(8,128)S(1)} %get-tuple-element.23), channel_id=1, source_target_pairs={{0,32},{32,64},{64,96},{96,128},{128,160},{160,192},{192,224},{224... | collective-permute-start | bytes 73736 | tf_op jit(solution)/shard_map/ppermute | solution.py:534
  19.5 9.0 %collective-permute-start.3 = (f32[16,384]{1,0:T(8,128)S(1)}, f32[16,384]{1,0:T(8,128)S(1)}, u32[]{:S(2)}, u32[]{:S(2)}) collective-permute-start(f32[16,384]{1,0:T(8,128)S(1)} %get-tuple-element.24), channel_id=1, source_target_pairs={{32,0},{64,32},{96,64},{128,96},{160,128},{192,160},{224,192},{256... | collective-permute-start | bytes 73736 | tf_op jit(solution)/shard_map/ppermute | solution.py:534
  23.2 0.9 copy-start.8
  26.1 2.5 %copy-start.7 = (f32[72,128]{1,0:T(8,128)S(1)}, f32[72,128]{1,0:T(8,128)}, u32[]{:S(2)}) copy-start(f32[72,128]{1,0:T(8,128)} %constant.32.clone.refs_8_.terms_ref) | copy-start | bytes 110596
  32.1 3.3 %collective-permute-start.4 = (f32[16,24,128]{2,1,0:T(8,128)S(1)}, f32[16,24,128]{2,1,0:T(8,128)S(1)}, u32[]{:S(2)}, u32[]{:S(2)}) collective-permute-start(f32[16,24,128]{2,1,0:T(8,128)S(1)} %get-tuple-element.29), channel_id=1, source_target_pairs={{0,1},{1,0},{2,3},{3,2},{4,5},{5,4},{6,7},{7,6},{8,9},{9,8},{10,11... | collective-permute-start | bytes 589832 | tf_op jit(solution)/shard_map/ppermute | solution.py:590
  35.4 31.2 %copy-start.13 = (f32[16,256]{1,0:T(8,128)S(1)}, f32[16,256]{1,0:T(8,128)}, u32[]{:S(2)}) copy-start(f32[16,256]{1,0:T(8,128)} %constant.34.clone.lines_ref) | copy-start | bytes 49156
  35.4 31.2 %copy-start.16 = (s32[64]{0:T(128)S(1)}, s32[64]{0:T(128)}, u32[]{:S(2)}) copy-start(s32[64]{0:T(128)} %param.27) | copy-start | bytes 772
  35.4 31.2 %copy-start.19 = (f32[8,128]{1,0:T(8,128)S(1)}, f32[8,128]{1,0:T(8,128)}, u32[]{:S(2)}) copy-start(f32[8,128]{1,0:T(8,128)} %constant.35.clone.slope_ref) | copy-start | bytes 12292
  60.2 6.5 %copy-start.2 = (f32[512,256]{1,0:T(8,128)S(1)}, f32[512,256]{1,0:T(8,128)}, u32[]{:S(2)}) copy-start(f32[512,256]{1,0:T(8,128)} %constant.37.clone.from_grid_ref) | copy-start | bytes 1572868
  60.2 6.5 %copy-start.3 = (f32[256,512]{1,0:T(8,128)S(1)}, f32[256,512]{1,0:T(8,128)}, u32[]{:S(2)}) copy-start(f32[256,512]{1,0:T(8,128)} %constant.36.clone.to_grid_ref) | copy-start | bytes 1572868
  60.2 40.2 %all-to-all-start.2 = ((f32[32,16,256]{2,1,0:T(8,128)}), f32[32,16,256]{2,1,0:T(8,128)S(1)}, u32[]{:S(2)}, u32[]{:S(2)}) async-start(f32[32,16,256]{2,1,0:T(8,128)} %get-tuple-element.30), calls=%async_computation.2 | async-start | bytes 1048576 | tf_op jit(solution)/shard_map/all_to_all | solution.py:613
  100.4 26.7 %all-to-all-start.1 = ((f32[32,16,128]{2,1,0:T(8,128)}), f32[32,16,128]{2,1,0:T(8,128)S(1)}, u32[]{:S(2)}, u32[]{:S(2)}) async-start(f32[32,16,128]{2,1,0:T(8,128)} %own_row.1), calls=%async_computation.1 | async-start | bytes 524288 | tf_op jit(solution)/shard_map/all_to_all | solution.py:612
  104.3 36.5 %copy-start.4 = (f32[256,384]{1,0:T(8,128)S(1)}, f32[256,384]{1,0:T(8,128)}, u32[]{:S(2)}) copy-start(f32[256,384]{1,0:T(8,128)} %constant.38.clone.table_ref) | copy-start | bytes 1179652
  104.9 22.2 %collective-permute-start.5 = (f32[64,128]{1,0:T(8,128)S(1)}, f32[64,128]{1,0:T(8,128)S(1)}, u32[]{:S(2)}, u32[]{:S(2)}) collective-permute-start(f32[64,128]{1,0:T(8,128)S(1)} %get-tuple-element.32), channel_id=1, source_target_pairs={{0,31},{1,0},{2,1},{3,2},{4,3},{5,4},{6,5},{7,6},{8,7},{9,8},{10,9... | collective-permute-start | bytes 98312 | tf_op jit(solution)/shard_map/ppermute | solution.py:534
  127.7 7.1 %collective-permute-start.6 = (f32[56,128]{1,0:T(8,128)S(1)}, f32[56,128]{1,0:T(8,128)S(1)}, u32[]{:S(2)}, u32[]{:S(2)}) collective-permute-start(f32[56,128]{1,0:T(8,128)S(1)} %get-tuple-element.35), channel_id=1, source_target_pairs={{0,32},{32,64},{64,96},{96,128},{128,160},{160,192},{192,224},{224... | collective-permute-start | bytes 86024 | tf_op jit(solution)/shard_map/ppermute | solution.py:534
  132.9 7.9 %collective-permute-start.7 = (f32[56,128]{1,0:T(8,128)S(1)}, f32[56,128]{1,0:T(8,128)S(1)}, u32[]{:S(2)}, u32[]{:S(2)}) collective-permute-start(f32[56,128]{1,0:T(8,128)S(1)} %get-tuple-element.36), channel_id=1, source_target_pairs={{32,0},{64,32},{96,64},{128,96},{160,128},{192,160},{224,192},{256... | collective-permute-start | bytes 86024 | tf_op jit(solution)/shard_map/ppermute | solution.py:534
  (8 other events, 5.7 us)

commit v2 on v1

--- a/solution.py
+++ b/solution.py
@@ -60,23 +60,61 @@
     rows = mask_row.shape[1]
     half = devices // 2
     line = iota((devices, rows), 0)
-    near = (line < half).astype(jnp.int32)
-    place = jnp.where(line < half, line, line - half)
-    slot = 2 * place + near * core + (1 - near) * (1 - core)
+    slot = jnp.where(line < half, 2 * line + core, 2 * (line - half) + 1 - core)
     hit = (slot == rank_in_row(mask_row)) & (mask_row == 1)
     return hit.astype(F32)
 
 
-def pack_lon(h_ref, e_ref, n_ref, d_ref, fields_ref, west_ref, east_ref):
-    cols = h_ref.shape[1]
+WEIGHT_LANE = 300 - 256
+
+
+def pack_tile(
+    h_hbm,
+    e_hbm,
+    n_hbm,
+    d_hbm,
+    mask_hbm,
+    keep_hbm,
+    fields_ref,
+    west_ref,
+    east_ref,
+    north_ref,
+    south_ref,
+    filter_ref,
+    h_ref,
+    e_ref,
+    n_ref,
+    d_ref,
+    mask_ref,
+    keep_ref,
+    sems,
+):
+    pairs = (
+        (h_hbm, h_ref),
+        (e_hbm, e_ref),
+        (n_hbm, n_ref),
+        (d_hbm, d_ref),
+        (mask_hbm, mask_ref),
+        (keep_hbm, keep_ref),
+    )
+    copies = [pltpu.make_async_copy(a, b, sems.at[i]) for i, (a, b) in enumerate(pairs)]
+    for copy in copies:
+        copy.start()
+    fields_ref[...] = jnp.zeros(fields_ref.shape, F32)
+    for copy in copies:
+        copy.wait()
+    rows, cols = h_ref.shape
+    filter_ref[0:1, :] = mask_ref[...].astype(F32)
+    filter_ref[1:2, :] = keep_ref[...]
+    filter_ref[2:8, :] = jnp.zeros((6, rows), F32)
+    weight = to_col(mask_ref[...].astype(F32) * (1.0 - keep_ref[...]))
     level = d_ref[...].astype(F32)
     wet = (level > 0).astype(F32)
     values = (h_ref[...], wet * e_ref[...], wet * n_ref[...], level)
-    lane = iota((h_ref.shape[0], 128), 1)
+    lane = iota((rows, 128), 1)
     west = jnp.zeros(lane.shape, F32)
     east = jnp.zeros(lane.shape, F32)
     last = cols - HALO - 256
-    fields_ref[...] = jnp.zeros(fields_ref.shape, F32)
     for f, value in enumerate(values):
         fields_ref[f, :, 0:cols] = value
         inside = (lane >= HALO * f) & (lane < HALO * f + HALO)
@@ -86,6 +124,14 @@
             head = pltpu.roll(head, HALO * f, 1)
         west = jnp.where(inside, head, west)
         east = jnp.where(inside, pltpu.roll(tail, (HALO * f - last) % 128, 1), east)
+        for out_ref, at in ((north_ref, 0), (south_ref, rows - HALO)):
+            span = slice(at, at + HALO)
+            lines = slice(HALO * f, HALO * f + HALO)
+            edge = fields_ref[f, span, 256:384]
+            if f == 3:
+                edge = jnp.where(iota(edge.shape, 1) == WEIGHT_LANE, weight[span, :], edge)
+            out_ref[lines, 0:256] = fields_ref[f, span, 0:256]
+            out_ref[lines, 256:384] = edge
     west_ref[...] = west
     east_ref[...] = east
 
@@ -97,24 +143,6 @@
     tail = jnp.where((lane >= first) & (lane < first + HALO), shifted, tail)
     shifted = pltpu.roll(left, (128 - HALO - HALO * f) % 128, 1)
     return jnp.where(lane >= 128 - HALO, shifted, tail)
-
-
-WEIGHT_LANE = 300 - 256
-
-
-def pack_lat(cols, fields_ref, left_ref, right_ref, mask_ref, keep_ref, north_ref, south_ref):
-    rows = fields_ref.shape[1]
-    weight = to_col(mask_ref[...].astype(F32) * (1.0 - keep_ref[...]))
-    for f in range(4):
-        for out_ref, at in ((north_ref, 0), (south_ref, rows - HALO)):
-            span = slice(at, at + HALO)
-            tail = third_tile(
-                fields_ref[f, span, 256:384], left_ref[span, :], right_ref[span, :], f, cols
-            )
-            if f == 3:
-                tail = jnp.where(iota(tail.shape, 1) == WEIGHT_LANE, weight[span, :], tail)
-            out_ref[HALO * f : HALO * f + HALO, 0:256] = fields_ref[f, span, 0:256]
-            out_ref[HALO * f : HALO * f + HALO, 256:384] = tail
 
 
 def row_terms(terms, band):
@@ -133,8 +161,7 @@
     right_ref,
     above_ref,
     below_ref,
-    mask_ref,
-    keep_ref,
+    filter_ref,
     terms_ref,
     cos_ref,
     sin_ref,
@@ -143,6 +170,8 @@
     placed_ref,
     ext_ref,
     weight_ref,
+    west_ref,
+    east_ref,
     mine_ref,
     other_ref,
     stack_ref,
@@ -153,29 +182,37 @@
     devices = cos_ref.shape[0]
     half = devices // 2
     band, lon = place_ref[0], place_ref[1]
-    core = lon % 2
     for f in range(4):
-        ext_ref[f, 0:rows, 0:256] = fields_ref[f, :, 0:256]
-        ext_ref[f, 0:rows, 256:384] = third_tile(
-            fields_ref[f, :, 256:384], left_ref[...], right_ref[...], f, cols
-        )
+        ext_ref[f, 0:rows, :] = fields_ref[f]
         ext_ref[f, rows : rows + HALO, :] = below_ref[HALO * f : HALO * f + HALO, :]
         ext_ref[f, rows + HALO : ext, :] = above_ref[HALO * f : HALO * f + HALO, :]
     edge = ext_ref[3, rows:ext, 256:384]
     marked = iota(edge.shape, 1) == WEIGHT_LANE
-    mask = mask_ref[...]
-    weight_ref[0:rows, :] = jnp.broadcast_to(
-        to_col(mask.astype(F32) * (1.0 - keep_ref[...])), (rows, 128)
-    )
+    mask, keep = filter_ref[0:1, :], filter_ref[1:2, :]
+    weight_ref[0:rows, :] = jnp.broadcast_to(to_col(mask * (1.0 - keep)), (rows, 128))
     weight_ref[rows:ext, :] = jnp.broadcast_to(
         jnp.sum(jnp.where(marked, edge, 0.0), axis=1, keepdims=True), (2 * HALO, 128)
     )
     ext_ref[3, rows:ext, 256:384] = jnp.where(marked, 0.0, edge)
+    corner = iota((2 * HALO, 128), 1)
+    last = cols - HALO - 256
+    for f in range(4):
+        lines = slice(2 * HALO * f, 2 * HALO * f + 2 * HALO)
+        inside = (corner >= HALO * f) & (corner < HALO * f + HALO)
+        head = ext_ref[f, rows:ext, 0:128]
+        tail = ext_ref[f, rows:ext, 256:384]
+        if f:
+            head = pltpu.roll(head, HALO * f, 1)
+        west_ref[lines, :] = jnp.where(inside, head, 0.0)
+        east_ref[lines, :] = jnp.where(inside, pltpu.roll(tail, (HALO * f - last) % 128, 1), 0.0)
     weight = weight_ref[:, 0:1]
     rest = 1.0 - weight
     metric, rotation, valid = row_terms(terms_ref[...], band)
     metric = metric * valid
     height, east, north = ext_ref[0], ext_ref[1], ext_ref[2]
+    ext_ref[3, 0:rows, 256:384] = third_tile(
+        ext_ref[3, 0:rows, 256:384], left_ref[...], right_ref[...], 3, cols
+    )
     share = ext_ref[3] / LEVELS
     low_height = weight * height + COURANT * (
         metric * lon_diff(weight * east) + lat_diff(weight * north)
@@ -187,7 +224,7 @@
     )
     new_east = east_rest - rotation * north_rest + COURANT * share * metric * lon_diff(middle)
     new_north = north_rest + rotation * east_rest + COURANT * share * lat_diff(middle)
-    chosen = slot_rows(mask, core, devices)
+    chosen = slot_rows(mask, place_ref[1] % 2, devices)
     sources = (height, east, north, low_height, lat_diff(low_height), middle, new_east, new_north)
     for v, field in enumerate(sources):
         stack_ref[devices * v : devices * v + devices, :] = hdot(chosen, field[0:rows, :])
@@ -218,92 +255,140 @@
 
 def pack_observations(
     place_ref,
+    values_hbm,
+    owner_hbm,
+    row_hbm,
+    count_hbm,
+    near_ref,
+    far_ref,
+    kept_ref,
+    marks_ref,
     values_ref,
     owner_ref,
     row_ref,
     count_ref,
-    mask_ref,
-    cos_ref,
-    sin_ref,
-    table_ref,
-    out_ref,
-    placed_ref,
+    sems,
 ):
+    pairs = (
+        (values_hbm, values_ref),
+        (owner_hbm, owner_ref),
+        (row_hbm, row_ref),
+        (count_hbm, count_ref),
+    )
+    copies = [pltpu.make_async_copy(a, b, sems.at[i]) for i, (a, b) in enumerate(pairs)]
+    for copy in copies:
+        copy.start()
+    for copy in copies:
+        copy.wait()
     number, width = values_ref.shape
-    devices = cos_ref.shape[0]
+    half = near_ref.shape[0]
     core = place_ref[1] % 2
     values = jnp.where(
         iota((number, width), 1) < to_col(count_ref[...]), values_ref[...], 0.0
     )
-    owner_col = owner_ref[...]
-    owner_row = to_row(owner_col)
+    kept_ref[...] = values
+    owner_row = owner_ref[...]
+    owner_col = to_col(owner_row)
+    marks_ref[0:1, :] = owner_row.astype(F32)
+    marks_ref[1:2, :] = row_ref[...].astype(F32)
+    marks_ref[2:8, :] = jnp.zeros((6, number), F32)
     same = owner_col == owner_row
     before = same & (iota((number, number), 0) < iota((number, number), 1))
     arrival_row = jnp.sum(before.astype(jnp.int32), axis=0, keepdims=True)
     after = same & (iota((number, number), 0) > iota((number, number), 1))
     arrival_col = jnp.sum(after.astype(jnp.int32), axis=1, keepdims=True)
-    target = owner_row * 16 + arrival_row
-    sent = (iota((16 * devices, number), 0) == target).astype(F32)
-    out_ref[...] = hdot(sent, values).reshape(devices, 16, width)
-    named = (iota((devices, number), 0) == owner_row).astype(F32) * row_ref[...].astype(F32)
-    lines = hdot(named, (iota((number, width), 1) == arrival_col).astype(F32))
-    out_ref[:, CAP, :] = lines
-    sums = hdot(values, table_ref[0:width, :])
-    whose = (iota((number, devices), 1) == owner_col).astype(F32)
+    chip_row, core_row = owner_row // 2, owner_row % 2
+    target = chip_row * 16 + arrival_row
+    label = row_ref[...].astype(F32)
+    arrived = (iota((number, 128), 1) == arrival_col).astype(F32)
+    for out_ref, side in ((near_ref, core), (far_ref, 1 - core)):
+        goes = core_row == side
+        sent = ((iota((16 * half, number), 0) == target) & goes).astype(F32)
+        block = hdot(sent, values).reshape(half, 16, width)
+        out_ref[:, 0:CAP, :] = block[:, 0:CAP, 0:128]
+        out_ref[:, CAP : 2 * CAP, :] = block[:, 0:CAP, 128:256]
+        named = ((iota((half, number), 0) == chip_row) & goes).astype(F32) * label
+        out_ref[:, 2 * CAP : 32, :] = jnp.zeros((half, 32 - 2 * CAP, 128), F32)
+        out_ref[:, 2 * CAP, :] = hdot(named, arrived)
+
+
+def sum_observations(
+    place_ref, values_ref, marks_ref, filter_ref, cos_ref, sin_ref, table_ref, placed_ref
+):
+    number, width = values_ref.shape
+    devices = cos_ref.shape[0]
+    owner_col = to_col(marks_ref[0:1, :])
+    sums = hdot(values_ref[...], table_ref[0:width, :])
+    whose = (iota((number, devices), 1).astype(F32) == owner_col).astype(F32)
     turn_cos, turn_sin = hdot(whose, cos_ref[...]), hdot(whose, sin_ref[...])
     on_cos, on_sin = sums[:, 0:128], sums[:, 128:256]
     all_cos = on_cos * turn_cos - on_sin * turn_sin
     all_sin = on_sin * turn_cos + on_cos * turn_sin
-    mask = mask_ref[...]
+    mask = filter_ref[0:1, :]
     rows = mask.shape[1]
-    in_row = (iota((rows, number), 0) == row_ref[...]).astype(F32)
-    chosen = hdot(slot_rows(mask, core, devices), in_row)
+    in_row = (iota((rows, number), 0).astype(F32) == marks_ref[1:2, :]).astype(F32)
+    chosen = hdot(slot_rows(mask, place_ref[1] % 2, devices), in_row)
     placed_ref[:, 0:128] = hdot(chosen, all_cos)
     placed_ref[:, 128:256] = hdot(chosen, all_sin)
 
 
-def unpack_observations(in_ref, dep_ref, edge_ref):
-    devices, lines, width = in_ref.shape
+def join(mine_ref, swapped_ref, near_ref, far_ref, out_ref):
+    half = out_ref.shape[0]
+    out_ref[:, 0:24, :] = mine_ref[...] + swapped_ref[...]
+    out_ref[:, 24:48, :] = near_ref[:, 0:24, :]
+    out_ref[:, 48:72, :] = far_ref[:, 0:24, :]
+    out_ref[:, 72:80, :] = jnp.zeros((half, 8, 128), F32)
+    out_ref[:, 72, :] = near_ref[:, 24, :]
+    out_ref[:, 73, :] = far_ref[:, 24, :]
+
+
+def unpack_observations(in_ref, corner_ref, dep_ref, west_ref):
+    half = in_ref.shape[0]
     rows = dep_ref.shape[0]
-    total = devices * lines
-    labels = in_ref[:, CAP, 0:128]
-    across = hdot(labels, (iota((128, total), 1) % lines == iota((128, total), 0)).astype(F32))
-    own = iota((devices, total), 1) // lines == iota((devices, total), 0)
-    label_row = jnp.sum(jnp.where(own, across, 0.0), axis=0, keepdims=True)
+    lines = 4 * CAP
+    total = half * lines
+    spot = iota((128, total), 1) % lines
+    label_row = jnp.zeros((1, total), F32)
+    own = iota((half, total), 1) // lines == iota((half, total), 0)
+    for s in range(2):
+        here = (spot // (2 * CAP) == s) & (spot % CAP == iota((128, total), 0))
+        across = hdot(in_ref[:, 72 + s, :], here.astype(F32))
+        label_row = label_row + jnp.sum(jnp.where(own, across, 0.0), axis=0, keepdims=True)
     line = iota((rows, total), 1) % lines
-    hit = (iota((rows, total), 0).astype(F32) == label_row) & (line < CAP)
-    summed = hdot(hit.astype(F32), in_ref[...].reshape(total, width))
-    dep_ref[:, 0:256] = summed
+    hit = iota((rows, total), 0).astype(F32) == label_row
+    data = in_ref[:, 24 : 24 + lines, :].reshape(total, 128)
+    for i in range(2):
+        side = (hit & ((line // CAP) % 2 == i)).astype(F32)
+        dep_ref[:, 128 * i : 128 * i + 128] = hdot(side, data)
     dep_ref[:, 256:384] = jnp.zeros((rows, 128), F32)
-    edge_ref[...] = pltpu.roll(summed[:, 0:128], 14, 1)
+    west_ref[0:rows, :] = pltpu.roll(dep_ref[:, 0:128], 14, 1)
+    west_ref[rows : rows + corner_ref.shape[0], :] = corner_ref[...]
 
 
 def own_row(
     place_ref,
     in_ref,
-    mask_ref,
-    keep_ref,
+    filter_ref,
     lines_ref,
     slope_ref,
     to_grid_ref,
     from_grid_ref,
-    out_ref,
+    res_ref,
     left_ref,
     grid_ref,
-    res_ref,
 ):
     band, lon = place_ref[0], place_ref[1]
-    sums = in_ref[0]
+    sums = in_ref[0, 0:24, :]
     for i in range(1, in_ref.shape[0]):
-        sums = sums + in_ref[i]
-    mask = mask_ref[...]
+        sums = sums + in_ref[i, 0:24, :]
+    mask, keep = filter_ref[0:1, :], filter_ref[1:2, :]
     chosen = ((rank_in_row(mask) == lon) & (mask == 1)).astype(F32)
 
     def pick(row):
         return jnp.sum(chosen * row, axis=1, keepdims=True)
 
     rows = mask.shape[1]
-    weight = pick(1.0 - keep_ref[...])
+    weight = pick(1.0 - keep)
     both = lines_ref[pl.ds(band, 1), :]
     metric = pick(both[:, 0:rows])
     rotation = pick(both[:, 128 : 128 + rows])
@@ -329,27 +414,35 @@
     grid_ref[0:1, :] = wet * at[0:1] + share * at[1:2]
     grid_ref[1:2, :] = wet * at[2:3] + share * at[3:4]
     back = hdot(grid_ref[...], from_grid_ref[...])
-    res_ref[...] = jnp.zeros(res_ref.shape, F32)
     res_ref[0:6, :] = sums[0:6]
     res_ref[6:8, :] = sums[10:12] + sums[6:8]
     for i in range(2):
         res_ref[8 + 2 * i : 9 + 2 * i, :] = line(12 + 2 * i) + back[i : i + 1, 0:128]
         res_ref[9 + 2 * i : 10 + 2 * i, :] = line(13 + 2 * i) + back[i : i + 1, 128:256]
-    out_ref[...] = jnp.broadcast_to(res_ref[...][None], out_ref.shape)
-
-
-def band_edges(cols, all_ref, dep_ref, edge_ref, mask_ref, coef_ref, depx_ref, north_ref, south_ref):
-    devices = all_ref.shape[0]
+
+
+def spread_pair(pair_ref, out_ref):
+    both = jnp.concatenate([pair_ref[0], pair_ref[1]], axis=0)
+    out_ref[...] = jnp.broadcast_to(both[None], out_ref.shape)
+
+
+def band_edges(cols, all_ref, dep_ref, edge_ref, filter_ref, coef_ref, depx_ref, north_ref, south_ref):
+    half = all_ref.shape[0]
     rows = dep_ref.shape[0]
-    mask = mask_ref[...]
+    mask = filter_ref[0:1, :]
     rank = to_col(rank_in_row(mask))
-    chosen = ((iota((rows, devices), 1) == rank) & (to_col(mask) == 1)).astype(F32)
+    kept = to_col(mask) == 1
     first = cols - 256
     lane = iota((rows, 128), 1)
     depx_ref[:, 0:256] = dep_ref[:, 0:256]
-    depx_ref[:, 256:384] = jnp.where((lane == first) | (lane == first + 1), edge_ref[...], 0.0)
+    depx_ref[:, 256:384] = jnp.where(
+        (lane == first) | (lane == first + 1), edge_ref[0:rows, :], 0.0
+    )
+    chosen = [
+        ((2 * iota((rows, half), 1) + c == rank) & kept).astype(F32) for c in range(2)
+    ]
     for v in range(12):
-        own = hdot(chosen, all_ref[:, v, :])
+        own = hdot(chosen[0], all_ref[:, v, :]) + hdot(chosen[1], all_ref[:, 12 + v, :])
         coef_ref[v] = own
         north_ref[4 * v : 4 * v + 4, :] = own[0:4]
         south_ref[4 * v : 4 * v + 4, :] = own[rows - 4 : rows]
@@ -364,7 +457,11 @@
 
 def last_stage(
     place_ref,
-    ext_ref,
+    wide_ref,
+    left_ref,
+    right_ref,
+    corner_left_ref,
+    corner_right_ref,
     weight_ref,
     coef_ref,
     depx_ref,
@@ -379,9 +476,23 @@
     n_ref,
     stack_ref,
     dep_ref,
+    ext_ref,
 ):
     ext = ext_ref.shape[1]
     rows, cols = h_ref.shape
+    for f in range(4):
+        ext_ref[f, :, 0:256] = wide_ref[f, :, 0:256]
+        ext_ref[f, 0:rows, 256:384] = third_tile(
+            wide_ref[f, 0:rows, 256:384], left_ref[...], right_ref[...], f, cols
+        )
+        lines = slice(2 * HALO * f, 2 * HALO * f + 2 * HALO)
+        ext_ref[f, rows:ext, 256:384] = third_tile(
+            wide_ref[f, rows:ext, 256:384],
+            corner_left_ref[lines, :],
+            corner_right_ref[rows + 2 * HALO * f : rows + 2 * HALO * f + 2 * HALO, :],
+            f,
+            cols,
+        )
     band, lon = place_ref[0], place_ref[1]
     turn_cos, turn_sin = cos_ref[pl.ds(lon, 1), :], sin_ref[pl.ds(lon, 1), :]
     for f in range(6):
@@ -440,12 +551,11 @@
         phase = (at[:, None].astype(np.int64) * number[None, :]) % length
         return phase * (2.0 * math.pi / length)
 
-    ahead = angle(lane, mode)
     inside = (lane < cols)[:, None]
-    analyse = np.concatenate([np.cos(ahead) * norm, np.sin(ahead) * norm], axis=1) * inside
     place = np.where(lane < LANES - HALO, lane, lane - LANES)
     shown = ((lane < cols + HALO) | (lane >= LANES - HALO))[:, None]
     around = angle(place, mode)
+    analyse = np.concatenate([np.cos(around) * norm, np.sin(around) * norm], axis=1) * shown
     evaluate = (np.concatenate([np.cos(around), np.sin(around)], axis=1) * shown).T
     wide = np.arange(1, 2 * MODES - 1)
     spot = np.arange(GRID) * (length / GRID)
@@ -490,20 +600,37 @@
 
 VMEM = pl.BlockSpec(memory_space=pltpu.VMEM)
 SMEM = pl.BlockSpec(memory_space=pltpu.SMEM)
-
-
-def call(kernel, name, outs, args, scratch=(), scalars=False):
+HBM = pl.BlockSpec(memory_space=pltpu.HBM)
+
+
+def call(kernel, name, outs, args, scratch=(), scalars=False, direct=(), cost=1.0):
     shapes = [jax.ShapeDtypeStruct(shape, F32) for shape in outs]
-    specs = [SMEM if scalars and i == 0 else VMEM for i in range(len(args))]
+    specs = [
+        SMEM if scalars and i == 0 else HBM if i in direct else VMEM for i in range(len(args))
+    ]
+    args = [
+        pltpu.with_memory_space_constraint(arg, pltpu.HBM) if i in direct else arg
+        for i, arg in enumerate(args)
+    ]
+    held = [pltpu.VMEM(args[i].shape, args[i].dtype) for i in direct]
+    held += [pltpu.SemaphoreType.DMA((len(direct),))] if direct else []
     return pl.pallas_call(
         kernel,
         name=name,
         out_shape=shapes,
         in_specs=specs,
         out_specs=[VMEM] * len(shapes),
-        scratch_shapes=[pltpu.VMEM(shape, F32) for shape in scratch],
-        compiler_params=pltpu.CompilerParams(vmem_limit_bytes=40 * 2**20),
+        scratch_shapes=held + [pltpu.VMEM(shape, F32) for shape in scratch],
+        cost_estimate=pl.CostEstimate(
+            flops=int(cost * 1e9), bytes_accessed=int(cost * 2e6), transcendentals=0
+        ),
+        compiler_params=pltpu.CompilerParams(
+            vmem_limit_bytes=40 * 2**20
+        ),
     )(*args)
+
+
+LON = ("z", "core")
 
 
 def on_device(
@@ -519,55 +646,62 @@
     depth_level,
 ):
     rows, cols = back_height.shape
-    bands, devices = lax.axis_size("band"), lax.axis_size("lon")
+    bands, devices = lax.axis_size("band"), lax.axis_size(LON)
     half = devices // 2
     number, width = obs_values.shape
     ext = rows + 2 * HALO
     made = tables(cols * devices, cols, devices, rows, bands)
-    place = jnp.stack([lax.axis_index("band"), lax.axis_index("lon")]).astype(jnp.int32)
-    mask = polar_mask.reshape(1, rows)
-    keep = keep_share.reshape(1, rows)
+    place = jnp.stack([lax.axis_index("band"), lax.axis_index(LON)]).astype(jnp.int32)
 
     def send(value, axis, shift, closed):
         count = lax.axis_size(axis)
         pairs = [(i, (i + shift) % count) for i in range(count) if closed or 0 <= i + shift < count]
         return lax.ppermute(value, axis, pairs)
 
-    fields, west, east = call(
-        pack_lon,
-        "pack_lon",
-        [(4, rows, LANES), (rows, 128), (rows, 128)],
-        (back_height, back_east, back_north, depth_level),
-    )
-    right, left = send(west, "lon", -1, True), send(east, "lon", 1, True)
-    outgoing, placed = call(
+    fields, west, east, north, south, kept = call(
+        pack_tile,
+        "pack_tile",
+        [(4, rows, LANES), (rows, 128), (rows, 128)] + [(4 * HALO, LANES)] * 2 + [(8, rows)],
+        (
+            back_height,
+            back_east,
+            back_north,
+            depth_level,
+            polar_mask.reshape(1, rows),
+            keep_share.reshape(1, rows),
+        ),
+        direct=range(6),
+    )
+    below, above = send(north, "band", -1, False), send(south, "band", 1, False)
+    right, left = send(west, LON, -1, True), send(east, LON, 1, True)
+    other_core = [(i, i ^ 1) for i in range(devices)]
+    near, far, values, marks = call(
         pack_observations,
         "pack_observations",
-        [(devices, 16, width), (devices, 256)],
+        [(half, 32, 128), (half, 32, 128), (number, width), (8, number)],
         (
             place,
             obs_values,
-            obs_owner,
+            obs_owner.reshape(1, number),
             obs_row.reshape(1, number),
             obs_count.reshape(1, number),
-            mask,
-            made["cos"],
-            made["sin"],
-            made["analyse"],
         ),
+        cost=3.0,
         scalars=True,
-    )
-    north, south = call(
-        lambda *refs: pack_lat(cols, *refs),
-        "pack_lat",
-        [(4 * HALO, LANES)] * 2,
-        (fields, left, right, mask, keep),
-    )
-    below, above = send(north, "band", -1, False), send(south, "band", 1, False)
-    ext_fields, weight, mine, other = call(
+        direct=range(1, 5),
+    )
+    far = lax.ppermute(far, LON, other_core)
+    (placed,) = call(
+        sum_observations,
+        "sum_observations",
+        [(devices, 256)],
+        (place, values, marks, kept, made["cos"], made["sin"], made["analyse"]),
+        scalars=True,
+    )
+    wide, weight, corner_west, corner_east, mine, other = call(
         lambda *refs: partial_sums(cols, *refs),
         "partial_sums",
-        [(4, ext, LANES), (ext, 128), (half, 24, 128), (half, 24, 128)],
+        [(4, ext, LANES), (ext, 128)] + [(8 * HALO, 128)] * 2 + [(half, 24, 128)] * 2,
         (
             place,
             fields,
@@ -575,8 +709,7 @@
             right,
             above,
             below,
-            mask,
-            keep,
+            kept,
             made["terms"],
             made["cos"],
             made["sin"],
@@ -587,39 +720,42 @@
         scratch=[(8 * devices, LANES), (2 * devices, LANES)],
         scalars=True,
     )
-    swapped = lax.ppermute(other, "lon", [(i, i ^ 1) for i in range(devices)])
-    groups = [[2 * i + c for i in range(half)] for c in range(2)]
-    owned = lax.all_to_all(
-        mine + swapped, "lon", split_axis=0, concat_axis=0, axis_index_groups=groups, tiled=True
-    )
-    (spread,) = call(
+    swapped = lax.ppermute(other, LON, other_core)
+    (joined,) = call(join, "join", [(half, 80, 128)], (mine, swapped, near, far))
+    owned = lax.all_to_all(joined, "z", split_axis=0, concat_axis=0, tiled=True)
+    (result,) = call(
         own_row,
         "own_row",
-        [(devices, 16, 128)],
+        [(12, 128)],
         (
             place,
             owned,
-            mask,
-            keep,
+            kept,
             made["lines"],
             made["slope"],
             made["to_grid"],
             made["from_grid"],
         ),
-        scratch=[(8, 256), (8, GRID), (16, 128)],
+        scratch=[(8, 256), (8, GRID)],
         scalars=True,
     )
-    everyone = lax.all_to_all(spread, "lon", split_axis=0, concat_axis=0, tiled=True)
-    incoming = lax.all_to_all(outgoing, "lon", split_axis=0, concat_axis=0, tiled=True)
-    dep, edge = call(
-        unpack_observations, "unpack_observations", [(rows, LANES), (rows, 128)], (incoming,)
-    )
-    dep_right = send(edge, "lon", -1, True)
+    pair = lax.all_gather(result, "core", axis=0, tiled=False)
+    (spread,) = call(spread_pair, "spread_pair", [(half, 24, 128)], (pair,))
+    everyone = lax.all_to_all(spread, "z", split_axis=0, concat_axis=0, tiled=True)
+    dep, west = call(
+        unpack_observations,
+        "unpack_observations",
+        [(rows, LANES), (rows + 8 * HALO, 128)],
+        (owned, corner_west),
+    )
+    corner_east = lax.optimization_barrier((corner_east, spread))[0]
+    corner_right, corner_left = send(west, LON, -1, True), send(corner_east, LON, 1, True)
+    dep, corner_left = lax.optimization_barrier((dep, corner_left))
     coef, depx, north, south = call(
         lambda *refs: band_edges(cols, *refs),
         "band_edges",
         [(12, rows, 128), (rows, LANES), (56, 128), (56, 128)],
-        (everyone, dep, dep_right, mask),
+        (everyone, dep, corner_right, kept),
     )
     below, above = send(north, "band", -1, False), send(south, "band", 1, False)
     return tuple(
@@ -629,7 +765,11 @@
             [(rows, cols)] * 3,
             (
                 place,
-                ext_fields,
+                wide,
+                left,
+                right,
+                corner_left,
+                corner_right,
                 weight,
                 coef,
                 depx,
@@ -640,7 +780,7 @@
                 made["sin"],
                 made["evaluate"],
             ),
-            scratch=[(6 * ext, 256), (ext, LANES)],
+            scratch=[(6 * ext, 256), (ext, LANES), (4, ext, LANES)],
             scalars=True,
         )
     )
@@ -648,21 +788,24 @@
 
 def solution(mesh):
     placed = (
-        P("band", "lon"),
-        P("band", "lon"),
-        P("band", "lon"),
-        P(("band", "lon"), None),
-        P(("band", "lon"), None),
-        P(("band", "lon")),
-        P(("band", "lon")),
+        P("band", LON),
+        P("band", LON),
+        P("band", LON),
+        P(("band", *LON), None),
+        P(("band", *LON), None),
+        P(("band", *LON)),
+        P(("band", *LON)),
         P("band"),
         P("band"),
-        P("band", "lon"),
+        P("band", LON),
+    )
+    fine = jax.sharding.Mesh(
+        mesh.devices.reshape(mesh.devices.shape[0], -1, 2), ("band", *LON)
     )
     return jax.shard_map(
         on_device,
-        mesh=mesh,
+        mesh=fine,
         in_specs=placed,
-        out_specs=(P("band", "lon"), P("band", "lon"), P("band", "lon")),
+        out_specs=(P("band", LON), P("band", LON), P("band", LON)),
         check_vma=False,
     )

time: 144 us -> 118 us (0.82)
  waiting for transfers between devices: 59.5 us -> 21.1 us
  blocking collectives: 24.8 us -> 48.4 us
  local copies, waits for them, and re-layouts: 9.28 us -> 0.06 us
  starting transfers between devices: 37 us -> 32.7 us
  Pallas kernels: 11.8 us -> 14.3 us
    all_to_all x2 -> x1, waiting for transfers between devices: 50.6 us -> 8.32 us  [on_device(): lax.all_to_all(spread, 'z', split_axis=0, concat_axis=0, tiled=True)]
    all_to_all x1, blocking collectives: 24.8 us -> 46.5 us  [on_device(): owned = lax.all_to_all(joined, 'z', split_axis=0, concat_axis=0, tiled=True)]
    unnamed x45 -> x20, local copies, waits for them, and re-layouts: 9.28 us -> 0.06 us
    all_to_all x2 -> x1, starting transfers between devices: 10.3 us -> 4.68 us  [on_device(): lax.all_to_all(spread, 'z', split_axis=0, concat_axis=0, tiled=True)]
    ppermute x7 -> x8, waiting for transfers between devices: 7.54 us -> 11.7 us  [send(): return lax.ppermute(value, axis, pairs)]
    pallas_call x8 -> x10, Pallas kernels: 11.8 us -> 14.3 us  [call(): pl.pallas_call(kernel, name=name, out_shape=shapes, in_specs=specs, out_s...]
    ppermute x1 -> x2, starting transfers between devices: 1.92 us -> 4.33 us  [the longest x1 2.41 us: on_device(): swapped = lax.ppermute(other, LON, other_core)]
    all_gather x0 -> x1, blocking collectives: none -> 1.82 us  [on_device(): pair = lax.all_gather(result, 'core', axis=0, tiled=False)]
  transfers between devices with their start and end apart: 10 -> 11, of which waited for: 5 -> 4; matrix products, arithmetic and copies ran while one was open for 1% -> 0% of each run, Pallas kernels for 4% -> 6%
where the time goes in v2:
time: 118 us; the launch traced here: 117 us
  blocking collectives  48.4 us (41%)
  starting transfers between devices  32.7 us (28%)
  waiting for transfers between devices  21.1 us (18%)
  Pallas kernels  14.3 us (12%)
    all_to_all x1, blocking collectives, on_device(): owned = lax.all_to_all(joined, 'z', split_axis=0, concat_axis=0, tiled=True)  46.5 us
    ppermute x8, starting transfers between devices, send(): return lax.ppermute(value, axis, pairs)  23.7 us
    pallas_call x10, Pallas kernels, call(): pl.pallas_call(kernel, name=name, out_shape=shapes, in_specs=specs, out_s...  14.3 us
    ppermute x8, waiting for transfers between devices, send(): return lax.ppermute(value, axis, pairs)  11.7 us
    all_to_all x1, waiting for transfers between devices, on_device(): lax.all_to_all(spread, 'z', split_axis=0, concat_axis=0, tiled=True)  8.32 us
    all_to_all x1, starting transfers between devices, on_device(): lax.all_to_all(spread, 'z', split_axis=0, concat_axis=0, tiled=True)  4.68 us
    ppermute x1, starting transfers between devices, on_device(): swapped = lax.ppermute(other, LON, other_core)  2.41 us
  transfers between devices with their start and end apart: 11, of which 4 were waited for; matrix products, arithmetic and copies ran while one was open for 0% of the time, Pallas kernels for 6%

profile of v2, /device:TPU:24, one launch (start us, length us, event | category | flops | bytes accessed | tf_op | source)
XLA Modules:
  0.0 117.5 jit_solution(16138845695991255911)
XLA Ops:
  0.6 1.3 %pack_tile.1 = (f32[4,64,384]{2,1,0:T(8,128)S(1)}, f32[64,128]{1,0:T(8,128)S(1)}, f32[64,128]{1,0:T(8,128)S(1)}, f32[16,384]{1,0:T(8,128)S(1)}, f32[16,384]{1,0:T(8,128)S(1)}, /*index=5*/f32[8,64]{1,0:T(8,128)S(1)}) custom-call(f32[64,270]{1,0:T(8,128)} %h_hbm.1, f32[64,270]{1,0:T(8,128)} %e_hbm.1, f32[64,270]{1,0:T(8,128)} %n_hbm.1, s32[64,270]{1,0:T(8,128)} %d_hbm.1, ...), custom_call_target="tpu_custom_call" | custom-call | flops 1000000000 | bytes 2000000 | tf_op jit(solution)/shard_map/pack_tile/pallas_call | solution.py:617
  1.9 3.1 %collective-permute-start.2 = (f32[16,384]{1,0:T(8,128)S(1)}, f32[16,384]{1,0:T(8,128)S(1)}, u32[]{:S(2)}, u32[]{:S(2)}) collective-permute-start(f32[16,384]{1,0:T(8,128)S(1)} %get-tuple-element.31), channel_id=1, source_target_pairs={{0,32},{32,64},{64,96},{96,128},{128,160},{160,192},{192,224},{224... | collective-permute-start | bytes 73736 | tf_op jit(solution)/shard_map/ppermute | solution.py:659
  5.0 2.8 %collective-permute-start.3 = (f32[16,384]{1,0:T(8,128)S(1)}, f32[16,384]{1,0:T(8,128)S(1)}, u32[]{:S(2)}, u32[]{:S(2)}) collective-permute-start(f32[16,384]{1,0:T(8,128)S(1)} %get-tuple-element.32), channel_id=1, source_target_pairs={{32,0},{64,32},{96,64},{128,96},{160,128},{192,160},{224,192},{256... | collective-permute-start | bytes 73736 | tf_op jit(solution)/shard_map/ppermute | solution.py:659
  7.8 8.4 %collective-permute-start.1 = (f32[64,128]{1,0:T(8,128)S(1)}, f32[64,128]{1,0:T(8,128)S(1)}, u32[]{:S(2)}, u32[]{:S(2)}) collective-permute-start(f32[64,128]{1,0:T(8,128)S(1)} %get-tuple-element.30), channel_id=1, source_target_pairs={{0,31},{1,0},{2,1},{3,2},{4,3},{5,4},{6,5},{7,6},{8,7},{9,8},{10,9... | collective-permute-start | bytes 98312 | tf_op jit(solution)/shard_map/ppermute | solution.py:659
  16.2 2.3 %pack_observations.1 = (f32[16,32,128]{2,1,0:T(8,128)S(1)}, f32[16,32,128]{2,1,0:T(8,128)S(1)}, f32[128,256]{1,0:T(8,128)S(1)}, f32[8,128]{1,0:T(8,128)S(1)}) custom-call(s32[2]{0:T(128)S(1)} %pad_add_fusion.place_ref.refs_0_, f32[128,256]{1,0:T(8,128)} %values_hbm.1, s32[1,128]{1,0:T(1,128)} %bitcast.11, s32[1,128]{1,0:T(1,128)} %bitcast.12, s32[1,128]{1,0:T(1,128)} %bitcast.13), custom_call_target="tpu_custom_call" | custom-call | flops 3000000000 | bytes 6000000 | tf_op jit(solution)/shard_map/pack_observations/pallas_call | solution.py:617
  18.6 1.9 %collective-permute-start.5 = (f32[16,32,128]{2,1,0:T(8,128)S(1)}, f32[16,32,128]{2,1,0:T(8,128)S(1)}, u32[]{:S(2)}, u32[]{:S(2)}) collective-permute-start(f32[16,32,128]{2,1,0:T(8,128)S(1)} %get-tuple-element.40), channel_id=1, source_target_pairs={{0,1},{1,0},{2,3},{3,2},{4,5},{5,4},{6,7},{7,6},{8,9},{9,8},{10,11... | collective-permute-start | bytes 786440 | tf_op jit(solution)/shard_map/ppermute | solution.py:693
  20.6 1.2 %sum_observations.1.refs_12_ = f32[32,256]{1,0:T(8,128)S(1)} custom-call(s32[2]{0:T(128)S(1)} %pad_add_fusion.place_ref.refs_0_, f32[128,256]{1,0:T(8,128)S(1)} %get-tuple-element.34.values_ref, f32[8,128]{1,0:T(8,128)S(1)} %get-tuple-element.35.marks_ref, f32[8,64]{1,0:T(8,128)S(1)} %get-tuple-element.33.filter_ref.refs_6_.refs_3_, ...), custom_call_target="tpu_custom_call" | custom-call | flops 1000000000 | bytes 2000000 | tf_op jit(solution)/shard_map/sum_observations/pallas_call | solution.py:617
  21.8 2.7 %partial_sums.1 = (f32[4,72,384]{2,1,0:T(8,128)S(1)}, f32[72,128]{1,0:T(8,128)S(1)}, f32[32,128]{1,0:T(8,128)S(1)}, f32[32,128]{1,0:T(8,128)S(1)}, f32[16,24,128...) custom-call(s32[2]{0:T(128)S(1)} %pad_add_fusion.place_ref.refs_0_, f32[4,64,384]{2,1,0:T(8,128)S(1)} %get-tuple-element.28.refs_1_, ...), custom_call_target="tpu_custom_call" | custom-call | flops 1000000000 | bytes 2000000 | tf_op jit(solution)/shard_map/partial_sums/pallas_call | solution.py:617
  24.5 2.4 %collective-permute-start.4 = (f32[16,24,128]{2,1,0:T(8,128)S(1)}, f32[16,24,128]{2,1,0:T(8,128)S(1)}, u32[]{:S(2)}, u32[]{:S(2)}) collective-permute-start(f32[16,24,128]{2,1,0:T(8,128)S(1)} %get-tuple-element.38), channel_id=1, source_target_pairs={{0,1},{1,0},{2,3},{3,2},{4,5},{5,4},{6,7},{7,6},{8,9},{9,8},{10,11... | collective-permute-start | bytes 589832 | tf_op jit(solution)/shard_map/ppermute | solution.py:723
  26.9 1.0 collective-permute-done.4.swapped_ref
  28.1 46.5 %all_to_all.10.in_ref = f32[16,80,128]{2,1,0:T(8,128)S(1)} all-to-all(f32[16,80,128]{2,1,0:T(8,128)S(1)} %join.1), channel_id=1, replica_groups=mesh['band'=16,'z'=16,'core'=2] {'z'}, dimensions={0} | all-to-all | bytes 1310720 | tf_op jit(solution)/shard_map/all_to_all | solution.py:725
  74.7 1.7 %own_row.1 = f32[12,128]{1,0:T(8,128)S(1)} custom-call(s32[2]{0:T(128)S(1)} %pad_add_fusion.place_ref.refs_0_, f32[16,80,128]{2,1,0:T(8,128)S(1)} %all_to_all.10.in_ref, f32[8,64]{1,0:T(8,128)S(1)} %get-tuple-element.33.filter_ref.refs_6_.refs_3_, f32[16,256]{1,0:T(8,128)S(1)} %copy-done.8, f32[8,128]{1,0:T(8,128)S(1)} %copy-done.9, ...), custom_call_target="tpu_custom_call" | custom-call | flops 1000000000 | bytes 2000000 | tf_op jit(solution)/shard_map/own_row/pallas_call | solution.py:617
  76.4 1.8 %all-gather.1.pair_ref = f32[2,12,128]{2,1,0:T(8,128)S(1)} all-gather(f32[1,12,128]{2,1,0:T(8,128)S(1)} %bitcast.8), channel_id=2, replica_groups=mesh['band'=16,'z'=16,'core'=2] {'core'}, dimensions={0}, use_global_device_ids=true | all-gather | bytes 18432 | tf_op jit(solution)/shard_map/all_gather | solution.py:742
  78.2 0.7 spread_pair.1
  78.9 4.7 %all-to-all-start.1 = ((f32[16,24,128]{2,1,0:T(8,128)}), f32[16,24,128]{2,1,0:T(8,128)S(1)}, u32[]{:S(2)}, u32[]{:S(2)}) async-start(f32[16,24,128]{2,1,0:T(8,128)} %spread_pair.1), calls=%async_computation.1 | async-start | bytes 393216 | tf_op jit(solution)/shard_map/all_to_all | solution.py:744
  83.6 0.9 unpack_observations.1
  84.5 2.4 %collective-permute-start.7 = (f32[96,128]{1,0:T(8,128)S(1)}, f32[96,128]{1,0:T(8,128)S(1)}, u32[]{:S(2)}, u32[]{:S(2)}) collective-permute-start(f32[96,128]{1,0:T(8,128)S(1)} %get-tuple-element.46), channel_id=1, source_target_pairs={{0,31},{1,0},{2,1},{3,2},{4,3},{5,4},{6,5},{7,6},{8,7},{9,8},{10,9... | collective-permute-start | bytes 147464 | tf_op jit(solution)/shard_map/ppermute | solution.py:659
  86.9 5.7 %collective-permute-done.6.corner_left_ref = f32[32,128]{1,0:T(8,128)S(1)} collective-permute-done((f32[32,128]{1,0:T(8,128)S(1)}, f32[32,128]{1,0:T(8,128)S(1)}, u32[]{:S(2)}, u32[]{:S(2)}) %collective-permute-start.6) | collective-permute-done | bytes 16416 | tf_op jit(solution)/shard_map/ppermute | solution.py:659
  92.6 8.3 %all-to-all-done.1.refs_0_ = f32[16,24,128]{2,1,0:T(8,128)S(1)} async-done(((f32[16,24,128]{2,1,0:T(8,128)}), f32[16,24,128]{2,1,0:T(8,128)S(1)}, u32[]{:S(2)}, u32[]{:S(2)}) %all-to-all-start.1) | async-done | bytes 196640 | tf_op jit(solution)/shard_map/all_to_all | solution.py:744
  101.0 0.9 band_edges.1
  101.9 5.2 %collective-permute-start.8 = (f32[56,128]{1,0:T(8,128)S(1)}, f32[56,128]{1,0:T(8,128)S(1)}, u32[]{:S(2)}, u32[]{:S(2)}) collective-permute-start(f32[56,128]{1,0:T(8,128)S(1)} %get-tuple-element.51), channel_id=1, source_target_pairs={{0,32},{32,64},{64,96},{96,128},{128,160},{160,192},{192,224},{224... | collective-permute-start | bytes 86024 | tf_op jit(solution)/shard_map/ppermute | solution.py:659
  107.0 1.9 %collective-permute-start.9 = (f32[56,128]{1,0:T(8,128)S(1)}, f32[56,128]{1,0:T(8,128)S(1)}, u32[]{:S(2)}, u32[]{:S(2)}) collective-permute-start(f32[56,128]{1,0:T(8,128)S(1)} %get-tuple-element.52), channel_id=1, source_target_pairs={{32,0},{64,32},{96,64},{128,96},{160,128},{192,160},{224,192},{256... | collective-permute-start | bytes 86024 | tf_op jit(solution)/shard_map/ppermute | solution.py:659
  109.0 5.9 %collective-permute-done.9.below_ref = f32[56,128]{1,0:T(8,128)S(1)} collective-permute-done((f32[56,128]{1,0:T(8,128)S(1)}, f32[56,128]{1,0:T(8,128)S(1)}, u32[]{:S(2)}, u32[]{:S(2)}) %collective-permute-start.9) | collective-permute-done | bytes 28704 | tf_op jit(solution)/shard_map/ppermute | solution.py:659
  114.9 2.6 %last_stage.1 = (f32[64,270]{1,0:T(8,128)}, f32[64,270]{1,0:T(8,128)}, f32[64,270]{1,0:T(8,128)}) custom-call(s32[2]{0:T(128)S(1)} %pad_add_fusion.place_ref.refs_0_, f32[4,72,384]{2,1,0:T(8,128)S(1)} %get-tuple-element.36.wide_ref, f32[64,128]{1,0:T(8,128)S(1)} %collective-permute-done.refs_2_.left_ref, ...), custom_call_target="tpu_custom_call" | custom-call | flops 1000000000 | bytes 2000000 | tf_op jit(solution)/shard_map/last_stage/pallas_call | solution.py:617
  (31 shorter events, 0.2 us)
Async XLA Ops:
  1.9 19.9 %collective-permute-start.2 = (f32[16,384]{1,0:T(8,128)S(1)}, f32[16,384]{1,0:T(8,128)S(1)}, u32[]{:S(2)}, u32[]{:S(2)}) collective-permute-start(f32[16,384]{1,0:T(8,128)S(1)} %get-tuple-element.31), channel_id=1, source_target_pairs={{0,32},{32,64},{64,96},{96,128},{128,160},{160,192},{192,224},{224... | collective-permute-start | bytes 73736 | tf_op jit(solution)/shard_map/ppermute | solution.py:659
  5.0 16.8 %collective-permute-start.3 = (f32[16,384]{1,0:T(8,128)S(1)}, f32[16,384]{1,0:T(8,128)S(1)}, u32[]{:S(2)}, u32[]{:S(2)}) collective-permute-start(f32[16,384]{1,0:T(8,128)S(1)} %get-tuple-element.32), channel_id=1, source_target_pairs={{32,0},{64,32},{96,64},{128,96},{160,128},{192,160},{224,192},{256... | collective-permute-start | bytes 73736 | tf_op jit(solution)/shard_map/ppermute | solution.py:659
  7.8 14.0 %collective-permute-start = (f32[64,128]{1,0:T(8,128)S(1)}, f32[64,128]{1,0:T(8,128)S(1)}, u32[]{:S(2)}, u32[]{:S(2)}) collective-permute-start(f32[64,128]{1,0:T(8,128)S(1)} %get-tuple-element.29), channel_id=1, source_target_pairs={{0,1},{1,2},{2,3},{3,4},{4,5},{5,6},{6,7},{7,8},{8,9},{9,10},{10,1... | collective-permute-start | bytes 98312 | tf_op jit(solution)/shard_map/ppermute | solution.py:659
  7.8 14.0 %collective-permute-start.1 = (f32[64,128]{1,0:T(8,128)S(1)}, f32[64,128]{1,0:T(8,128)S(1)}, u32[]{:S(2)}, u32[]{:S(2)}) collective-permute-start(f32[64,128]{1,0:T(8,128)S(1)} %get-tuple-element.30), channel_id=1, source_target_pairs={{0,31},{1,0},{2,1},{3,2},{4,3},{5,4},{6,5},{7,6},{8,7},{9,8},{10,9... | collective-permute-start | bytes 98312 | tf_op jit(solution)/shard_map/ppermute | solution.py:659
  16.2 4.3 %copy-start.4 = (f32[384,256]{1,0:T(8,128)S(1)}, f32[384,256]{1,0:T(8,128)}, u32[]{:S(2)}) copy-start(f32[384,256]{1,0:T(8,128)} %constant.36.clone.table_ref.refs_10_) | copy-start | bytes 1179652
  16.2 4.3 %copy-start.6 = (f32[32,128]{1,0:T(8,128)S(1)}, f32[32,128]{1,0:T(8,128)}, u32[]{:S(2)}) copy-start(f32[32,128]{1,0:T(8,128)} %constant.35.clone.sin_ref.refs_9_) | copy-start | bytes 49156
  16.2 4.3 %copy-start.7 = (f32[32,128]{1,0:T(8,128)S(1)}, f32[32,128]{1,0:T(8,128)}, u32[]{:S(2)}) copy-start(f32[32,128]{1,0:T(8,128)} %constant.34.clone.cos_ref.refs_8_) | copy-start | bytes 49156
  18.6 9.4 %collective-permute-start.5 = (f32[16,32,128]{2,1,0:T(8,128)S(1)}, f32[16,32,128]{2,1,0:T(8,128)S(1)}, u32[]{:S(2)}, u32[]{:S(2)}) collective-permute-start(f32[16,32,128]{2,1,0:T(8,128)S(1)} %get-tuple-element.40), channel_id=1, source_target_pairs={{0,1},{1,0},{2,3},{3,2},{4,5},{5,4},{6,7},{7,6},{8,9},{9,8},{10,11... | collective-permute-start | bytes 786440 | tf_op jit(solution)/shard_map/ppermute | solution.py:693
  20.5 1.3 %copy-start = (f32[384,512]{1,0:T(8,128)S(1)}, f32[384,512]{1,0:T(8,128)}, u32[]{:S(2)}) copy-start(f32[384,512]{1,0:T(8,128)} %constant.38.clone.refs_11_) | copy-start | bytes 2359300
  20.6 1.3 %copy-start.5 = (f32[72,128]{1,0:T(8,128)S(1)}, f32[72,128]{1,0:T(8,128)}, u32[]{:S(2)}) copy-start(f32[72,128]{1,0:T(8,128)} %constant.37.clone.refs_7_.terms_ref) | copy-start | bytes 110596
  24.5 3.5 %collective-permute-start.4 = (f32[16,24,128]{2,1,0:T(8,128)S(1)}, f32[16,24,128]{2,1,0:T(8,128)S(1)}, u32[]{:S(2)}, u32[]{:S(2)}) collective-permute-start(f32[16,24,128]{2,1,0:T(8,128)S(1)} %get-tuple-element.38), channel_id=1, source_target_pairs={{0,1},{1,0},{2,3},{3,2},{4,5},{5,4},{6,7},{7,6},{8,9},{9,8},{10,11... | collective-permute-start | bytes 589832 | tf_op jit(solution)/shard_map/ppermute | solution.py:723
  28.0 46.6 %copy-start.1 = (f32[512,256]{1,0:T(8,128)S(1)}, f32[512,256]{1,0:T(8,128)}, u32[]{:S(2)}) copy-start(f32[512,256]{1,0:T(8,128)} %constant.42.clone.from_grid_ref) | copy-start | bytes 1572868
  28.1 46.6 %copy-start.2 = (f32[256,512]{1,0:T(8,128)S(1)}, f32[256,512]{1,0:T(8,128)}, u32[]{:S(2)}) copy-start(f32[256,512]{1,0:T(8,128)} %constant.41.clone.to_grid_ref) | copy-start | bytes 1572868
  28.1 46.6 %copy-start.8 = (f32[16,256]{1,0:T(8,128)S(1)}, f32[16,256]{1,0:T(8,128)}, u32[]{:S(2)}) copy-start(f32[16,256]{1,0:T(8,128)} %constant.39.clone.lines_ref) | copy-start | bytes 49156
  28.1 46.6 %copy-start.9 = (f32[8,128]{1,0:T(8,128)S(1)}, f32[8,128]{1,0:T(8,128)}, u32[]{:S(2)}) copy-start(f32[8,128]{1,0:T(8,128)} %constant.40.clone.slope_ref) | copy-start | bytes 12292
  78.9 22.1 %all-to-all-start.1 = ((f32[16,24,128]{2,1,0:T(8,128)}), f32[16,24,128]{2,1,0:T(8,128)S(1)}, u32[]{:S(2)}, u32[]{:S(2)}) async-start(f32[16,24,128]{2,1,0:T(8,128)} %spread_pair.1), calls=%async_computation.1 | async-start | bytes 393216 | tf_op jit(solution)/shard_map/all_to_all | solution.py:744
  84.5 8.1 %collective-permute-start.7 = (f32[96,128]{1,0:T(8,128)S(1)}, f32[96,128]{1,0:T(8,128)S(1)}, u32[]{:S(2)}, u32[]{:S(2)}) collective-permute-start(f32[96,128]{1,0:T(8,128)S(1)} %get-tuple-element.46), channel_id=1, source_target_pairs={{0,31},{1,0},{2,1},{3,2},{4,3},{5,4},{6,5},{7,6},{8,7},{9,8},{10,9... | collective-permute-start | bytes 147464 | tf_op jit(solution)/shard_map/ppermute | solution.py:659
  86.9 5.7 %collective-permute-start.6 = (f32[32,128]{1,0:T(8,128)S(1)}, f32[32,128]{1,0:T(8,128)S(1)}, u32[]{:S(2)}, u32[]{:S(2)}) collective-permute-start(f32[32,128]{1,0:T(8,128)S(1)} %get-tuple-element.44), channel_id=1, source_target_pairs={{0,1},{1,2},{2,3},{3,4},{4,5},{5,6},{6,7},{7,8},{8,9},{9,10},{10,1... | collective-permute-start | bytes 49160 | tf_op jit(solution)/shard_map/ppermute | solution.py:659
  92.6 22.3 %copy-start.3 = (f32[256,384]{1,0:T(8,128)S(1)}, f32[256,384]{1,0:T(8,128)}, u32[]{:S(2)}) copy-start(f32[256,384]{1,0:T(8,128)} %constant.43.clone.table_ref) | copy-start | bytes 1179652
  101.9 7.1 %collective-permute-start.8 = (f32[56,128]{1,0:T(8,128)S(1)}, f32[56,128]{1,0:T(8,128)S(1)}, u32[]{:S(2)}, u32[]{:S(2)}) collective-permute-start(f32[56,128]{1,0:T(8,128)S(1)} %get-tuple-element.51), channel_id=1, source_target_pairs={{0,32},{32,64},{64,96},{96,128},{128,160},{160,192},{192,224},{224... | collective-permute-start | bytes 86024 | tf_op jit(solution)/shard_map/ppermute | solution.py:659
  107.0 7.9 %collective-permute-start.9 = (f32[56,128]{1,0:T(8,128)S(1)}, f32[56,128]{1,0:T(8,128)S(1)}, u32[]{:S(2)}, u32[]{:S(2)}) collective-permute-start(f32[56,128]{1,0:T(8,128)S(1)} %get-tuple-element.52), channel_id=1, source_target_pairs={{32,0},{64,32},{96,64},{128,96},{160,128},{192,160},{224,192},{256... | collective-permute-start | bytes 86024 | tf_op jit(solution)/shard_map/ppermute | solution.py:659

commit v3 on v2

--- a/solution.py
+++ b/solution.py
@@ -2,6 +2,7 @@
 
 import jax
 import jax.numpy as jnp
+import ml_dtypes
 import numpy as np
 from jax import lax
 from jax.experimental import pallas as pl
@@ -24,6 +25,24 @@
     return jnp.dot(left, right, precision=lax.Precision.HIGHEST, preferred_element_type=F32)
 
 
+def halves_of(value):
+    high = value.astype(jnp.bfloat16)
+    return high, (value - high.astype(F32)).astype(jnp.bfloat16)
+
+
+def bdot(left, right):
+    return jnp.dot(left, right, preferred_element_type=F32)
+
+
+def tdot(left, table_ref):
+    high, low = halves_of(left)
+    return bdot(high, table_ref[0]) + bdot(low, table_ref[0]) + bdot(high, table_ref[1])
+
+
+def mdot(left, right):
+    return jnp.dot(left, right, precision=lax.Precision.HIGH, preferred_element_type=F32)
+
+
 def iota(shape, dim):
     return lax.broadcasted_iota(jnp.int32, shape, dim)
 
@@ -75,18 +94,25 @@
     d_hbm,
     mask_hbm,
     keep_hbm,
+    owner_hbm,
+    row_hbm,
+    count_hbm,
     fields_ref,
     west_ref,
     east_ref,
     north_ref,
     south_ref,
     filter_ref,
+    marks_ref,
     h_ref,
     e_ref,
     n_ref,
     d_ref,
     mask_ref,
     keep_ref,
+    owner_ref,
+    row_ref,
+    count_ref,
     sems,
 ):
     pairs = (
@@ -96,6 +122,9 @@
         (d_hbm, d_ref),
         (mask_hbm, mask_ref),
         (keep_hbm, keep_ref),
+        (owner_hbm, owner_ref),
+        (row_hbm, row_ref),
+        (count_hbm, count_ref),
     )
     copies = [pltpu.make_async_copy(a, b, sems.at[i]) for i, (a, b) in enumerate(pairs)]
     for copy in copies:
@@ -107,6 +136,9 @@
     filter_ref[0:1, :] = mask_ref[...].astype(F32)
     filter_ref[1:2, :] = keep_ref[...]
     filter_ref[2:8, :] = jnp.zeros((6, rows), F32)
+    for i, in_ref in enumerate((owner_ref, row_ref, count_ref)):
+        marks_ref[i : i + 1, :] = in_ref[...].astype(F32)
+    marks_ref[3:8, :] = jnp.zeros((5, marks_ref.shape[1]), F32)
     weight = to_col(mask_ref[...].astype(F32) * (1.0 - keep_ref[...]))
     level = d_ref[...].astype(F32)
     wet = (level > 0).astype(F32)
@@ -168,13 +200,16 @@
     table_ref,
     kernel_ref,
     placed_ref,
+    near_ref,
+    far_ref,
     ext_ref,
     weight_ref,
     west_ref,
     east_ref,
     mine_ref,
     other_ref,
-    stack_ref,
+    high_ref,
+    low_ref,
     cells_ref,
 ):
     rows = fields_ref.shape[1]
@@ -224,14 +259,22 @@
     )
     new_east = east_rest - rotation * north_rest + COURANT * share * metric * lon_diff(middle)
     new_north = north_rest + rotation * east_rest + COURANT * share * lat_diff(middle)
-    chosen = slot_rows(mask, place_ref[1] % 2, devices)
+    chosen = slot_rows(mask, place_ref[1] % 2, devices).astype(jnp.bfloat16)
     sources = (height, east, north, low_height, lat_diff(low_height), middle, new_east, new_north)
     for v, field in enumerate(sources):
-        stack_ref[devices * v : devices * v + devices, :] = hdot(chosen, field[0:rows, :])
+        lines = slice(devices * v, devices * v + devices)
+        high, low = halves_of(field[0:rows, :])
+        high_ref[lines, :] = bdot(chosen, high).astype(jnp.bfloat16)
+        low_ref[lines, :] = bdot(chosen, low).astype(jnp.bfloat16)
+    mine_ref[:, 24:56, :] = near_ref[...]
+    other_ref[:, 24:56, :] = far_ref[...]
     level = ext_ref[3, 0:rows, :]
-    cells_ref[0:devices, :] = hdot(chosen, (level > 0).astype(F32))
-    cells_ref[devices : 2 * devices, :] = hdot(chosen, share[0:rows, :])
-    sums = hdot(stack_ref[...], table_ref[...])
+    for c, cells in enumerate(((level > 0).astype(F32), level)):
+        cells_ref[devices * c : devices * c + devices, :] = bdot(
+            chosen, cells.astype(jnp.bfloat16)
+        ).astype(jnp.bfloat16)
+    sums = bdot(high_ref[...], table_ref[0]) + bdot(low_ref[...], table_ref[0])
+    sums = sums + bdot(high_ref[...], table_ref[1])
     turn_cos, turn_sin = cos_ref[pl.ds(lon, 1), :], sin_ref[pl.ds(lon, 1), :]
     for v in range(len(sources)):
         lines = slice(devices * v, devices * v + devices)
@@ -244,7 +287,8 @@
         for i, value in enumerate((all_cos, all_sin)):
             mine_ref[:, 2 * v + i, :] = value[0:half]
             other_ref[:, 2 * v + i, :] = value[half:devices]
-    spread = pltpu.roll(hdot(cells_ref[...], kernel_ref[...]), lon * (GRID // devices), 1)
+    spread = bdot(cells_ref[...], kernel_ref[0]) + bdot(cells_ref[...], kernel_ref[1])
+    spread = pltpu.roll(spread, lon * (GRID // devices), 1)
     for c in range(2):
         for i in range(4):
             part = spread[devices * c : devices * c + devices, 128 * i : 128 * i + 128]
@@ -253,45 +297,15 @@
             other_ref[:, at, :] = part[half:devices]
 
 
-def pack_observations(
-    place_ref,
-    values_hbm,
-    owner_hbm,
-    row_hbm,
-    count_hbm,
-    near_ref,
-    far_ref,
-    kept_ref,
-    marks_ref,
-    values_ref,
-    owner_ref,
-    row_ref,
-    count_ref,
-    sems,
-):
-    pairs = (
-        (values_hbm, values_ref),
-        (owner_hbm, owner_ref),
-        (row_hbm, row_ref),
-        (count_hbm, count_ref),
-    )
-    copies = [pltpu.make_async_copy(a, b, sems.at[i]) for i, (a, b) in enumerate(pairs)]
-    for copy in copies:
-        copy.start()
-    for copy in copies:
-        copy.wait()
+def pack_observations(place_ref, values_ref, marks_ref, near_ref, far_ref, kept_ref):
     number, width = values_ref.shape
     half = near_ref.shape[0]
     core = place_ref[1] % 2
-    values = jnp.where(
-        iota((number, width), 1) < to_col(count_ref[...]), values_ref[...], 0.0
-    )
+    lengths = to_col(marks_ref[2:3, :])
+    values = jnp.where(iota((number, width), 1).astype(F32) < lengths, values_ref[...], 0.0)
     kept_ref[...] = values
-    owner_row = owner_ref[...]
+    owner_row = marks_ref[0:1, :].astype(jnp.int32)
     owner_col = to_col(owner_row)
-    marks_ref[0:1, :] = owner_row.astype(F32)
-    marks_ref[1:2, :] = row_ref[...].astype(F32)
-    marks_ref[2:8, :] = jnp.zeros((6, number), F32)
     same = owner_col == owner_row
     before = same & (iota((number, number), 0) < iota((number, number), 1))
     arrival_row = jnp.sum(before.astype(jnp.int32), axis=0, keepdims=True)
@@ -299,7 +313,7 @@
     arrival_col = jnp.sum(after.astype(jnp.int32), axis=1, keepdims=True)
     chip_row, core_row = owner_row // 2, owner_row % 2
     target = chip_row * 16 + arrival_row
-    label = row_ref[...].astype(F32)
+    label = marks_ref[1:2, :]
     arrived = (iota((number, 128), 1) == arrival_col).astype(F32)
     for out_ref, side in ((near_ref, core), (far_ref, 1 - core)):
         goes = core_row == side
@@ -318,31 +332,32 @@
     number, width = values_ref.shape
     devices = cos_ref.shape[0]
     owner_col = to_col(marks_ref[0:1, :])
-    sums = hdot(values_ref[...], table_ref[0:width, :])
+    sums = tdot(values_ref[...], table_ref.at[:, 0:width, :])
     whose = (iota((number, devices), 1).astype(F32) == owner_col).astype(F32)
-    turn_cos, turn_sin = hdot(whose, cos_ref[...]), hdot(whose, sin_ref[...])
+    turn_cos, turn_sin = mdot(whose, cos_ref[...]), mdot(whose, sin_ref[...])
     on_cos, on_sin = sums[:, 0:128], sums[:, 128:256]
     all_cos = on_cos * turn_cos - on_sin * turn_sin
     all_sin = on_sin * turn_cos + on_cos * turn_sin
     mask = filter_ref[0:1, :]
     rows = mask.shape[1]
     in_row = (iota((rows, number), 0).astype(F32) == marks_ref[1:2, :]).astype(F32)
-    chosen = hdot(slot_rows(mask, place_ref[1] % 2, devices), in_row)
-    placed_ref[:, 0:128] = hdot(chosen, all_cos)
-    placed_ref[:, 128:256] = hdot(chosen, all_sin)
-
-
-def join(mine_ref, swapped_ref, near_ref, far_ref, out_ref):
-    half = out_ref.shape[0]
-    out_ref[:, 0:24, :] = mine_ref[...] + swapped_ref[...]
-    out_ref[:, 24:48, :] = near_ref[:, 0:24, :]
-    out_ref[:, 48:72, :] = far_ref[:, 0:24, :]
-    out_ref[:, 72:80, :] = jnp.zeros((half, 8, 128), F32)
-    out_ref[:, 72, :] = near_ref[:, 24, :]
-    out_ref[:, 73, :] = far_ref[:, 24, :]
-
-
-def unpack_observations(in_ref, corner_ref, dep_ref, west_ref):
+    chosen = mdot(slot_rows(mask, place_ref[1] % 2, devices), in_row)
+    placed_ref[:, 0:128] = mdot(chosen, all_cos)
+    placed_ref[:, 128:256] = mdot(chosen, all_sin)
+
+
+def join(mine_ref, swapped_ref, out_ref):
+    for i in range(12):
+        pair = slice(2 * i, 2 * i + 2)
+        out_ref[:, i, :, :] = mine_ref[:, pair, :] + swapped_ref[:, pair, :]
+    for i in range(12, 24):
+        out_ref[:, i, :, :] = mine_ref[:, 2 * i : 2 * i + 2, :]
+        out_ref[:, i + 12, :, :] = swapped_ref[:, 2 * i : 2 * i + 2, :]
+    out_ref[:, 36, 0, :] = mine_ref[:, 48, :]
+    out_ref[:, 36, 1, :] = swapped_ref[:, 48, :]
+
+
+def unpack_observations(in_ref, corner_ref, dep_ref, west_ref, data_ref):
     half = in_ref.shape[0]
     rows = dep_ref.shape[0]
     lines = 4 * CAP
@@ -352,11 +367,13 @@
     own = iota((half, total), 1) // lines == iota((half, total), 0)
     for s in range(2):
         here = (spot // (2 * CAP) == s) & (spot % CAP == iota((128, total), 0))
-        across = hdot(in_ref[:, 72 + s, :], here.astype(F32))
+        across = hdot(in_ref[:, 36, s, :], here.astype(F32))
         label_row = label_row + jnp.sum(jnp.where(own, across, 0.0), axis=0, keepdims=True)
     line = iota((rows, total), 1) % lines
     hit = iota((rows, total), 0).astype(F32) == label_row
-    data = in_ref[:, 24 : 24 + lines, :].reshape(total, 128)
+    for i in range(2 * CAP):
+        data_ref[:, 2 * i : 2 * i + 2, :] = in_ref[:, 12 + i, :, :]
+    data = data_ref[...].reshape(total, 128)
     for i in range(2):
         side = (hit & ((line // CAP) % 2 == i)).astype(F32)
         dep_ref[:, 128 * i : 128 * i + 128] = hdot(side, data)
@@ -373,14 +390,19 @@
     slope_ref,
     to_grid_ref,
     from_grid_ref,
-    res_ref,
+    out_ref,
     left_ref,
     grid_ref,
+    res_ref,
+    sum_ref,
 ):
     band, lon = place_ref[0], place_ref[1]
-    sums = in_ref[0, 0:24, :]
+    pairs = in_ref[0, 0:12, :, :]
     for i in range(1, in_ref.shape[0]):
-        sums = sums + in_ref[i, 0:24, :]
+        pairs = pairs + in_ref[i, 0:12, :, :]
+    for i in range(12):
+        sum_ref[2 * i : 2 * i + 2, :] = pairs[i]
+    sums = sum_ref[...]
     mask, keep = filter_ref[0:1, :], filter_ref[1:2, :]
     chosen = ((rank_in_row(mask) == lon) & (mask == 1)).astype(F32)
 
@@ -407,27 +429,26 @@
     for i, (on_cos, on_sin) in enumerate(pairs):
         left_ref[i : i + 1, 0:128] = on_cos
         left_ref[i : i + 1, 128:256] = on_sin
-    at = hdot(left_ref[...], to_grid_ref[...])
+    at = tdot(left_ref[...], to_grid_ref)
     wet = jnp.concatenate([line(16), line(17), line(18), line(19)], axis=1)
-    share = COURANT * jnp.concatenate([line(20), line(21), line(22), line(23)], axis=1)
+    share = (COURANT / LEVELS) * jnp.concatenate([line(20), line(21), line(22), line(23)], axis=1)
     grid_ref[...] = jnp.zeros(grid_ref.shape, F32)
     grid_ref[0:1, :] = wet * at[0:1] + share * at[1:2]
     grid_ref[1:2, :] = wet * at[2:3] + share * at[3:4]
-    back = hdot(grid_ref[...], from_grid_ref[...])
+    back = tdot(grid_ref[...], from_grid_ref)
     res_ref[0:6, :] = sums[0:6]
     res_ref[6:8, :] = sums[10:12] + sums[6:8]
     for i in range(2):
         res_ref[8 + 2 * i : 9 + 2 * i, :] = line(12 + 2 * i) + back[i : i + 1, 0:128]
         res_ref[9 + 2 * i : 10 + 2 * i, :] = line(13 + 2 * i) + back[i : i + 1, 128:256]
-
-
-def spread_pair(pair_ref, out_ref):
-    both = jnp.concatenate([pair_ref[0], pair_ref[1]], axis=0)
-    out_ref[...] = jnp.broadcast_to(both[None], out_ref.shape)
+    for i in range(3):
+        out_ref[:, i, :, :] = jnp.broadcast_to(
+            res_ref[4 * i : 4 * i + 4, :][None], (out_ref.shape[0], 4, 128)
+        )
 
 
 def band_edges(cols, all_ref, dep_ref, edge_ref, filter_ref, coef_ref, depx_ref, north_ref, south_ref):
-    half = all_ref.shape[0]
+    half = all_ref.shape[1]
     rows = dep_ref.shape[0]
     mask = filter_ref[0:1, :]
     rank = to_col(rank_in_row(mask))
@@ -442,7 +463,9 @@
         ((2 * iota((rows, half), 1) + c == rank) & kept).astype(F32) for c in range(2)
     ]
     for v in range(12):
-        own = hdot(chosen[0], all_ref[:, v, :]) + hdot(chosen[1], all_ref[:, 12 + v, :])
+        own = hdot(chosen[0], all_ref[0, :, v // 4, v % 4, :]) + hdot(
+            chosen[1], all_ref[1, :, v // 4, v % 4, :]
+        )
         coef_ref[v] = own
         north_ref[4 * v : 4 * v + 4, :] = own[0:4]
         south_ref[4 * v : 4 * v + 4, :] = own[rows - 4 : rows]
@@ -455,6 +478,18 @@
         out_ref[54:56, :] = jnp.zeros((2, 128), F32)
 
 
+def own_modes(place_ref, coef_ref, cos_ref, sin_ref, table_ref, low_ref, stack_ref):
+    rows = coef_ref.shape[1]
+    lon = place_ref[1]
+    turn_cos, turn_sin = cos_ref[pl.ds(lon, 1), :], sin_ref[pl.ds(lon, 1), :]
+    for f in range(6):
+        lines = slice(rows * f, rows * f + rows)
+        on_cos, on_sin = coef_ref[2 * f], coef_ref[2 * f + 1]
+        stack_ref[lines, 0:128] = on_cos * turn_cos + on_sin * turn_sin
+        stack_ref[lines, 128:256] = on_sin * turn_cos - on_cos * turn_sin
+    low_ref[...] = tdot(stack_ref[...], table_ref)
+
+
 def last_stage(
     place_ref,
     wide_ref,
@@ -463,7 +498,7 @@
     corner_left_ref,
     corner_right_ref,
     weight_ref,
-    coef_ref,
+    own_ref,
     depx_ref,
     above_ref,
     below_ref,
@@ -477,6 +512,7 @@
     stack_ref,
     dep_ref,
     ext_ref,
+    low_ref,
 ):
     ext = ext_ref.shape[1]
     rows, cols = h_ref.shape
@@ -496,22 +532,16 @@
     band, lon = place_ref[0], place_ref[1]
     turn_cos, turn_sin = cos_ref[pl.ds(lon, 1), :], sin_ref[pl.ds(lon, 1), :]
     for f in range(6):
-        for lines, on_cos, on_sin in (
-            (slice(ext * f, ext * f + rows), coef_ref[2 * f], coef_ref[2 * f + 1]),
-            (
-                slice(ext * f + rows, ext * f + rows + 4),
-                below_ref[8 * f : 8 * f + 4, :],
-                below_ref[8 * f + 4 : 8 * f + 8, :],
-            ),
-            (
-                slice(ext * f + rows + 4, ext * f + ext),
-                above_ref[8 * f : 8 * f + 4, :],
-                above_ref[8 * f + 4 : 8 * f + 8, :],
-            ),
-        ):
-            stack_ref[lines, 0:128] = on_cos * turn_cos + on_sin * turn_sin
-            stack_ref[lines, 128:256] = on_sin * turn_cos - on_cos * turn_sin
-    low = hdot(stack_ref[...], table_ref[...])
+        for at, in_ref in ((8 * f, below_ref), (8 * f + 4, above_ref)):
+            on_cos = in_ref[8 * f : 8 * f + 4, :]
+            on_sin = in_ref[8 * f + 4 : 8 * f + 8, :]
+            stack_ref[at : at + 4, 0:128] = on_cos * turn_cos + on_sin * turn_sin
+            stack_ref[at : at + 4, 128:256] = on_sin * turn_cos - on_cos * turn_sin
+    edges = tdot(stack_ref[...], table_ref)
+    for f in range(6):
+        low_ref[ext * f : ext * f + rows, :] = own_ref[rows * f : rows * f + rows, :]
+        low_ref[ext * f + rows : ext * f + ext, :] = edges[8 * f : 8 * f + 8, :]
+    low = low_ref
     dep_ref[0:rows, :] = depx_ref[...]
     dep_ref[rows:ext, :] = jnp.zeros((ext - rows, LANES), F32)
     for in_ref, at in ((below_ref, rows), (above_ref, ext - 2)):
@@ -595,7 +625,13 @@
         terms=terms,
         lines=lines,
     )
-    return {name: value.astype(np.float32) for name, value in made.items()}
+    for name, value in made.items():
+        made[name] = value.astype(np.float32)
+        if name in ("analyse", "evaluate", "kernel", "to_grid", "from_grid"):
+            high = value.astype(ml_dtypes.bfloat16)
+            low = (value - high.astype(np.float64)).astype(ml_dtypes.bfloat16)
+            made[name] = np.stack([high, low])
+    return made
 
 
 VMEM = pl.BlockSpec(memory_space=pltpu.VMEM)
@@ -620,7 +656,9 @@
         out_shape=shapes,
         in_specs=specs,
         out_specs=[VMEM] * len(shapes),
-        scratch_shapes=held + [pltpu.VMEM(shape, F32) for shape in scratch],
+        scratch_shapes=held + [
+            pltpu.VMEM(shape, F32) if isinstance(shape, tuple) else shape for shape in scratch
+        ],
         cost_estimate=pl.CostEstimate(
             flops=int(cost * 1e9), bytes_accessed=int(cost * 2e6), transcendentals=0
         ),
@@ -658,10 +696,10 @@
         pairs = [(i, (i + shift) % count) for i in range(count) if closed or 0 <= i + shift < count]
         return lax.ppermute(value, axis, pairs)
 
-    fields, west, east, north, south, kept = call(
+    fields, west, east, north, south, kept, marks = call(
         pack_tile,
         "pack_tile",
-        [(4, rows, LANES), (rows, 128), (rows, 128)] + [(4 * HALO, LANES)] * 2 + [(8, rows)],
+        [(4, rows, LANES), (rows, 128), (rows, 128)] + [(4 * HALO, LANES)] * 2 + [(8, rows), (8, number)],
         (
             back_height,
             back_east,
@@ -669,28 +707,23 @@
             depth_level,
             polar_mask.reshape(1, rows),
             keep_share.reshape(1, rows),
-        ),
-        direct=range(6),
-    )
-    below, above = send(north, "band", -1, False), send(south, "band", 1, False)
-    right, left = send(west, LON, -1, True), send(east, LON, 1, True)
-    other_core = [(i, i ^ 1) for i in range(devices)]
-    near, far, values, marks = call(
-        pack_observations,
-        "pack_observations",
-        [(half, 32, 128), (half, 32, 128), (number, width), (8, number)],
-        (
-            place,
-            obs_values,
             obs_owner.reshape(1, number),
             obs_row.reshape(1, number),
             obs_count.reshape(1, number),
         ),
+        direct=range(9),
+    )
+    below, above = send(north, "band", -1, False), send(south, "band", 1, False)
+    right, left = send(west, LON, -1, True), send(east, LON, 1, True)
+    other_core = [(i, i ^ 1) for i in range(devices)]
+    near, far, values = call(
+        pack_observations,
+        "pack_observations",
+        [(half, 32, 128), (half, 32, 128), (number, width)],
+        (place, obs_values, marks),
         cost=3.0,
         scalars=True,
-        direct=range(1, 5),
-    )
-    far = lax.ppermute(far, LON, other_core)
+    )
     (placed,) = call(
         sum_observations,
         "sum_observations",
@@ -701,7 +734,7 @@
     wide, weight, corner_west, corner_east, mine, other = call(
         lambda *refs: partial_sums(cols, *refs),
         "partial_sums",
-        [(4, ext, LANES), (ext, 128)] + [(8 * HALO, 128)] * 2 + [(half, 24, 128)] * 2,
+        [(4, ext, LANES), (ext, 128)] + [(8 * HALO, 128)] * 2 + [(half, 56, 128)] * 2,
         (
             place,
             fields,
@@ -716,17 +749,19 @@
             made["analyse"],
             made["kernel"],
             placed,
+            near,
+            far,
         ),
-        scratch=[(8 * devices, LANES), (2 * devices, LANES)],
+        scratch=[pltpu.VMEM((n * devices, LANES), jnp.bfloat16) for n in (8, 8, 2)],
         scalars=True,
     )
     swapped = lax.ppermute(other, LON, other_core)
-    (joined,) = call(join, "join", [(half, 80, 128)], (mine, swapped, near, far))
+    (joined,) = call(join, "join", [(half, 37, 2, 128)], (mine, swapped))
     owned = lax.all_to_all(joined, "z", split_axis=0, concat_axis=0, tiled=True)
-    (result,) = call(
+    (spread,) = call(
         own_row,
         "own_row",
-        [(12, 128)],
+        [(half, 3, 4, 128)],
         (
             place,
             owned,
@@ -736,17 +771,17 @@
             made["to_grid"],
             made["from_grid"],
         ),
-        scratch=[(8, 256), (8, GRID)],
+        scratch=[(8, 256), (8, GRID), (12, 128), (24, 128)],
         scalars=True,
     )
-    pair = lax.all_gather(result, "core", axis=0, tiled=False)
-    (spread,) = call(spread_pair, "spread_pair", [(half, 24, 128)], (pair,))
-    everyone = lax.all_to_all(spread, "z", split_axis=0, concat_axis=0, tiled=True)
+    shared = lax.all_to_all(spread, "z", split_axis=0, concat_axis=0, tiled=True)
+    everyone = lax.all_gather(shared, "core", axis=0, tiled=False)
     dep, west = call(
         unpack_observations,
         "unpack_observations",
         [(rows, LANES), (rows + 8 * HALO, 128)],
         (owned, corner_west),
+        scratch=[(half, 48, 128)],
     )
     corner_east = lax.optimization_barrier((corner_east, spread))[0]
     corner_right, corner_left = send(west, LON, -1, True), send(corner_east, LON, 1, True)
@@ -758,6 +793,14 @@
         (everyone, dep, corner_right, kept),
     )
     below, above = send(north, "band", -1, False), send(south, "band", 1, False)
+    (own,) = call(
+        own_modes,
+        "own_modes",
+        [(6 * rows, LANES)],
+        (place, coef, made["cos"], made["sin"], made["evaluate"]),
+        scratch=[(6 * rows, 256)],
+        scalars=True,
+    )
     return tuple(
         call(
             last_stage,
@@ -771,7 +814,7 @@
                 corner_left,
                 corner_right,
                 weight,
-                coef,
+                own,
                 depx,
                 above,
                 below,
@@ -780,7 +823,7 @@
                 made["sin"],
                 made["evaluate"],
             ),
-            scratch=[(6 * ext, 256), (ext, LANES), (4, ext, LANES)],
+            scratch=[(48, 256), (ext, LANES), (4, ext, LANES), (6 * ext, LANES)],
             scalars=True,
         )
     )

time: 118 us -> 108 us (0.915)
  waiting for transfers between devices: 21.1 us -> 17 us
  starting transfers between devices: 32.7 us -> 29.9 us
  Pallas kernels: 14.3 us -> 12.6 us
  blocking collectives: 48.4 us -> 47.2 us
    ppermute x8, waiting for transfers between devices: 11.7 us -> 5.39 us  [send(): return lax.ppermute(value, axis, pairs)]
    ppermute x1 -> x0, starting transfers between devices: 1.92 us -> none  [on_device(): far = lax.ppermute(far, LON, other_core)]
    pallas_call x10, Pallas kernels: 14.3 us -> 12.6 us  [call(): pl.pallas_call(kernel, name=name, out_shape=shapes, in_specs=specs, out_s...]
    all_to_all x1, waiting for transfers between devices: 8.32 us -> 9.81 us  [on_device(): lax.all_to_all(spread, 'z', split_axis=0, concat_axis=0, tiled=True)]
    all_to_all x1, blocking collectives: 46.5 us -> 45.2 us  [on_device(): owned = lax.all_to_all(joined, 'z', split_axis=0, concat_axis=0, tiled=True)]
  transfers between devices with their start and end apart: 11 -> 10, of which waited for: 4 -> 4; matrix products, arithmetic and copies ran while one was open for 0% -> 0% of each run, Pallas kernels for 6% -> 4%
where the time goes in v3:
time: 108 us
  blocking collectives  47.2 us (44%)
  starting transfers between devices  29.9 us (28%)
  waiting for transfers between devices  17 us (16%)
  Pallas kernels  12.6 us (12%)
    all_to_all x1, blocking collectives, on_device(): owned = lax.all_to_all(joined, 'z', split_axis=0, concat_axis=0, tiled=True)  45.2 us
    ppermute x8, starting transfers between devices, send(): return lax.ppermute(value, axis, pairs)  24.3 us
    pallas_call x10, Pallas kernels, call(): pl.pallas_call(kernel, name=name, out_shape=shapes, in_specs=specs, out_s...  12.6 us
    all_to_all x1, waiting for transfers between devices, on_device(): lax.all_to_all(spread, 'z', split_axis=0, concat_axis=0, tiled=True)  9.81 us
    ppermute x8, waiting for transfers between devices, send(): return lax.ppermute(value, axis, pairs)  5.39 us
    all_to_all x1, starting transfers between devices, on_device(): lax.all_to_all(spread, 'z', split_axis=0, concat_axis=0, tiled=True)  3.66 us
  transfers between devices with their start and end apart: 10, of which 4 were waited for; matrix products, arithmetic and copies ran while one was open for 0% of the time, Pallas kernels for 4%

profile of v3, /device:TPU:24, one launch (start us, length us, event | category | flops | bytes accessed | tf_op | source)
XLA Modules:
  0.0 107.7 jit_solution(7547260050550499190)
XLA Ops:
  0.6 1.3 %pack_tile.1 = (f32[4,64,384]{2,1,0:T(8,128)S(1)}, f32[64,128]{1,0:T(8,128)S(1)}, f32[64,128]{1,0:T(8,128)S(1)}, f32[16,384]{1,0:T(8,128)S(1)}, f32[16,384]{1,0:...) custom-call(f32[64,270]{1,0:T(8,128)} %h_hbm.1, f32[64,270]{1,0:T(8,128)} %e_hbm.1, f32[64,270]{1,0:T(8,128)} %n_hbm.1, ...), custom_call_target="tpu_custom_call" | custom-call | flops 1000000000 | bytes 2000000 | tf_op jit(solution)/shard_map/pack_tile/pallas_call | solution.py:653
  2.0 3.1 %collective-permute-start.2 = (f32[16,384]{1,0:T(8,128)S(1)}, f32[16,384]{1,0:T(8,128)S(1)}, u32[]{:S(2)}, u32[]{:S(2)}) collective-permute-start(f32[16,384]{1,0:T(8,128)S(1)} %get-tuple-element.31), channel_id=1, source_target_pairs={{0,32},{32,64},{64,96},{96,128},{128,160},{160,192},{192,224},{224... | collective-permute-start | bytes 73736 | tf_op jit(solution)/shard_map/ppermute | solution.py:697
  5.0 2.8 %collective-permute-start.3 = (f32[16,384]{1,0:T(8,128)S(1)}, f32[16,384]{1,0:T(8,128)S(1)}, u32[]{:S(2)}, u32[]{:S(2)}) collective-permute-start(f32[16,384]{1,0:T(8,128)S(1)} %get-tuple-element.32), channel_id=1, source_target_pairs={{32,0},{64,32},{96,64},{128,96},{160,128},{192,160},{224,192},{256... | collective-permute-start | bytes 73736 | tf_op jit(solution)/shard_map/ppermute | solution.py:697
  7.9 8.4 %collective-permute-start.1 = (f32[64,128]{1,0:T(8,128)S(1)}, f32[64,128]{1,0:T(8,128)S(1)}, u32[]{:S(2)}, u32[]{:S(2)}) collective-permute-start(f32[64,128]{1,0:T(8,128)S(1)} %get-tuple-element.30), channel_id=1, source_target_pairs={{0,31},{1,0},{2,1},{3,2},{4,3},{5,4},{6,5},{7,6},{8,7},{9,8},{10,9... | collective-permute-start | bytes 98312 | tf_op jit(solution)/shard_map/ppermute | solution.py:697
  16.3 1.4 %pack_observations.1 = (f32[16,32,128]{2,1,0:T(8,128)S(1)}, f32[16,32,128]{2,1,0:T(8,128)S(1)}, f32[128,256]{1,0:T(8,128)S(1)}) custom-call(s32[2]{0:T(128)S(1)} %pad_add_fusion.place_ref.refs_0_, f32[128,256]{1,0:T(8,128)S(1)} %copy-done, f32[8,128]{1,0:T(8,128)S(1)} %get-tuple-element.34.marks_ref), custom_call_target="tpu_custom_call" | custom-call | flops 3000000000 | bytes 6000000 | tf_op jit(solution)/shard_map/pack_observations/pallas_call | solution.py:653
  17.8 1.0 sum_observations.1.refs_12_
  18.9 1.8 %partial_sums.1 = (f32[4,72,384]{2,1,0:T(8,128)S(1)}, f32[72,128]{1,0:T(8,128)S(1)}, f32[32,128]{1,0:T(8,128)S(1)}, f32[32,128]{1,0:T(8,128)S(1)}, f32[16,56,128...) custom-call(s32[2]{0:T(128)S(1)} %pad_add_fusion.place_ref.refs_0_, f32[4,64,384]{2,1,0:T(8,128)S(1)} %get-tuple-element.28.refs_1_, ...), custom_call_target="tpu_custom_call" | custom-call | flops 1000000000 | bytes 2000000 | tf_op jit(solution)/shard_map/partial_sums/pallas_call | solution.py:653
  20.7 1.9 %collective-permute-start.4 = (f32[16,56,128]{2,1,0:T(8,128)S(1)}, f32[16,56,128]{2,1,0:T(8,128)S(1)}, u32[]{:S(2)}, u32[]{:S(2)}) collective-permute-start(f32[16,56,128]{2,1,0:T(8,128)S(1)} %get-tuple-element.40), channel_id=1, source_target_pairs={{0,1},{1,0},{2,3},{3,2},{4,5},{5,4},{6,7},{7,6},{8,9},{9,8},{10,11... | collective-permute-start | bytes 1376264 | tf_op jit(solution)/shard_map/ppermute | solution.py:758
  22.7 1.8 %collective-permute-done.4.swapped_ref = f32[16,56,128]{2,1,0:T(8,128)S(1)} collective-permute-done((f32[16,56,128]{2,1,0:T(8,128)S(1)}, f32[16,56,128]{2,1,0:T(8,128)S(1)}, u32[]{:S(2)}, u32[]{:S(2)}) %collective-permute-start.4) | collective-permute-done | bytes 458784 | tf_op jit(solution)/shard_map/ppermute | solution.py:758
  24.4 0.1 join.1
  24.6 45.2 %all_to_all.10.in_ref = f32[16,37,2,128]{3,2,1,0:T(2,128)S(1)} all-to-all(f32[16,37,2,128]{3,2,1,0:T(2,128)S(1)} %join.1), channel_id=1, replica_groups=mesh['band'=16,'z'=16,'core'=2] {'z'}, dimensions={0} | all-to-all | bytes 1212416 | tf_op jit(solution)/shard_map/all_to_all | solution.py:760
  69.9 2.0 %own_row.1 = f32[16,3,4,128]{3,2,1,0:T(4,128)} custom-call(s32[2]{0:T(128)S(1)} %pad_add_fusion.place_ref.refs_0_, f32[16,37,2,128]{3,2,1,0:T(2,128)S(1)} %all_to_all.10.in_ref, f32[8,64]{1,0:T(8,128)S(1)} %get-tuple-element.33.filter_ref.refs_6_.refs_3_, f32[16,256]{1,0:T(8,128)S(1)} %copy-done.9, f32[8,128]{1,0:T(8,128)S(1)} %copy-done.10, ...), custom_call_target="tpu_custom_call" | custom-call | flops 1000000000 | bytes 2000000 | tf_op jit(solution)/shard_map/own_row/pallas_call | solution.py:653
  71.8 3.7 %all-to-all-start.1 = ((f32[16,3,4,128]{3,2,1,0:T(4,128)}), f32[16,3,4,128]{3,2,1,0:T(4,128)S(1)}, u32[]{:S(2)}, u32[]{:S(2)}) async-start(f32[16,3,4,128]{3,2,1,0:T(4,128)} %own_row.1), calls=%async_computation.1 | async-start | bytes 196608 | tf_op jit(solution)/shard_map/all_to_all | solution.py:777
  75.5 0.9 unpack_observations.1
  76.5 3.0 %collective-permute-start.6 = (f32[96,128]{1,0:T(8,128)S(1)}, f32[96,128]{1,0:T(8,128)S(1)}, u32[]{:S(2)}, u32[]{:S(2)}) collective-permute-start(f32[96,128]{1,0:T(8,128)S(1)} %get-tuple-element.46), channel_id=1, source_target_pairs={{0,31},{1,0},{2,1},{3,2},{4,3},{5,4},{6,5},{7,6},{8,7},{9,8},{10,9... | collective-permute-start | bytes 147464 | tf_op jit(solution)/shard_map/ppermute | solution.py:697
  79.4 0.5 collective-permute-done.5.corner_left_ref
  79.9 9.8 %all-to-all-done.1 = f32[16,3,4,128]{3,2,1,0:T(4,128)S(1)} async-done(((f32[16,3,4,128]{3,2,1,0:T(4,128)}), f32[16,3,4,128]{3,2,1,0:T(4,128)S(1)}, u32[]{:S(2)}, u32[]{:S(2)}) %all-to-all-start.1) | async-done | bytes 98336 | tf_op jit(solution)/shard_map/all_to_all | solution.py:777
  89.7 1.9 %all-gather = f32[32,3,4,128]{3,2,1,0:T(4,128)S(1)} all-gather(f32[16,3,4,128]{3,2,1,0:T(4,128)S(1)} %all-to-all-done.1), channel_id=2, replica_groups=mesh['band'=16,'z'=16,'core'=2] {'core'}, dimensions={0}, use_global_device_ids=true | all-gather | bytes 294912 | tf_op jit(solution)/shard_map/all_gather | solution.py:778
  91.7 0.9 band_edges.1
  92.6 5.2 %collective-permute-start.7 = (f32[56,128]{1,0:T(8,128)S(1)}, f32[56,128]{1,0:T(8,128)S(1)}, u32[]{:S(2)}, u32[]{:S(2)}) collective-permute-start(f32[56,128]{1,0:T(8,128)S(1)} %get-tuple-element.51), channel_id=1, source_target_pairs={{0,32},{32,64},{64,96},{96,128},{128,160},{160,192},{192,224},{224... | collective-permute-start | bytes 86024 | tf_op jit(solution)/shard_map/ppermute | solution.py:697
  97.8 1.9 %collective-permute-start.8 = (f32[56,128]{1,0:T(8,128)S(1)}, f32[56,128]{1,0:T(8,128)S(1)}, u32[]{:S(2)}, u32[]{:S(2)}) collective-permute-start(f32[56,128]{1,0:T(8,128)S(1)} %get-tuple-element.52), channel_id=1, source_target_pairs={{32,0},{64,32},{96,64},{128,96},{160,128},{192,160},{224,192},{256... | collective-permute-start | bytes 86024 | tf_op jit(solution)/shard_map/ppermute | solution.py:697
  99.7 1.0 own_modes.1.own_ref
  100.8 4.9 %collective-permute-done.8.below_ref = f32[56,128]{1,0:T(8,128)S(1)} collective-permute-done((f32[56,128]{1,0:T(8,128)S(1)}, f32[56,128]{1,0:T(8,128)S(1)}, u32[]{:S(2)}, u32[]{:S(2)}) %collective-permute-start.8) | collective-permute-done | bytes 28704 | tf_op jit(solution)/shard_map/ppermute | solution.py:697
  105.6 2.0 %last_stage.1 = (f32[64,270]{1,0:T(8,128)}, f32[64,270]{1,0:T(8,128)}, f32[64,270]{1,0:T(8,128)}) custom-call(s32[2]{0:T(128)S(1)} %pad_add_fusion.place_ref.refs_0_, f32[4,72,384]{2,1,0:T(8,128)S(1)} %get-tuple-element.38.wide_ref, f32[64,128]{1,0:T(8,128)S(1)} %collective-permute-done.refs_2_.left_ref, ...), custom_call_target="tpu_custom_call" | custom-call | flops 1000000000 | bytes 2000000 | tf_op jit(solution)/shard_map/last_stage/pallas_call | solution.py:653
  (31 shorter events, 0.3 us)
Async XLA Ops:
  0.6 15.7 %copy-start = (f32[128,256]{1,0:T(8,128)S(1)}, f32[128,256]{1,0:T(8,128)}, u32[]{:S(2)}) copy-start(f32[128,256]{1,0:T(8,128)} %values_ref.1) | copy-start | bytes 393220
  2.0 16.8 %collective-permute-start.2 = (f32[16,384]{1,0:T(8,128)S(1)}, f32[16,384]{1,0:T(8,128)S(1)}, u32[]{:S(2)}, u32[]{:S(2)}) collective-permute-start(f32[16,384]{1,0:T(8,128)S(1)} %get-tuple-element.31), channel_id=1, source_target_pairs={{0,32},{32,64},{64,96},{96,128},{128,160},{160,192},{192,224},{224... | collective-permute-start | bytes 73736 | tf_op jit(solution)/shard_map/ppermute | solution.py:697
  5.0 13.8 %collective-permute-start.3 = (f32[16,384]{1,0:T(8,128)S(1)}, f32[16,384]{1,0:T(8,128)S(1)}, u32[]{:S(2)}, u32[]{:S(2)}) collective-permute-start(f32[16,384]{1,0:T(8,128)S(1)} %get-tuple-element.32), channel_id=1, source_target_pairs={{32,0},{64,32},{96,64},{128,96},{160,128},{192,160},{224,192},{256... | collective-permute-start | bytes 73736 | tf_op jit(solution)/shard_map/ppermute | solution.py:697
  7.8 11.0 %collective-permute-start = (f32[64,128]{1,0:T(8,128)S(1)}, f32[64,128]{1,0:T(8,128)S(1)}, u32[]{:S(2)}, u32[]{:S(2)}) collective-permute-start(f32[64,128]{1,0:T(8,128)S(1)} %get-tuple-element.29), channel_id=1, source_target_pairs={{0,1},{1,2},{2,3},{3,4},{4,5},{5,6},{6,7},{7,8},{8,9},{9,10},{10,1... | collective-permute-start | bytes 98312 | tf_op jit(solution)/shard_map/ppermute | solution.py:697
  7.9 11.0 %collective-permute-start.1 = (f32[64,128]{1,0:T(8,128)S(1)}, f32[64,128]{1,0:T(8,128)S(1)}, u32[]{:S(2)}, u32[]{:S(2)}) collective-permute-start(f32[64,128]{1,0:T(8,128)S(1)} %get-tuple-element.30), channel_id=1, source_target_pairs={{0,31},{1,0},{2,1},{3,2},{4,3},{5,4},{6,5},{7,6},{8,7},{9,8},{10,9... | collective-permute-start | bytes 98312 | tf_op jit(solution)/shard_map/ppermute | solution.py:697
  16.3 1.4 %copy-start.5 = (bf16[2,384,256]{2,1,0:T(8,128)(2,1)S(1)}, bf16[2,384,256]{2,1,0:T(8,128)(2,1)}, u32[]{:S(2)}) copy-start(bf16[2,384,256]{2,1,0:T(8,128)(2,1)} %constant.36.clone.table_ref.refs_10_) | copy-start | bytes 1179652
  16.3 1.4 %copy-start.7 = (f32[32,128]{1,0:T(8,128)S(1)}, f32[32,128]{1,0:T(8,128)}, u32[]{:S(2)}) copy-start(f32[32,128]{1,0:T(8,128)} %constant.35.clone.sin_ref.refs_9_) | copy-start | bytes 49156
  16.3 1.4 %copy-start.8 = (f32[32,128]{1,0:T(8,128)S(1)}, f32[32,128]{1,0:T(8,128)}, u32[]{:S(2)}) copy-start(f32[32,128]{1,0:T(8,128)} %constant.34.clone.cos_ref.refs_8_) | copy-start | bytes 49156
  17.8 1.1 %copy-start.1 = (bf16[2,384,512]{2,1,0:T(8,128)(2,1)S(1)}, bf16[2,384,512]{2,1,0:T(8,128)(2,1)}, u32[]{:S(2)}) copy-start(bf16[2,384,512]{2,1,0:T(8,128)(2,1)} %constant.38.clone.refs_11_) | copy-start | bytes 2359300
  17.8 1.1 %copy-start.6 = (f32[72,128]{1,0:T(8,128)S(1)}, f32[72,128]{1,0:T(8,128)}, u32[]{:S(2)}) copy-start(f32[72,128]{1,0:T(8,128)} %constant.37.clone.refs_7_.terms_ref) | copy-start | bytes 110596
  20.7 3.7 %collective-permute-start.4 = (f32[16,56,128]{2,1,0:T(8,128)S(1)}, f32[16,56,128]{2,1,0:T(8,128)S(1)}, u32[]{:S(2)}, u32[]{:S(2)}) collective-permute-start(f32[16,56,128]{2,1,0:T(8,128)S(1)} %get-tuple-element.40), channel_id=1, source_target_pairs={{0,1},{1,0},{2,3},{3,2},{4,5},{5,4},{6,7},{7,6},{8,9},{9,8},{10,11... | collective-permute-start | bytes 1376264 | tf_op jit(solution)/shard_map/ppermute | solution.py:758
  24.6 45.3 %copy-start.2 = (bf16[2,512,256]{2,1,0:T(8,128)(2,1)S(1)}, bf16[2,512,256]{2,1,0:T(8,128)(2,1)}, u32[]{:S(2)}) copy-start(bf16[2,512,256]{2,1,0:T(8,128)(2,1)} %constant.42.clone.from_grid_ref) | copy-start | bytes 1572868
  24.6 45.3 %copy-start.3 = (bf16[2,256,512]{2,1,0:T(8,128)(2,1)S(1)}, bf16[2,256,512]{2,1,0:T(8,128)(2,1)}, u32[]{:S(2)}) copy-start(bf16[2,256,512]{2,1,0:T(8,128)(2,1)} %constant.41.clone.to_grid_ref) | copy-start | bytes 1572868
  24.6 45.3 %copy-start.9 = (f32[16,256]{1,0:T(8,128)S(1)}, f32[16,256]{1,0:T(8,128)}, u32[]{:S(2)}) copy-start(f32[16,256]{1,0:T(8,128)} %constant.39.clone.lines_ref) | copy-start | bytes 49156
  24.6 45.2 %copy-start.10 = (f32[8,128]{1,0:T(8,128)S(1)}, f32[8,128]{1,0:T(8,128)}, u32[]{:S(2)}) copy-start(f32[8,128]{1,0:T(8,128)} %constant.40.clone.slope_ref) | copy-start | bytes 12292
  71.8 17.9 %all-to-all-start.1 = ((f32[16,3,4,128]{3,2,1,0:T(4,128)}), f32[16,3,4,128]{3,2,1,0:T(4,128)S(1)}, u32[]{:S(2)}, u32[]{:S(2)}) async-start(f32[16,3,4,128]{3,2,1,0:T(4,128)} %own_row.1), calls=%async_computation.1 | async-start | bytes 196608 | tf_op jit(solution)/shard_map/all_to_all | solution.py:777
  75.5 4.4 %collective-permute-start.5 = (f32[32,128]{1,0:T(8,128)S(1)}, f32[32,128]{1,0:T(8,128)S(1)}, u32[]{:S(2)}, u32[]{:S(2)}) collective-permute-start(f32[32,128]{1,0:T(8,128)S(1)} %get-tuple-element.44), channel_id=1, source_target_pairs={{0,1},{1,2},{2,3},{3,4},{4,5},{5,6},{6,7},{7,8},{8,9},{9,10},{10,1... | collective-permute-start | bytes 49160 | tf_op jit(solution)/shard_map/ppermute | solution.py:697
  76.5 15.2 %collective-permute-start.6 = (f32[96,128]{1,0:T(8,128)S(1)}, f32[96,128]{1,0:T(8,128)S(1)}, u32[]{:S(2)}, u32[]{:S(2)}) collective-permute-start(f32[96,128]{1,0:T(8,128)S(1)} %get-tuple-element.46), channel_id=1, source_target_pairs={{0,31},{1,0},{2,1},{3,2},{4,3},{5,4},{6,5},{7,6},{8,7},{9,8},{10,9... | collective-permute-start | bytes 147464 | tf_op jit(solution)/shard_map/ppermute | solution.py:697
  91.7 8.0 %copy-start.4 = (bf16[2,256,384]{2,1,0:T(8,128)(2,1)S(1)}, bf16[2,256,384]{2,1,0:T(8,128)(2,1)}, u32[]{:S(2)}) copy-start(bf16[2,256,384]{2,1,0:T(8,128)(2,1)} %constant.43.clone.table_ref) | copy-start | bytes 1179652
  92.6 8.1 %collective-permute-start.7 = (f32[56,128]{1,0:T(8,128)S(1)}, f32[56,128]{1,0:T(8,128)S(1)}, u32[]{:S(2)}, u32[]{:S(2)}) collective-permute-start(f32[56,128]{1,0:T(8,128)S(1)} %get-tuple-element.51), channel_id=1, source_target_pairs={{0,32},{32,64},{64,96},{96,128},{128,160},{160,192},{192,224},{224... | collective-permute-start | bytes 86024 | tf_op jit(solution)/shard_map/ppermute | solution.py:697
  97.8 7.9 %collective-permute-start.8 = (f32[56,128]{1,0:T(8,128)S(1)}, f32[56,128]{1,0:T(8,128)S(1)}, u32[]{:S(2)}, u32[]{:S(2)}) collective-permute-start(f32[56,128]{1,0:T(8,128)S(1)} %get-tuple-element.52), channel_id=1, source_target_pairs={{32,0},{64,32},{96,64},{128,96},{160,128},{192,160},{224,192},{256... | collective-permute-start | bytes 86024 | tf_op jit(solution)/shard_map/ppermute | solution.py:697

commit v4 on v3

--- a/solution.py
+++ b/solution.py
@@ -34,9 +34,24 @@
     return jnp.dot(left, right, preferred_element_type=F32)
 
 
+def pick_dot(chosen, value):
+    high, low = halves_of(value)
+    rest = (value - high.astype(F32) - low.astype(F32)).astype(jnp.bfloat16)
+    chosen = chosen.astype(jnp.bfloat16)
+    return bdot(chosen, high) + bdot(chosen, low) + bdot(chosen, rest)
+
+
 def tdot(left, table_ref):
     high, low = halves_of(left)
     return bdot(high, table_ref[0]) + bdot(low, table_ref[0]) + bdot(high, table_ref[1])
+
+
+def tdot_few(left, table_ref):
+    lines = left.shape[0]
+    high = left.astype(jnp.bfloat16).astype(F32)
+    both = jnp.concatenate([high, left - high], axis=0).astype(jnp.bfloat16)
+    first = bdot(both, table_ref[0])
+    return first[0:lines] + first[lines:] + bdot(left.astype(jnp.bfloat16), table_ref[1])
 
 
 def mdot(left, right):
@@ -297,13 +312,26 @@
             other_ref[:, at, :] = part[half:devices]
 
 
-def pack_observations(place_ref, values_ref, marks_ref, near_ref, far_ref, kept_ref):
+def pack_observations(
+    place_ref,
+    values_ref,
+    marks_ref,
+    filter_ref,
+    cos_ref,
+    sin_ref,
+    table_ref,
+    near_ref,
+    far_ref,
+    placed_ref,
+):
     number, width = values_ref.shape
     half = near_ref.shape[0]
+    devices = 2 * half
     core = place_ref[1] % 2
     lengths = to_col(marks_ref[2:3, :])
     values = jnp.where(iota((number, width), 1).astype(F32) < lengths, values_ref[...], 0.0)
-    kept_ref[...] = values
+    high, low = halves_of(values)
+    rest = (values - high.astype(F32) - low.astype(F32)).astype(jnp.bfloat16)
     owner_row = marks_ref[0:1, :].astype(jnp.int32)
     owner_col = to_col(owner_row)
     same = owner_col == owner_row
@@ -314,36 +342,32 @@
     chip_row, core_row = owner_row // 2, owner_row % 2
     target = chip_row * 16 + arrival_row
     label = marks_ref[1:2, :]
-    arrived = (iota((number, 128), 1) == arrival_col).astype(F32)
+    arrived = (iota((number, 128), 1) == arrival_col).astype(F32).astype(jnp.bfloat16)
     for out_ref, side in ((near_ref, core), (far_ref, 1 - core)):
         goes = core_row == side
         sent = ((iota((16 * half, number), 0) == target) & goes).astype(F32)
-        block = hdot(sent, values).reshape(half, 16, width)
+        sent = sent.astype(jnp.bfloat16)
+        block = bdot(sent, high) + bdot(sent, low) + bdot(sent, rest)
+        block = block.reshape(half, 16, width)
         out_ref[:, 0:CAP, :] = block[:, 0:CAP, 0:128]
         out_ref[:, CAP : 2 * CAP, :] = block[:, 0:CAP, 128:256]
         named = ((iota((half, number), 0) == chip_row) & goes).astype(F32) * label
         out_ref[:, 2 * CAP : 32, :] = jnp.zeros((half, 32 - 2 * CAP, 128), F32)
-        out_ref[:, 2 * CAP, :] = hdot(named, arrived)
-
-
-def sum_observations(
-    place_ref, values_ref, marks_ref, filter_ref, cos_ref, sin_ref, table_ref, placed_ref
-):
-    number, width = values_ref.shape
-    devices = cos_ref.shape[0]
-    owner_col = to_col(marks_ref[0:1, :])
-    sums = tdot(values_ref[...], table_ref.at[:, 0:width, :])
-    whose = (iota((number, devices), 1).astype(F32) == owner_col).astype(F32)
-    turn_cos, turn_sin = mdot(whose, cos_ref[...]), mdot(whose, sin_ref[...])
+        out_ref[:, 2 * CAP, :] = bdot(named.astype(jnp.bfloat16), arrived)
+    head = table_ref[0, 0:width, :]
+    sums = bdot(high, head) + bdot(low, head) + bdot(high, table_ref[1, 0:width, :])
+    whose = (iota((number, devices), 1) == owner_col).astype(F32)
+    turn_cos, turn_sin = pick_dot(whose, cos_ref[...]), pick_dot(whose, sin_ref[...])
     on_cos, on_sin = sums[:, 0:128], sums[:, 128:256]
     all_cos = on_cos * turn_cos - on_sin * turn_sin
     all_sin = on_sin * turn_cos + on_cos * turn_sin
     mask = filter_ref[0:1, :]
     rows = mask.shape[1]
-    in_row = (iota((rows, number), 0).astype(F32) == marks_ref[1:2, :]).astype(F32)
-    chosen = mdot(slot_rows(mask, place_ref[1] % 2, devices), in_row)
-    placed_ref[:, 0:128] = mdot(chosen, all_cos)
-    placed_ref[:, 128:256] = mdot(chosen, all_sin)
+    in_row = (iota((rows, number), 0).astype(F32) == label).astype(F32)
+    slots = slot_rows(mask, core, devices).astype(jnp.bfloat16)
+    chosen = bdot(slots, in_row.astype(jnp.bfloat16))
+    placed_ref[:, 0:128] = pick_dot(chosen, all_cos)
+    placed_ref[:, 128:256] = pick_dot(chosen, all_sin)
 
 
 def join(mine_ref, swapped_ref, out_ref):
@@ -367,7 +391,9 @@
     own = iota((half, total), 1) // lines == iota((half, total), 0)
     for s in range(2):
         here = (spot // (2 * CAP) == s) & (spot % CAP == iota((128, total), 0))
-        across = hdot(in_ref[:, 36, s, :], here.astype(F32))
+        across = bdot(
+            in_ref[:, 36, s, :].astype(jnp.bfloat16), here.astype(F32).astype(jnp.bfloat16)
+        )
         label_row = label_row + jnp.sum(jnp.where(own, across, 0.0), axis=0, keepdims=True)
     line = iota((rows, total), 1) % lines
     hit = iota((rows, total), 0).astype(F32) == label_row
@@ -376,7 +402,7 @@
     data = data_ref[...].reshape(total, 128)
     for i in range(2):
         side = (hit & ((line // CAP) % 2 == i)).astype(F32)
-        dep_ref[:, 128 * i : 128 * i + 128] = hdot(side, data)
+        dep_ref[:, 128 * i : 128 * i + 128] = pick_dot(side, data)
     dep_ref[:, 256:384] = jnp.zeros((rows, 128), F32)
     west_ref[0:rows, :] = pltpu.roll(dep_ref[:, 0:128], 14, 1)
     west_ref[rows : rows + corner_ref.shape[0], :] = corner_ref[...]
@@ -429,13 +455,13 @@
     for i, (on_cos, on_sin) in enumerate(pairs):
         left_ref[i : i + 1, 0:128] = on_cos
         left_ref[i : i + 1, 128:256] = on_sin
-    at = tdot(left_ref[...], to_grid_ref)
+    at = tdot_few(left_ref[...], to_grid_ref)
     wet = jnp.concatenate([line(16), line(17), line(18), line(19)], axis=1)
     share = (COURANT / LEVELS) * jnp.concatenate([line(20), line(21), line(22), line(23)], axis=1)
     grid_ref[...] = jnp.zeros(grid_ref.shape, F32)
     grid_ref[0:1, :] = wet * at[0:1] + share * at[1:2]
     grid_ref[1:2, :] = wet * at[2:3] + share * at[3:4]
-    back = tdot(grid_ref[...], from_grid_ref)
+    back = tdot_few(grid_ref[...], from_grid_ref)
     res_ref[0:6, :] = sums[0:6]
     res_ref[6:8, :] = sums[10:12] + sums[6:8]
     for i in range(2):
@@ -447,28 +473,36 @@
         )
 
 
-def band_edges(cols, all_ref, dep_ref, edge_ref, filter_ref, coef_ref, depx_ref, north_ref, south_ref):
+def slots_to_rows(all_ref, mask, at):
     half = all_ref.shape[1]
+    lines = at.shape[0]
+    here = iota((lines, mask.shape[1]), 1) == at
+    rank = jnp.sum(
+        jnp.where(here & (mask == 1), rank_in_row(mask) + 1.0, 0.0), axis=1, keepdims=True
+    )
+    total = jnp.zeros((lines, 12 * 128), F32)
+    for c in range(2):
+        chosen = (2 * iota((lines, half), 1) + c + 1).astype(F32) == rank
+        every = [all_ref[c, :, v // 4, v % 4, :] for v in range(12)]
+        total = total + pick_dot(chosen.astype(F32), jnp.concatenate(every, axis=1))
+    return total
+
+
+def band_edges(cols, all_ref, dep_ref, edge_ref, filter_ref, depx_ref, north_ref, south_ref):
     rows = dep_ref.shape[0]
     mask = filter_ref[0:1, :]
-    rank = to_col(rank_in_row(mask))
-    kept = to_col(mask) == 1
     first = cols - 256
     lane = iota((rows, 128), 1)
     depx_ref[:, 0:256] = dep_ref[:, 0:256]
     depx_ref[:, 256:384] = jnp.where(
         (lane == first) | (lane == first + 1), edge_ref[0:rows, :], 0.0
     )
-    chosen = [
-        ((2 * iota((rows, half), 1) + c == rank) & kept).astype(F32) for c in range(2)
-    ]
+    line = iota((8, 1), 0)
+    ends = slots_to_rows(all_ref, mask, jnp.where(line < 4, line, line + (rows - 8)))
     for v in range(12):
-        own = hdot(chosen[0], all_ref[0, :, v // 4, v % 4, :]) + hdot(
-            chosen[1], all_ref[1, :, v // 4, v % 4, :]
-        )
-        coef_ref[v] = own
+        own = ends[:, 128 * v : 128 * v + 128]
         north_ref[4 * v : 4 * v + 4, :] = own[0:4]
-        south_ref[4 * v : 4 * v + 4, :] = own[rows - 4 : rows]
+        south_ref[4 * v : 4 * v + 4, :] = own[4:8]
     for out_ref, at in ((north_ref, 0), (south_ref, rows - 2)):
         for r in range(2):
             for t in range(3):
@@ -478,16 +512,74 @@
         out_ref[54:56, :] = jnp.zeros((2, 128), F32)
 
 
-def own_modes(place_ref, coef_ref, cos_ref, sin_ref, table_ref, low_ref, stack_ref):
-    rows = coef_ref.shape[1]
-    lon = place_ref[1]
+EDGE = 16
+SURE = 8
+
+
+def two_steps(fields, low, weight, terms, dep):
+    metric, rotation, valid = terms
+    level = fields[3]
+    wet = (level > 0).astype(F32)
+    share = COURANT * (level / LEVELS)
+
+    def half_step(height, east, north, f):
+        height = height + weight * (low[f] - height)
+        east = east + weight * (low[f + 1] - east)
+        north = north + weight * (low[f + 2] - north)
+        middle = valid * (height + COURANT * (metric * lon_diff(east) + lat_diff(north)))
+        new_east = east - rotation * north + share * (metric * lon_diff(middle))
+        new_north = north + rotation * east + share * lat_diff(middle)
+        return middle, new_east, new_north
+
+    middle, east, north = half_step(fields[0], fields[1], fields[2], 0)
+    return half_step(middle + dep, wet * east, wet * north, 3)
+
+
+def own_rows(
+    cols,
+    place_ref,
+    all_ref,
+    filter_ref,
+    cos_ref,
+    sin_ref,
+    table_ref,
+    wide_ref,
+    left_ref,
+    right_ref,
+    weight_ref,
+    depx_ref,
+    terms_ref,
+    low_ref,
+    inner_ref,
+    stack_ref,
+    ext_ref,
+):
+    mask = filter_ref[0:1, :]
+    rows = mask.shape[1]
+    band, lon = place_ref[0], place_ref[1]
     turn_cos, turn_sin = cos_ref[pl.ds(lon, 1), :], sin_ref[pl.ds(lon, 1), :]
+    coef = slots_to_rows(all_ref, mask, iota((rows, 1), 0))
     for f in range(6):
         lines = slice(rows * f, rows * f + rows)
-        on_cos, on_sin = coef_ref[2 * f], coef_ref[2 * f + 1]
+        on_cos = coef[:, 256 * f : 256 * f + 128]
+        on_sin = coef[:, 256 * f + 128 : 256 * f + 256]
         stack_ref[lines, 0:128] = on_cos * turn_cos + on_sin * turn_sin
         stack_ref[lines, 128:256] = on_sin * turn_cos - on_cos * turn_sin
     low_ref[...] = tdot(stack_ref[...], table_ref)
+    for f in range(4):
+        ext_ref[f, :, 0:256] = wide_ref[f, 0:rows, 0:256]
+        ext_ref[f, :, 256:384] = third_tile(
+            wide_ref[f, 0:rows, 256:384], left_ref[...], right_ref[...], f, cols
+        )
+    state = two_steps(
+        [ext_ref[f] for f in range(4)],
+        [low_ref[rows * f : rows * f + rows, :] for f in range(6)],
+        weight_ref[0:rows, 0:1],
+        row_terms(terms_ref[0:rows, :], band),
+        depx_ref[...],
+    )
+    for i in range(3):
+        inner_ref[i] = state[i][SURE : rows - SURE]
 
 
 def last_stage(
@@ -499,6 +591,7 @@
     corner_right_ref,
     weight_ref,
     own_ref,
+    inner_ref,
     depx_ref,
     above_ref,
     below_ref,
@@ -506,30 +599,52 @@
     cos_ref,
     sin_ref,
     table_ref,
+    h_hbm,
+    e_hbm,
+    n_hbm,
+    stack_ref,
+    dep_ref,
+    ext_ref,
     h_ref,
     e_ref,
     n_ref,
-    stack_ref,
-    dep_ref,
-    ext_ref,
-    low_ref,
+    sems,
 ):
-    ext = ext_ref.shape[1]
     rows, cols = h_ref.shape
+    ext = rows + 2 * HALO
+    band, lon = place_ref[0], place_ref[1]
+    pairs = ((h_ref, h_hbm), (e_ref, e_hbm), (n_ref, n_hbm))
+    spans = (pl.ds(SURE, rows - 2 * SURE), pl.ds(0, SURE), pl.ds(rows - SURE, SURE))
+    copies = [
+        [
+            pltpu.make_async_copy(a.at[span, :], b.at[span, :], sems.at[i, j])
+            for j, span in enumerate(spans)
+        ]
+        for i, (a, b) in enumerate(pairs)
+    ]
+    for i, (out_ref, _) in enumerate(pairs):
+        out_ref[SURE : rows - SURE, :] = inner_ref[i, :, 0:cols]
+        copies[i][0].start()
     for f in range(4):
-        ext_ref[f, :, 0:256] = wide_ref[f, :, 0:256]
-        ext_ref[f, 0:rows, 256:384] = third_tile(
-            wide_ref[f, 0:rows, 256:384], left_ref[...], right_ref[...], f, cols
+        parts = (
+            (slice(0, EDGE), slice(rows - EDGE, rows)),
+            (slice(EDGE + 2 * HALO, 2 * EDGE + 2 * HALO), slice(0, EDGE)),
         )
+        for to, at in parts:
+            ext_ref[f, to, 0:256] = wide_ref[f, at, 0:256]
+            ext_ref[f, to, 256:384] = third_tile(
+                wide_ref[f, at, 256:384], left_ref[at, :], right_ref[at, :], f, cols
+            )
+        to = slice(EDGE, EDGE + 2 * HALO)
         lines = slice(2 * HALO * f, 2 * HALO * f + 2 * HALO)
-        ext_ref[f, rows:ext, 256:384] = third_tile(
+        ext_ref[f, to, 0:256] = wide_ref[f, rows:ext, 0:256]
+        ext_ref[f, to, 256:384] = third_tile(
             wide_ref[f, rows:ext, 256:384],
             corner_left_ref[lines, :],
             corner_right_ref[rows + 2 * HALO * f : rows + 2 * HALO * f + 2 * HALO, :],
             f,
             cols,
         )
-    band, lon = place_ref[0], place_ref[1]
     turn_cos, turn_sin = cos_ref[pl.ds(lon, 1), :], sin_ref[pl.ds(lon, 1), :]
     for f in range(6):
         for at, in_ref in ((8 * f, below_ref), (8 * f + 4, above_ref)):
@@ -538,38 +653,46 @@
             stack_ref[at : at + 4, 0:128] = on_cos * turn_cos + on_sin * turn_sin
             stack_ref[at : at + 4, 128:256] = on_sin * turn_cos - on_cos * turn_sin
     edges = tdot(stack_ref[...], table_ref)
-    for f in range(6):
-        low_ref[ext * f : ext * f + rows, :] = own_ref[rows * f : rows * f + rows, :]
-        low_ref[ext * f + rows : ext * f + ext, :] = edges[8 * f : 8 * f + 8, :]
-    low = low_ref
-    dep_ref[0:rows, :] = depx_ref[...]
-    dep_ref[rows:ext, :] = jnp.zeros((ext - rows, LANES), F32)
-    for in_ref, at in ((below_ref, rows), (above_ref, ext - 2)):
+    low = [
+        jnp.concatenate(
+            [
+                own_ref[rows * f + rows - EDGE : rows * f + rows, :],
+                edges[8 * f : 8 * f + 8, :],
+                own_ref[rows * f : rows * f + EDGE, :],
+            ],
+            axis=0,
+        )
+        for f in range(6)
+    ]
+    dep_ref[0:EDGE, :] = depx_ref[rows - EDGE : rows, :]
+    dep_ref[EDGE : EDGE + 2 * HALO, :] = jnp.zeros((2 * HALO, LANES), F32)
+    dep_ref[EDGE + 2 * HALO : 2 * EDGE + 2 * HALO, :] = depx_ref[0:EDGE, :]
+    for in_ref, at in ((below_ref, EDGE), (above_ref, EDGE + 2 * HALO - 2)):
         for r in range(2):
             for t in range(3):
                 dep_ref[at + r : at + r + 1, 128 * t : 128 * t + 128] = in_ref[
                     48 + 3 * r + t : 49 + 3 * r + t, :
                 ]
-    weight = weight_ref[:, 0:1]
-    metric, rotation, valid = row_terms(terms_ref[...], band)
-    level = ext_ref[3]
-    wet = (level > 0).astype(F32)
-    share = COURANT * (level / LEVELS)
-
-    def step(height, east, north, f):
-        height = height + weight * (low[ext * f : ext * f + ext] - height)
-        east = east + weight * (low[ext * f + ext : ext * f + 2 * ext] - east)
-        north = north + weight * (low[ext * f + 2 * ext : ext * f + 3 * ext] - north)
-        middle = valid * (height + COURANT * (metric * lon_diff(east) + lat_diff(north)))
-        new_east = east - rotation * north + share * (metric * lon_diff(middle))
-        new_north = north + rotation * east + share * lat_diff(middle)
-        return middle, new_east, new_north
-
-    middle, east, north = step(ext_ref[0], ext_ref[1], ext_ref[2], 0)
-    middle, east, north = step(middle + dep_ref[...], wet * east, wet * north, 3)
-    h_ref[...] = middle[0:rows, 0:cols]
-    e_ref[...] = east[0:rows, 0:cols]
-    n_ref[...] = north[0:rows, 0:cols]
+
+    def around(ref):
+        return jnp.concatenate([ref[rows - EDGE : ext, :], ref[0:EDGE, :]], axis=0)
+
+    state = two_steps(
+        [ext_ref[f] for f in range(4)],
+        low,
+        around(weight_ref)[:, 0:1],
+        row_terms(around(terms_ref), band),
+        dep_ref[...],
+    )
+    south, north = slice(EDGE - SURE, EDGE), slice(EDGE + 2 * HALO, EDGE + 2 * HALO + SURE)
+    for i, (out_ref, _) in enumerate(pairs):
+        out_ref[0:SURE, :] = state[i][north, 0:cols]
+        out_ref[rows - SURE : rows, :] = state[i][south, 0:cols]
+        copies[i][1].start()
+        copies[i][2].start()
+    for group in copies:
+        for copy in group:
+            copy.wait()
 
 
 def tables(length, cols, devices, rows, bands):
@@ -639,7 +762,7 @@
 HBM = pl.BlockSpec(memory_space=pltpu.HBM)
 
 
-def call(kernel, name, outs, args, scratch=(), scalars=False, direct=(), cost=1.0):
+def call(kernel, name, outs, args, scratch=(), scalars=False, direct=(), cost=1.0, outside=False):
     shapes = [jax.ShapeDtypeStruct(shape, F32) for shape in outs]
     specs = [
         SMEM if scalars and i == 0 else HBM if i in direct else VMEM for i in range(len(args))
@@ -655,7 +778,7 @@
         name=name,
         out_shape=shapes,
         in_specs=specs,
-        out_specs=[VMEM] * len(shapes),
+        out_specs=[HBM if outside else VMEM] * len(shapes),
         scratch_shapes=held + [
             pltpu.VMEM(shape, F32) if isinstance(shape, tuple) else shape for shape in scratch
         ],
@@ -716,19 +839,12 @@
     below, above = send(north, "band", -1, False), send(south, "band", 1, False)
     right, left = send(west, LON, -1, True), send(east, LON, 1, True)
     other_core = [(i, i ^ 1) for i in range(devices)]
-    near, far, values = call(
+    near, far, placed = call(
         pack_observations,
         "pack_observations",
-        [(half, 32, 128), (half, 32, 128), (number, width)],
-        (place, obs_values, marks),
+        [(half, 32, 128), (half, 32, 128), (devices, 256)],
+        (place, obs_values, marks, kept, made["cos"], made["sin"], made["analyse"]),
         cost=3.0,
-        scalars=True,
-    )
-    (placed,) = call(
-        sum_observations,
-        "sum_observations",
-        [(devices, 256)],
-        (place, values, marks, kept, made["cos"], made["sin"], made["analyse"]),
         scalars=True,
     )
     wide, weight, corner_west, corner_east, mine, other = call(
@@ -786,21 +902,35 @@
     corner_east = lax.optimization_barrier((corner_east, spread))[0]
     corner_right, corner_left = send(west, LON, -1, True), send(corner_east, LON, 1, True)
     dep, corner_left = lax.optimization_barrier((dep, corner_left))
-    coef, depx, north, south = call(
+    depx, north, south = call(
         lambda *refs: band_edges(cols, *refs),
         "band_edges",
-        [(12, rows, 128), (rows, LANES), (56, 128), (56, 128)],
+        [(rows, LANES), (56, 128), (56, 128)],
         (everyone, dep, corner_right, kept),
     )
     below, above = send(north, "band", -1, False), send(south, "band", 1, False)
-    (own,) = call(
-        own_modes,
-        "own_modes",
-        [(6 * rows, LANES)],
-        (place, coef, made["cos"], made["sin"], made["evaluate"]),
-        scratch=[(6 * rows, 256)],
+    own, inner = call(
+        lambda *refs: own_rows(cols, *refs),
+        "own_rows",
+        [(6 * rows, LANES), (3, rows - 2 * SURE, LANES)],
+        (
+            place,
+            everyone,
+            kept,
+            made["cos"],
+            made["sin"],
+            made["evaluate"],
+            wide,
+            left,
+            right,
+            weight,
+            depx,
+            made["terms"],
+        ),
+        scratch=[(6 * rows, 256), (4, rows, LANES)],
         scalars=True,
     )
+    edge = 2 * EDGE + 2 * HALO
     return tuple(
         call(
             last_stage,
@@ -815,6 +945,7 @@
                 corner_right,
                 weight,
                 own,
+                inner,
                 depx,
                 above,
                 below,
@@ -823,7 +954,10 @@
                 made["sin"],
                 made["evaluate"],
             ),
-            scratch=[(48, 256), (ext, LANES), (4, ext, LANES), (6 * ext, LANES)],
+            scratch=[(48, 256), (edge, LANES), (4, edge, LANES)]
+            + [(rows, cols)] * 3
+            + [pltpu.SemaphoreType.DMA((3, 3))],
+            outside=True,
             scalars=True,
         )
     )

time: 108 us -> 107 us (level)
  Pallas kernels: 12.6 us -> 10.9 us
    pallas_call x10 -> x9, Pallas kernels: 12.6 us -> 10.9 us  [call(): pl.pallas_call(kernel, name=name, out_shape=shapes, in_specs=specs, out_s...]
  transfers between devices with their start and end apart: 10 -> 10, of which waited for: 4 -> 5; matrix products, arithmetic and copies ran while one was open for 0% -> 0% of each run, Pallas kernels for 4% -> 4%
where the time goes in v4:
time: 107 us; the launch traced here: 106 us
  blocking collectives  47.7 us (45%)
  starting transfers between devices  29.9 us (28%)
  waiting for transfers between devices  16.6 us (16%)
  Pallas kernels  10.9 us (10%)
    all_to_all x1, blocking collectives, on_device(): owned = lax.all_to_all(joined, 'z', split_axis=0, concat_axis=0, tiled=True)  45.8 us
    ppermute x8, starting transfers between devices, send(): return lax.ppermute(value, axis, pairs)  24.3 us
    pallas_call x9, Pallas kernels, call(): pl.pallas_call(kernel, name=name, out_shape=shapes, in_specs=specs, out_s...  10.9 us
    all_to_all x1, waiting for transfers between devices, on_device(): lax.all_to_all(spread, 'z', split_axis=0, concat_axis=0, tiled=True)  9.81 us
    ppermute x8, waiting for transfers between devices, send(): return lax.ppermute(value, axis, pairs)  4.99 us
    all_to_all x1, starting transfers between devices, on_device(): lax.all_to_all(spread, 'z', split_axis=0, concat_axis=0, tiled=True)  3.63 us
  transfers between devices with their start and end apart: 10, of which 5 were waited for; matrix products, arithmetic and copies ran while one was open for 0% of the time, Pallas kernels for 4%

profile of v4, /device:TPU:24, one launch (start us, length us, event | category | flops | bytes accessed | tf_op | source)
XLA Modules:
  0.0 106.2 jit_solution(15024910188047763886)
XLA Ops:
  0.7 1.3 %pack_tile.1 = (f32[4,64,384]{2,1,0:T(8,128)S(1)}, f32[64,128]{1,0:T(8,128)S(1)}, f32[64,128]{1,0:T(8,128)S(1)}, f32[16,384]{1,0:T(8,128)S(1)}, f32[16,384]{1,0:...) custom-call(f32[64,270]{1,0:T(8,128)} %h_hbm.1, f32[64,270]{1,0:T(8,128)} %e_hbm.1, f32[64,270]{1,0:T(8,128)} %n_hbm.1, ...), custom_call_target="tpu_custom_call" | custom-call | flops 1000000000 | bytes 2000000 | tf_op jit(solution)/shard_map/pack_tile/pallas_call | solution.py:776
  2.0 3.1 %collective-permute-start.2 = (f32[16,384]{1,0:T(8,128)S(1)}, f32[16,384]{1,0:T(8,128)S(1)}, u32[]{:S(2)}, u32[]{:S(2)}) collective-permute-start(f32[16,384]{1,0:T(8,128)S(1)} %get-tuple-element.32), channel_id=1, source_target_pairs={{0,32},{32,64},{64,96},{96,128},{128,160},{160,192},{192,224},{224... | collective-permute-start | bytes 73736 | tf_op jit(solution)/shard_map/ppermute | solution.py:820
  5.1 2.8 %collective-permute-start.3 = (f32[16,384]{1,0:T(8,128)S(1)}, f32[16,384]{1,0:T(8,128)S(1)}, u32[]{:S(2)}, u32[]{:S(2)}) collective-permute-start(f32[16,384]{1,0:T(8,128)S(1)} %get-tuple-element.33), channel_id=1, source_target_pairs={{32,0},{64,32},{96,64},{128,96},{160,128},{192,160},{224,192},{256... | collective-permute-start | bytes 73736 | tf_op jit(solution)/shard_map/ppermute | solution.py:820
  7.9 8.4 %collective-permute-start.1 = (f32[64,128]{1,0:T(8,128)S(1)}, f32[64,128]{1,0:T(8,128)S(1)}, u32[]{:S(2)}, u32[]{:S(2)}) collective-permute-start(f32[64,128]{1,0:T(8,128)S(1)} %get-tuple-element.31), channel_id=1, source_target_pairs={{0,31},{1,0},{2,1},{3,2},{4,3},{5,4},{6,5},{7,6},{8,7},{9,8},{10,9... | collective-permute-start | bytes 98312 | tf_op jit(solution)/shard_map/ppermute | solution.py:820
  16.4 1.4 %pack_observations.1 = (f32[16,32,128]{2,1,0:T(8,128)S(1)}, f32[16,32,128]{2,1,0:T(8,128)S(1)}, f32[32,256]{1,0:T(8,128)S(1)}) custom-call(s32[2]{0:T(128)S(1)} %pad_add_fusion.place_ref.refs_0_, f32[128,256]{1,0:T(8,128)S(1)} %copy-done, f32[8,128]{1,0:T(8,128)S(1)} %get-tuple-element.35.marks_ref, ...), custom_call_target="tpu_custom_call" | custom-call | flops 3000000000 | bytes 6000000 | tf_op jit(solution)/shard_map/pack_observations/pallas_call | solution.py:776
  17.8 0.1 collective-permute-done.refs_2_.refs_7_.left_ref
  17.9 1.8 %partial_sums.1 = (f32[4,72,384]{2,1,0:T(8,128)S(1)}, f32[72,128]{1,0:T(8,128)S(1)}, f32[32,128]{1,0:T(8,128)S(1)}, f32[32,128]{1,0:T(8,128)S(1)}, f32[16,56,128...) custom-call(s32[2]{0:T(128)S(1)} %pad_add_fusion.place_ref.refs_0_, f32[4,64,384]{2,1,0:T(8,128)S(1)} %get-tuple-element.29.refs_1_, ...), custom_call_target="tpu_custom_call" | custom-call | flops 1000000000 | bytes 2000000 | tf_op jit(solution)/shard_map/partial_sums/pallas_call | solution.py:776
  19.8 1.9 %collective-permute-start.4 = (f32[16,56,128]{2,1,0:T(8,128)S(1)}, f32[16,56,128]{2,1,0:T(8,128)S(1)}, u32[]{:S(2)}, u32[]{:S(2)}) collective-permute-start(f32[16,56,128]{2,1,0:T(8,128)S(1)} %get-tuple-element.41), channel_id=1, source_target_pairs={{0,1},{1,0},{2,3},{3,2},{4,5},{5,4},{6,7},{7,6},{8,9},{9,8},{10,11... | collective-permute-start | bytes 1376264 | tf_op jit(solution)/shard_map/ppermute | solution.py:874
  21.7 1.8 %collective-permute-done.4.swapped_ref = f32[16,56,128]{2,1,0:T(8,128)S(1)} collective-permute-done((f32[16,56,128]{2,1,0:T(8,128)S(1)}, f32[16,56,128]{2,1,0:T(8,128)S(1)}, u32[]{:S(2)}, u32[]{:S(2)}) %collective-permute-start.4) | collective-permute-done | bytes 458784 | tf_op jit(solution)/shard_map/ppermute | solution.py:874
  23.5 0.1 join.1
  23.7 45.8 %all_to_all.10.in_ref = f32[16,37,2,128]{3,2,1,0:T(2,128)S(1)} all-to-all(f32[16,37,2,128]{3,2,1,0:T(2,128)S(1)} %join.1), channel_id=1, replica_groups=mesh['band'=16,'z'=16,'core'=2] {'z'}, dimensions={0} | all-to-all | bytes 1212416 | tf_op jit(solution)/shard_map/all_to_all | solution.py:876
  69.5 1.7 %own_row.1 = f32[16,3,4,128]{3,2,1,0:T(4,128)} custom-call(s32[2]{0:T(128)S(1)} %pad_add_fusion.place_ref.refs_0_, f32[16,37,2,128]{3,2,1,0:T(2,128)S(1)} %all_to_all.10.in_ref, f32[8,64]{1,0:T(8,128)S(1)} %get-tuple-element.34.filter_ref.refs_6_.refs_3_.refs_2_, f32[16,256]{1,0:T(8,128)S(1)} %copy-done.9, f32[8,128]{1,0:T(8,128)S(1)} %copy-done.10, ...), custom_call_target="tpu_custom_call" | custom-call | flops 1000000000 | bytes 2000000 | tf_op jit(solution)/shard_map/own_row/pallas_call | solution.py:776
  71.2 3.6 %all-to-all-start.1 = ((f32[16,3,4,128]{3,2,1,0:T(4,128)}), f32[16,3,4,128]{3,2,1,0:T(4,128)S(1)}, u32[]{:S(2)}, u32[]{:S(2)}) async-start(f32[16,3,4,128]{3,2,1,0:T(4,128)} %own_row.1), calls=%async_computation.1 | async-start | bytes 196608 | tf_op jit(solution)/shard_map/all_to_all | solution.py:893
  74.8 0.5 unpack_observations.1
  75.4 3.0 %collective-permute-start.6 = (f32[96,128]{1,0:T(8,128)S(1)}, f32[96,128]{1,0:T(8,128)S(1)}, u32[]{:S(2)}, u32[]{:S(2)}) collective-permute-start(f32[96,128]{1,0:T(8,128)S(1)} %get-tuple-element.47), channel_id=1, source_target_pairs={{0,31},{1,0},{2,1},{3,2},{4,3},{5,4},{6,5},{7,6},{8,7},{9,8},{10,9... | collective-permute-start | bytes 147464 | tf_op jit(solution)/shard_map/ppermute | solution.py:820
  78.3 0.9 collective-permute-done.5.corner_left_ref
  79.2 9.8 %all-to-all-done.1 = f32[16,3,4,128]{3,2,1,0:T(4,128)S(1)} async-done(((f32[16,3,4,128]{3,2,1,0:T(4,128)}), f32[16,3,4,128]{3,2,1,0:T(4,128)S(1)}, u32[]{:S(2)}, u32[]{:S(2)}) %all-to-all-start.1) | async-done | bytes 98336 | tf_op jit(solution)/shard_map/all_to_all | solution.py:893
  89.0 1.9 %all-gather = f32[32,3,4,128]{3,2,1,0:T(4,128)S(1)} all-gather(f32[16,3,4,128]{3,2,1,0:T(4,128)S(1)} %all-to-all-done.1), channel_id=2, replica_groups=mesh['band'=16,'z'=16,'core'=2] {'core'}, dimensions={0}, use_global_device_ids=true | all-gather | bytes 294912 | tf_op jit(solution)/shard_map/all_gather | solution.py:894
  91.0 0.4 band_edges.1
  91.3 5.2 %collective-permute-start.7 = (f32[56,128]{1,0:T(8,128)S(1)}, f32[56,128]{1,0:T(8,128)S(1)}, u32[]{:S(2)}, u32[]{:S(2)}) collective-permute-start(f32[56,128]{1,0:T(8,128)S(1)} %get-tuple-element.53), channel_id=1, source_target_pairs={{0,32},{32,64},{64,96},{96,128},{128,160},{160,192},{192,224},{224... | collective-permute-start | bytes 86024 | tf_op jit(solution)/shard_map/ppermute | solution.py:820
  96.6 1.9 %collective-permute-start.8 = (f32[56,128]{1,0:T(8,128)S(1)}, f32[56,128]{1,0:T(8,128)S(1)}, u32[]{:S(2)}, u32[]{:S(2)}) collective-permute-start(f32[56,128]{1,0:T(8,128)S(1)} %get-tuple-element.54), channel_id=1, source_target_pairs={{32,0},{64,32},{96,64},{128,96},{160,128},{192,160},{224,192},{256... | collective-permute-start | bytes 86024 | tf_op jit(solution)/shard_map/ppermute | solution.py:820
  98.5 1.9 %own_rows.1 = (f32[384,384]{1,0:T(8,128)S(1)}, f32[3,48,384]{2,1,0:T(8,128)S(1)}) custom-call(s32[2]{0:T(128)S(1)} %pad_add_fusion.place_ref.refs_0_, f32[2,16,3,4,128]{4,3,2,1,0:T(4,128)S(1)} %bitcast.9, f32[8,64]{1,0:T(8,128)S(1)} %get-tuple-element.34.filter_ref.refs_6_.refs_3_.refs_2_, f32[32,128]{1,0:T(8,128)S(1)} %copy-done.8, ...), custom_call_target="tpu_custom_call" | custom-call | flops 1000000000 | bytes 2000000 | tf_op jit(solution)/shard_map/own_rows/pallas_call | solution.py:776
  100.5 4.0 %collective-permute-done.8.below_ref = f32[56,128]{1,0:T(8,128)S(1)} collective-permute-done((f32[56,128]{1,0:T(8,128)S(1)}, f32[56,128]{1,0:T(8,128)S(1)}, u32[]{:S(2)}, u32[]{:S(2)}) %collective-permute-start.8) | collective-permute-done | bytes 28704 | tf_op jit(solution)/shard_map/ppermute | solution.py:820
  104.4 1.7 %last_stage.1 = (f32[64,270]{1,0:T(8,128)}, f32[64,270]{1,0:T(8,128)}, f32[64,270]{1,0:T(8,128)}) custom-call(s32[2]{0:T(128)S(1)} %pad_add_fusion.place_ref.refs_0_, f32[4,72,384]{2,1,0:T(8,128)S(1)} %get-tuple-element.39.refs_6_.wide_ref, f32[64,128]{1,0:T(8,128)S(1)} %collective-permute-done.refs_2_.refs_7_.left_ref, ...), custom_call_target="tpu_custom_call" | custom-call | flops 1000000000 | bytes 2000000 | tf_op jit(solution)/shard_map/last_stage/pallas_call | solution.py:776
  (30 shorter events, 0.2 us)
Async XLA Ops:
  0.6 15.7 %copy-start = (f32[128,256]{1,0:T(8,128)S(1)}, f32[128,256]{1,0:T(8,128)}, u32[]{:S(2)}) copy-start(f32[128,256]{1,0:T(8,128)} %values_ref.1) | copy-start | bytes 393220
  0.6 15.7 %copy-start.5 = (bf16[2,384,256]{2,1,0:T(8,128)(2,1)S(1)}, bf16[2,384,256]{2,1,0:T(8,128)(2,1)}, u32[]{:S(2)}) copy-start(bf16[2,384,256]{2,1,0:T(8,128)(2,1)} %constant.36.clone.table_ref.refs_10_) | copy-start | bytes 1179652
  2.0 15.8 %collective-permute-start.2 = (f32[16,384]{1,0:T(8,128)S(1)}, f32[16,384]{1,0:T(8,128)S(1)}, u32[]{:S(2)}, u32[]{:S(2)}) collective-permute-start(f32[16,384]{1,0:T(8,128)S(1)} %get-tuple-element.32), channel_id=1, source_target_pairs={{0,32},{32,64},{64,96},{96,128},{128,160},{160,192},{192,224},{224... | collective-permute-start | bytes 73736 | tf_op jit(solution)/shard_map/ppermute | solution.py:820
  5.1 12.7 %collective-permute-start.3 = (f32[16,384]{1,0:T(8,128)S(1)}, f32[16,384]{1,0:T(8,128)S(1)}, u32[]{:S(2)}, u32[]{:S(2)}) collective-permute-start(f32[16,384]{1,0:T(8,128)S(1)} %get-tuple-element.33), channel_id=1, source_target_pairs={{32,0},{64,32},{96,64},{128,96},{160,128},{192,160},{224,192},{256... | collective-permute-start | bytes 73736 | tf_op jit(solution)/shard_map/ppermute | solution.py:820
  7.9 8.5 %copy-start.7 = (f32[32,128]{1,0:T(8,128)S(1)}, f32[32,128]{1,0:T(8,128)}, u32[]{:S(2)}) copy-start(f32[32,128]{1,0:T(8,128)} %constant.35.clone.sin_ref.refs_9_.refs_4_) | copy-start | bytes 49156
  7.9 8.5 %copy-start.8 = (f32[32,128]{1,0:T(8,128)S(1)}, f32[32,128]{1,0:T(8,128)}, u32[]{:S(2)}) copy-start(f32[32,128]{1,0:T(8,128)} %constant.34.clone.cos_ref.refs_8_.refs_3_) | copy-start | bytes 49156
  7.9 10.0 %collective-permute-start = (f32[64,128]{1,0:T(8,128)S(1)}, f32[64,128]{1,0:T(8,128)S(1)}, u32[]{:S(2)}, u32[]{:S(2)}) collective-permute-start(f32[64,128]{1,0:T(8,128)S(1)} %get-tuple-element.30), channel_id=1, source_target_pairs={{0,1},{1,2},{2,3},{3,4},{4,5},{5,6},{6,7},{7,8},{8,9},{9,10},{10,1... | collective-permute-start | bytes 98312 | tf_op jit(solution)/shard_map/ppermute | solution.py:820
  7.9 10.0 %collective-permute-start.1 = (f32[64,128]{1,0:T(8,128)S(1)}, f32[64,128]{1,0:T(8,128)S(1)}, u32[]{:S(2)}, u32[]{:S(2)}) collective-permute-start(f32[64,128]{1,0:T(8,128)S(1)} %get-tuple-element.31), channel_id=1, source_target_pairs={{0,31},{1,0},{2,1},{3,2},{4,3},{5,4},{6,5},{7,6},{8,7},{9,8},{10,9... | collective-permute-start | bytes 98312 | tf_op jit(solution)/shard_map/ppermute | solution.py:820
  16.4 1.5 %copy-start.1 = (bf16[2,384,512]{2,1,0:T(8,128)(2,1)S(1)}, bf16[2,384,512]{2,1,0:T(8,128)(2,1)}, u32[]{:S(2)}) copy-start(bf16[2,384,512]{2,1,0:T(8,128)(2,1)} %constant.38.clone.refs_11_) | copy-start | bytes 2359300
  16.4 1.5 %copy-start.6 = (f32[72,128]{1,0:T(8,128)S(1)}, f32[72,128]{1,0:T(8,128)}, u32[]{:S(2)}) copy-start(f32[72,128]{1,0:T(8,128)} %constant.37.clone.refs_7_.refs_11_.terms_ref) | copy-start | bytes 110596
  19.8 3.7 %collective-permute-start.4 = (f32[16,56,128]{2,1,0:T(8,128)S(1)}, f32[16,56,128]{2,1,0:T(8,128)S(1)}, u32[]{:S(2)}, u32[]{:S(2)}) collective-permute-start(f32[16,56,128]{2,1,0:T(8,128)S(1)} %get-tuple-element.41), channel_id=1, source_target_pairs={{0,1},{1,0},{2,3},{3,2},{4,5},{5,4},{6,7},{7,6},{8,9},{9,8},{10,11... | collective-permute-start | bytes 1376264 | tf_op jit(solution)/shard_map/ppermute | solution.py:874
  23.6 45.8 %copy-start.2 = (bf16[2,512,256]{2,1,0:T(8,128)(2,1)S(1)}, bf16[2,512,256]{2,1,0:T(8,128)(2,1)}, u32[]{:S(2)}) copy-start(bf16[2,512,256]{2,1,0:T(8,128)(2,1)} %constant.42.clone.from_grid_ref) | copy-start | bytes 1572868
  23.6 45.8 %copy-start.3 = (bf16[2,256,512]{2,1,0:T(8,128)(2,1)S(1)}, bf16[2,256,512]{2,1,0:T(8,128)(2,1)}, u32[]{:S(2)}) copy-start(bf16[2,256,512]{2,1,0:T(8,128)(2,1)} %constant.41.clone.to_grid_ref) | copy-start | bytes 1572868
  23.6 45.8 %copy-start.9 = (f32[16,256]{1,0:T(8,128)S(1)}, f32[16,256]{1,0:T(8,128)}, u32[]{:S(2)}) copy-start(f32[16,256]{1,0:T(8,128)} %constant.39.clone.lines_ref) | copy-start | bytes 49156
  23.6 45.8 %copy-start.10 = (f32[8,128]{1,0:T(8,128)S(1)}, f32[8,128]{1,0:T(8,128)}, u32[]{:S(2)}) copy-start(f32[8,128]{1,0:T(8,128)} %constant.40.clone.slope_ref) | copy-start | bytes 12292
  71.2 17.8 %all-to-all-start.1 = ((f32[16,3,4,128]{3,2,1,0:T(4,128)}), f32[16,3,4,128]{3,2,1,0:T(4,128)S(1)}, u32[]{:S(2)}, u32[]{:S(2)}) async-start(f32[16,3,4,128]{3,2,1,0:T(4,128)} %own_row.1), calls=%async_computation.1 | async-start | bytes 196608 | tf_op jit(solution)/shard_map/all_to_all | solution.py:893
  74.8 4.4 %collective-permute-start.5 = (f32[32,128]{1,0:T(8,128)S(1)}, f32[32,128]{1,0:T(8,128)S(1)}, u32[]{:S(2)}, u32[]{:S(2)}) collective-permute-start(f32[32,128]{1,0:T(8,128)S(1)} %get-tuple-element.45), channel_id=1, source_target_pairs={{0,1},{1,2},{2,3},{3,4},{4,5},{5,6},{6,7},{7,8},{8,9},{9,10},{10,1... | collective-permute-start | bytes 49160 | tf_op jit(solution)/shard_map/ppermute | solution.py:820
  75.4 15.6 %collective-permute-start.6 = (f32[96,128]{1,0:T(8,128)S(1)}, f32[96,128]{1,0:T(8,128)S(1)}, u32[]{:S(2)}, u32[]{:S(2)}) collective-permute-start(f32[96,128]{1,0:T(8,128)S(1)} %get-tuple-element.47), channel_id=1, source_target_pairs={{0,31},{1,0},{2,1},{3,2},{4,3},{5,4},{6,5},{7,6},{8,7},{9,8},{10,9... | collective-permute-start | bytes 147464 | tf_op jit(solution)/shard_map/ppermute | solution.py:820
  91.0 7.5 %copy-start.4 = (bf16[2,256,384]{2,1,0:T(8,128)(2,1)S(1)}, bf16[2,256,384]{2,1,0:T(8,128)(2,1)}, u32[]{:S(2)}) copy-start(bf16[2,256,384]{2,1,0:T(8,128)(2,1)} %constant.43.clone.refs_5_.table_ref) | copy-start | bytes 1179652
  91.3 9.1 %collective-permute-start.7 = (f32[56,128]{1,0:T(8,128)S(1)}, f32[56,128]{1,0:T(8,128)S(1)}, u32[]{:S(2)}, u32[]{:S(2)}) collective-permute-start(f32[56,128]{1,0:T(8,128)S(1)} %get-tuple-element.53), channel_id=1, source_target_pairs={{0,32},{32,64},{64,96},{96,128},{128,160},{160,192},{192,224},{224... | collective-permute-start | bytes 86024 | tf_op jit(solution)/shard_map/ppermute | solution.py:820
  96.6 7.9 %collective-permute-start.8 = (f32[56,128]{1,0:T(8,128)S(1)}, f32[56,128]{1,0:T(8,128)S(1)}, u32[]{:S(2)}, u32[]{:S(2)}) collective-permute-start(f32[56,128]{1,0:T(8,128)S(1)} %get-tuple-element.54), channel_id=1, source_target_pairs={{32,0},{64,32},{96,64},{128,96},{160,128},{192,160},{224,192},{256... | collective-permute-start | bytes 86024 | tf_op jit(solution)/shard_map/ppermute | solution.py:820

commit v5 on v4

--- a/solution.py
+++ b/solution.py
@@ -60,6 +60,10 @@
 
 def iota(shape, dim):
     return lax.broadcasted_iota(jnp.int32, shape, dim)
+
+
+def own_place():
+    return lax.axis_index("band"), 2 * lax.axis_index("z") + lax.axis_index("core")
 
 
 def to_col(row):
@@ -202,7 +206,6 @@
 
 def partial_sums(
     cols,
-    place_ref,
     fields_ref,
     left_ref,
     right_ref,
@@ -231,7 +234,7 @@
     ext = rows + 2 * HALO
     devices = cos_ref.shape[0]
     half = devices // 2
-    band, lon = place_ref[0], place_ref[1]
+    band, lon = own_place()
     for f in range(4):
         ext_ref[f, 0:rows, :] = fields_ref[f]
         ext_ref[f, rows : rows + HALO, :] = below_ref[HALO * f : HALO * f + HALO, :]
@@ -274,7 +277,7 @@
     )
     new_east = east_rest - rotation * north_rest + COURANT * share * metric * lon_diff(middle)
     new_north = north_rest + rotation * east_rest + COURANT * share * lat_diff(middle)
-    chosen = slot_rows(mask, place_ref[1] % 2, devices).astype(jnp.bfloat16)
+    chosen = slot_rows(mask, own_place()[1] % 2, devices).astype(jnp.bfloat16)
     sources = (height, east, north, low_height, lat_diff(low_height), middle, new_east, new_north)
     for v, field in enumerate(sources):
         lines = slice(devices * v, devices * v + devices)
@@ -313,7 +316,6 @@
 
 
 def pack_observations(
-    place_ref,
     values_ref,
     marks_ref,
     filter_ref,
@@ -327,7 +329,7 @@
     number, width = values_ref.shape
     half = near_ref.shape[0]
     devices = 2 * half
-    core = place_ref[1] % 2
+    core = own_place()[1] % 2
     lengths = to_col(marks_ref[2:3, :])
     values = jnp.where(iota((number, width), 1).astype(F32) < lengths, values_ref[...], 0.0)
     high, low = halves_of(values)
@@ -370,15 +372,16 @@
     placed_ref[:, 128:256] = pick_dot(chosen, all_sin)
 
 
-def join(mine_ref, swapped_ref, out_ref):
+def join(mine_ref, both_ref, out_ref):
+    other = 1 - own_place()[1] % 2
     for i in range(12):
         pair = slice(2 * i, 2 * i + 2)
-        out_ref[:, i, :, :] = mine_ref[:, pair, :] + swapped_ref[:, pair, :]
+        out_ref[:, i, :, :] = mine_ref[:, pair, :] + both_ref[other, :, pair, :]
     for i in range(12, 24):
         out_ref[:, i, :, :] = mine_ref[:, 2 * i : 2 * i + 2, :]
-        out_ref[:, i + 12, :, :] = swapped_ref[:, 2 * i : 2 * i + 2, :]
+        out_ref[:, i + 12, :, :] = both_ref[other, :, 2 * i : 2 * i + 2, :]
     out_ref[:, 36, 0, :] = mine_ref[:, 48, :]
-    out_ref[:, 36, 1, :] = swapped_ref[:, 48, :]
+    out_ref[:, 36, 1, :] = both_ref[other, :, 48, :]
 
 
 def unpack_observations(in_ref, corner_ref, dep_ref, west_ref, data_ref):
@@ -409,7 +412,6 @@
 
 
 def own_row(
-    place_ref,
     in_ref,
     filter_ref,
     lines_ref,
@@ -422,7 +424,7 @@
     res_ref,
     sum_ref,
 ):
-    band, lon = place_ref[0], place_ref[1]
+    band, lon = own_place()
     pairs = in_ref[0, 0:12, :, :]
     for i in range(1, in_ref.shape[0]):
         pairs = pairs + in_ref[i, 0:12, :, :]
@@ -537,7 +539,6 @@
 
 def own_rows(
     cols,
-    place_ref,
     all_ref,
     filter_ref,
     cos_ref,
@@ -556,7 +557,7 @@
 ):
     mask = filter_ref[0:1, :]
     rows = mask.shape[1]
-    band, lon = place_ref[0], place_ref[1]
+    band, lon = own_place()
     turn_cos, turn_sin = cos_ref[pl.ds(lon, 1), :], sin_ref[pl.ds(lon, 1), :]
     coef = slots_to_rows(all_ref, mask, iota((rows, 1), 0))
     for f in range(6):
@@ -583,7 +584,6 @@
 
 
 def last_stage(
-    place_ref,
     wide_ref,
     left_ref,
     right_ref,
@@ -612,7 +612,7 @@
 ):
     rows, cols = h_ref.shape
     ext = rows + 2 * HALO
-    band, lon = place_ref[0], place_ref[1]
+    band, lon = own_place()
     pairs = ((h_ref, h_hbm), (e_ref, e_hbm), (n_ref, n_hbm))
     spans = (pl.ds(SURE, rows - 2 * SURE), pl.ds(0, SURE), pl.ds(rows - SURE, SURE))
     copies = [
@@ -758,14 +758,13 @@
 
 
 VMEM = pl.BlockSpec(memory_space=pltpu.VMEM)
-SMEM = pl.BlockSpec(memory_space=pltpu.SMEM)
 HBM = pl.BlockSpec(memory_space=pltpu.HBM)
 
 
-def call(kernel, name, outs, args, scratch=(), scalars=False, direct=(), cost=1.0, outside=False):
+def call(kernel, name, outs, args, scratch=(), direct=(), cost=1.0, outside=False):
     shapes = [jax.ShapeDtypeStruct(shape, F32) for shape in outs]
     specs = [
-        SMEM if scalars and i == 0 else HBM if i in direct else VMEM for i in range(len(args))
+        HBM if i in direct else VMEM for i in range(len(args))
     ]
     args = [
         pltpu.with_memory_space_constraint(arg, pltpu.HBM) if i in direct else arg
@@ -812,7 +811,6 @@
     number, width = obs_values.shape
     ext = rows + 2 * HALO
     made = tables(cols * devices, cols, devices, rows, bands)
-    place = jnp.stack([lax.axis_index("band"), lax.axis_index(LON)]).astype(jnp.int32)
 
     def send(value, axis, shift, closed):
         count = lax.axis_size(axis)
@@ -838,21 +836,18 @@
     )
     below, above = send(north, "band", -1, False), send(south, "band", 1, False)
     right, left = send(west, LON, -1, True), send(east, LON, 1, True)
-    other_core = [(i, i ^ 1) for i in range(devices)]
     near, far, placed = call(
         pack_observations,
         "pack_observations",
         [(half, 32, 128), (half, 32, 128), (devices, 256)],
-        (place, obs_values, marks, kept, made["cos"], made["sin"], made["analyse"]),
+        (obs_values, marks, kept, made["cos"], made["sin"], made["analyse"]),
         cost=3.0,
-        scalars=True,
     )
     wide, weight, corner_west, corner_east, mine, other = call(
         lambda *refs: partial_sums(cols, *refs),
         "partial_sums",
         [(4, ext, LANES), (ext, 128)] + [(8 * HALO, 128)] * 2 + [(half, 56, 128)] * 2,
         (
-            place,
             fields,
             left,
             right,
@@ -869,17 +864,17 @@
             far,
         ),
         scratch=[pltpu.VMEM((n * devices, LANES), jnp.bfloat16) for n in (8, 8, 2)],
-        scalars=True,
-    )
-    swapped = lax.ppermute(other, LON, other_core)
-    (joined,) = call(join, "join", [(half, 37, 2, 128)], (mine, swapped))
+    )
+    swapped = lax.all_gather(other, "core", axis=0, tiled=False)
+    (joined,) = call(
+        join, "join", [(half, 37, 2, 128)], (mine, swapped)
+    )
     owned = lax.all_to_all(joined, "z", split_axis=0, concat_axis=0, tiled=True)
     (spread,) = call(
         own_row,
         "own_row",
         [(half, 3, 4, 128)],
         (
-            place,
             owned,
             kept,
             made["lines"],
@@ -888,7 +883,6 @@
             made["from_grid"],
         ),
         scratch=[(8, 256), (8, GRID), (12, 128), (24, 128)],
-        scalars=True,
     )
     shared = lax.all_to_all(spread, "z", split_axis=0, concat_axis=0, tiled=True)
     everyone = lax.all_gather(shared, "core", axis=0, tiled=False)
@@ -914,7 +908,6 @@
         "own_rows",
         [(6 * rows, LANES), (3, rows - 2 * SURE, LANES)],
         (
-            place,
             everyone,
             kept,
             made["cos"],
@@ -928,7 +921,6 @@
             made["terms"],
         ),
         scratch=[(6 * rows, 256), (4, rows, LANES)],
-        scalars=True,
     )
     edge = 2 * EDGE + 2 * HALO
     return tuple(
@@ -937,7 +929,6 @@
             "last_stage",
             [(rows, cols)] * 3,
             (
-                place,
                 wide,
                 left,
                 right,
@@ -958,7 +949,6 @@
             + [(rows, cols)] * 3
             + [pltpu.SemaphoreType.DMA((3, 3))],
             outside=True,
-            scalars=True,
         )
     )
 

time: 107 us -> 104 us (0.972)
  Pallas kernels: 10.9 us -> 8.25 us
  blocking collectives: 47.7 us -> 50.2 us
  starting transfers between devices: 29.9 us -> 28 us
    pallas_call x9, Pallas kernels: 10.9 us -> 8.25 us  [call(): pl.pallas_call(kernel, name=name, out_shape=shapes, in_specs=specs, out_s...]
    all_gather x0 -> x1, blocking collectives: none -> 2.46 us  [on_device(): swapped = lax.all_gather(other, 'core', axis=0, tiled=False)]
    ppermute x1 -> x0, starting transfers between devices: 1.92 us -> none  [on_device(): swapped = lax.ppermute(other, LON, other_core)]
    ppermute x1 -> x0, waiting for transfers between devices: 1.78 us -> none  [on_device(): swapped = lax.ppermute(other, LON, other_core)]
    ppermute x8, waiting for transfers between devices: 4.99 us -> 6.14 us  [send(): return lax.ppermute(value, axis, pairs)]
  transfers between devices with their start and end apart: 10 -> 9, of which waited for: 5 -> 4; matrix products, arithmetic and copies ran while one was open for 0% -> 0% of each run, Pallas kernels for 4% -> 3%
where the time goes in v5:
time: 104 us; the launch traced here: 103 us
  blocking collectives  50.2 us (48%)
  starting transfers between devices  28 us (27%)
  waiting for transfers between devices  15.9 us (15%)
  Pallas kernels  8.25 us (8%)
    all_to_all x1, blocking collectives, on_device(): owned = lax.all_to_all(joined, 'z', split_axis=0, concat_axis=0, tiled=True)  45.8 us
    ppermute x8, starting transfers between devices, send(): return lax.ppermute(value, axis, pairs)  24.4 us
    all_to_all x1, waiting for transfers between devices, on_device(): lax.all_to_all(spread, 'z', split_axis=0, concat_axis=0, tiled=True)  9.81 us
    pallas_call x9, Pallas kernels, call(): pl.pallas_call(kernel, name=name, out_shape=shapes, in_specs=specs, out_s...  8.25 us
    ppermute x8, waiting for transfers between devices, send(): return lax.ppermute(value, axis, pairs)  6.14 us
    all_to_all x1, starting transfers between devices, on_device(): lax.all_to_all(spread, 'z', split_axis=0, concat_axis=0, tiled=True)  3.64 us
    all_gather x1, blocking collectives, on_device(): swapped = lax.all_gather(other, 'core', axis=0, tiled=False)  2.46 us
  transfers between devices with their start and end apart: 9, of which 4 were waited for; matrix products, arithmetic and copies ran while one was open for 0% of the time, Pallas kernels for 3%

profile of v5, /device:TPU:24, one launch (start us, length us, event | category | flops | bytes accessed | tf_op | source)
XLA Modules:
  0.0 103.3 jit_solution(18141007013827456069)
XLA Ops:
  0.7 1.3 %pack_tile.1 = (f32[4,64,384]{2,1,0:T(8,128)S(1)}, f32[64,128]{1,0:T(8,128)S(1)}, f32[64,128]{1,0:T(8,128)S(1)}, f32[16,384]{1,0:T(8,128)S(1)}, f32[16,384]{1,0:...) custom-call(f32[64,270]{1,0:T(8,128)} %h_hbm.1, f32[64,270]{1,0:T(8,128)} %e_hbm.1, f32[64,270]{1,0:T(8,128)} %n_hbm.1, ...), custom_call_target="tpu_custom_call" | custom-call | flops 1000000000 | bytes 2000000 | tf_op jit(solution)/shard_map/pack_tile/pallas_call | solution.py:775
  2.0 3.1 %collective-permute-start.2 = (f32[16,384]{1,0:T(8,128)S(1)}, f32[16,384]{1,0:T(8,128)S(1)}, u32[]{:S(2)}, u32[]{:S(2)}) collective-permute-start(f32[16,384]{1,0:T(8,128)S(1)} %get-tuple-element.32), channel_id=1, source_target_pairs={{0,32},{32,64},{64,96},{96,128},{128,160},{160,192},{192,224},{224... | collective-permute-start | bytes 73736 | tf_op jit(solution)/shard_map/ppermute | solution.py:818
  5.1 2.8 %collective-permute-start.3 = (f32[16,384]{1,0:T(8,128)S(1)}, f32[16,384]{1,0:T(8,128)S(1)}, u32[]{:S(2)}, u32[]{:S(2)}) collective-permute-start(f32[16,384]{1,0:T(8,128)S(1)} %get-tuple-element.33), channel_id=1, source_target_pairs={{32,0},{64,32},{96,64},{128,96},{160,128},{192,160},{224,192},{256... | collective-permute-start | bytes 73736 | tf_op jit(solution)/shard_map/ppermute | solution.py:818
  7.9 8.4 %collective-permute-start.1 = (f32[64,128]{1,0:T(8,128)S(1)}, f32[64,128]{1,0:T(8,128)S(1)}, u32[]{:S(2)}, u32[]{:S(2)}) collective-permute-start(f32[64,128]{1,0:T(8,128)S(1)} %get-tuple-element.31), channel_id=1, source_target_pairs={{0,31},{1,0},{2,1},{3,2},{4,3},{5,4},{6,5},{7,6},{8,7},{9,8},{10,9... | collective-permute-start | bytes 98312 | tf_op jit(solution)/shard_map/ppermute | solution.py:818
  16.3 0.8 pack_observations.1
  17.2 0.7 collective-permute-done.refs_1_.refs_6_.left_ref
  17.9 0.0 collective-permute-done.1.refs_2_.refs_7_.right_ref
  17.9 1.3 %partial_sums.1 = (f32[4,72,384]{2,1,0:T(8,128)S(1)}, f32[72,128]{1,0:T(8,128)S(1)}, f32[32,128]{1,0:T(8,128)S(1)}, f32[32,128]{1,0:T(8,128)S(1)}, f32[16,56,128...) custom-call(f32[4,64,384]{2,1,0:T(8,128)S(1)} %get-tuple-element.29.refs_0_, ...), custom_call_target="tpu_custom_call" | custom-call | flops 1000000000 | bytes 2000000 | tf_op jit(solution)/shard_map/partial_sums/pallas_call | solution.py:775
  19.2 2.5 %all-gather = f32[32,56,128]{2,1,0:T(8,128)S(1)} all-gather(f32[16,56,128]{2,1,0:T(8,128)S(1)} %get-tuple-element.41), channel_id=2, replica_groups=mesh['band'=16,'z'=16,'core'=2] {'core'}, dimensions={0}, use_global_device_ids=true | all-gather | bytes 1376256 | tf_op jit(solution)/shard_map/all_gather | solution.py:868
  21.7 0.1 join.1
  21.9 45.8 %all_to_all.10.in_ref = f32[16,37,2,128]{3,2,1,0:T(2,128)S(1)} all-to-all(f32[16,37,2,128]{3,2,1,0:T(2,128)S(1)} %join.1), channel_id=1, replica_groups=mesh['band'=16,'z'=16,'core'=2] {'z'}, dimensions={0} | all-to-all | bytes 1212416 | tf_op jit(solution)/shard_map/all_to_all | solution.py:872
  67.7 1.2 %own_row.1 = f32[16,3,4,128]{3,2,1,0:T(4,128)} custom-call(f32[16,37,2,128]{3,2,1,0:T(2,128)S(1)} %all_to_all.10.in_ref, f32[8,64]{1,0:T(8,128)S(1)} %get-tuple-element.34.filter_ref.refs_5_.refs_3_.refs_1_, f32[16,256]{1,0:T(8,128)S(1)} %copy-done.9, f32[8,128]{1,0:T(8,128)S(1)} %copy-done.10, bf16[2,256,512]{2,1,0:T(8,128)(2,1)S(1)} %copy-done.3, ...), custom_call_target="tpu_custom_call" | custom-call | flops 1000000000 | bytes 2000000 | tf_op jit(solution)/shard_map/own_row/pallas_call | solution.py:775
  68.8 3.6 %all-to-all-start.1 = ((f32[16,3,4,128]{3,2,1,0:T(4,128)}), f32[16,3,4,128]{3,2,1,0:T(4,128)S(1)}, u32[]{:S(2)}, u32[]{:S(2)}) async-start(f32[16,3,4,128]{3,2,1,0:T(4,128)} %own_row.1), calls=%async_computation.1 | async-start | bytes 196608 | tf_op jit(solution)/shard_map/all_to_all | solution.py:887
  72.5 0.5 unpack_observations.1
  73.0 3.0 %collective-permute-start.5 = (f32[96,128]{1,0:T(8,128)S(1)}, f32[96,128]{1,0:T(8,128)S(1)}, u32[]{:S(2)}, u32[]{:S(2)}) collective-permute-start(f32[96,128]{1,0:T(8,128)S(1)} %get-tuple-element.47), channel_id=1, source_target_pairs={{0,31},{1,0},{2,1},{3,2},{4,3},{5,4},{6,5},{7,6},{8,7},{9,8},{10,9... | collective-permute-start | bytes 147464 | tf_op jit(solution)/shard_map/ppermute | solution.py:818
  76.0 0.9 collective-permute-done.4.corner_left_ref
  76.9 9.8 %all-to-all-done.1 = f32[16,3,4,128]{3,2,1,0:T(4,128)S(1)} async-done(((f32[16,3,4,128]{3,2,1,0:T(4,128)}), f32[16,3,4,128]{3,2,1,0:T(4,128)S(1)}, u32[]{:S(2)}, u32[]{:S(2)}) %all-to-all-start.1) | async-done | bytes 98336 | tf_op jit(solution)/shard_map/all_to_all | solution.py:887
  86.7 1.9 %all-gather.1 = f32[32,3,4,128]{3,2,1,0:T(4,128)S(1)} all-gather(f32[16,3,4,128]{3,2,1,0:T(4,128)S(1)} %all-to-all-done.1), channel_id=3, replica_groups=mesh['band'=16,'z'=16,'core'=2] {'core'}, dimensions={0}, use_global_device_ids=true | all-gather | bytes 294912 | tf_op jit(solution)/shard_map/all_gather | solution.py:888
  88.6 0.4 band_edges.1
  89.0 5.2 %collective-permute-start.6 = (f32[56,128]{1,0:T(8,128)S(1)}, f32[56,128]{1,0:T(8,128)S(1)}, u32[]{:S(2)}, u32[]{:S(2)}) collective-permute-start(f32[56,128]{1,0:T(8,128)S(1)} %get-tuple-element.53), channel_id=1, source_target_pairs={{0,32},{32,64},{64,96},{96,128},{128,160},{160,192},{192,224},{224... | collective-permute-start | bytes 86024 | tf_op jit(solution)/shard_map/ppermute | solution.py:818
  94.2 1.9 %collective-permute-start.7 = (f32[56,128]{1,0:T(8,128)S(1)}, f32[56,128]{1,0:T(8,128)S(1)}, u32[]{:S(2)}, u32[]{:S(2)}) collective-permute-start(f32[56,128]{1,0:T(8,128)S(1)} %get-tuple-element.54), channel_id=1, source_target_pairs={{32,0},{64,32},{96,64},{128,96},{160,128},{192,160},{224,192},{256... | collective-permute-start | bytes 86024 | tf_op jit(solution)/shard_map/ppermute | solution.py:818
  96.2 1.4 %own_rows.1 = (f32[384,384]{1,0:T(8,128)S(1)}, f32[3,48,384]{2,1,0:T(8,128)S(1)}) custom-call(f32[2,16,3,4,128]{4,3,2,1,0:T(4,128)S(1)} %bitcast.9, f32[8,64]{1,0:T(8,128)S(1)} %get-tuple-element.34.filter_ref.refs_5_.refs_3_.refs_1_, f32[32,128]{1,0:T(8,128)S(1)} %copy-done.8, f32[32,128]{1,0:T(8,128)S(1)} %copy-done.7, bf16[2,256,384]{2,1,0:T(8,128)(2,1)S(1)} %copy-done.4, ...), custom_call_target="tpu_custom_call" | custom-call | flops 1000000000 | bytes 2000000 | tf_op jit(solution)/shard_map/own_rows/pallas_call | solution.py:775
  97.6 4.5 %collective-permute-done.7.below_ref = f32[56,128]{1,0:T(8,128)S(1)} collective-permute-done((f32[56,128]{1,0:T(8,128)S(1)}, f32[56,128]{1,0:T(8,128)S(1)}, u32[]{:S(2)}, u32[]{:S(2)}) %collective-permute-start.7) | collective-permute-done | bytes 28704 | tf_op jit(solution)/shard_map/ppermute | solution.py:818
  102.1 1.2 %last_stage.1 = (f32[64,270]{1,0:T(8,128)}, f32[64,270]{1,0:T(8,128)}, f32[64,270]{1,0:T(8,128)}) custom-call(f32[4,72,384]{2,1,0:T(8,128)S(1)} %get-tuple-element.39.refs_5_.wide_ref, f32[64,128]{1,0:T(8,128)S(1)} %collective-permute-done.refs_1_.refs_6_.left_ref, f32[64,128]{1,0:T(8,128)S(1)} %collective-permute-done.1.refs_2_.refs_7_.right_ref, ...), custom_call_target="tpu_custom_call" | custom-call | flops 1000000000 | bytes 2000000 | tf_op jit(solution)/shard_map/last_stage/pallas_call | solution.py:775
  (28 shorter events, 0.1 us)
Async XLA Ops:
  0.6 15.7 %copy-start = (f32[128,256]{1,0:T(8,128)S(1)}, f32[128,256]{1,0:T(8,128)}, u32[]{:S(2)}) copy-start(f32[128,256]{1,0:T(8,128)} %values_ref.1) | copy-start | bytes 393220
  0.6 15.7 %copy-start.5 = (bf16[2,384,256]{2,1,0:T(8,128)(2,1)S(1)}, bf16[2,384,256]{2,1,0:T(8,128)(2,1)}, u32[]{:S(2)}) copy-start(bf16[2,384,256]{2,1,0:T(8,128)(2,1)} %constant.22.clone.table_ref.refs_9_) | copy-start | bytes 1179652
  0.7 15.7 %copy-start.7 = (f32[32,128]{1,0:T(8,128)S(1)}, f32[32,128]{1,0:T(8,128)}, u32[]{:S(2)}) copy-start(f32[32,128]{1,0:T(8,128)} %constant.21.clone.sin_ref.refs_8_.refs_3_) | copy-start | bytes 49156
  0.7 15.6 %copy-start.8 = (f32[32,128]{1,0:T(8,128)S(1)}, f32[32,128]{1,0:T(8,128)}, u32[]{:S(2)}) copy-start(f32[32,128]{1,0:T(8,128)} %constant.20.clone.cos_ref.refs_7_.refs_2_) | copy-start | bytes 49156
  2.0 15.1 %collective-permute-start.2 = (f32[16,384]{1,0:T(8,128)S(1)}, f32[16,384]{1,0:T(8,128)S(1)}, u32[]{:S(2)}, u32[]{:S(2)}) collective-permute-start(f32[16,384]{1,0:T(8,128)S(1)} %get-tuple-element.32), channel_id=1, source_target_pairs={{0,32},{32,64},{64,96},{96,128},{128,160},{160,192},{192,224},{224... | collective-permute-start | bytes 73736 | tf_op jit(solution)/shard_map/ppermute | solution.py:818
  5.1 12.1 %collective-permute-start.3 = (f32[16,384]{1,0:T(8,128)S(1)}, f32[16,384]{1,0:T(8,128)S(1)}, u32[]{:S(2)}, u32[]{:S(2)}) collective-permute-start(f32[16,384]{1,0:T(8,128)S(1)} %get-tuple-element.33), channel_id=1, source_target_pairs={{32,0},{64,32},{96,64},{128,96},{160,128},{192,160},{224,192},{256... | collective-permute-start | bytes 73736 | tf_op jit(solution)/shard_map/ppermute | solution.py:818
  7.9 10.0 %collective-permute-start = (f32[64,128]{1,0:T(8,128)S(1)}, f32[64,128]{1,0:T(8,128)S(1)}, u32[]{:S(2)}, u32[]{:S(2)}) collective-permute-start(f32[64,128]{1,0:T(8,128)S(1)} %get-tuple-element.30), channel_id=1, source_target_pairs={{0,1},{1,2},{2,3},{3,4},{4,5},{5,6},{6,7},{7,8},{8,9},{9,10},{10,1... | collective-permute-start | bytes 98312 | tf_op jit(solution)/shard_map/ppermute | solution.py:818
  7.9 10.0 %collective-permute-start.1 = (f32[64,128]{1,0:T(8,128)S(1)}, f32[64,128]{1,0:T(8,128)S(1)}, u32[]{:S(2)}, u32[]{:S(2)}) collective-permute-start(f32[64,128]{1,0:T(8,128)S(1)} %get-tuple-element.31), channel_id=1, source_target_pairs={{0,31},{1,0},{2,1},{3,2},{4,3},{5,4},{6,5},{7,6},{8,7},{9,8},{10,9... | collective-permute-start | bytes 98312 | tf_op jit(solution)/shard_map/ppermute | solution.py:818
  16.3 1.6 %copy-start.1 = (bf16[2,384,512]{2,1,0:T(8,128)(2,1)S(1)}, bf16[2,384,512]{2,1,0:T(8,128)(2,1)}, u32[]{:S(2)}) copy-start(bf16[2,384,512]{2,1,0:T(8,128)(2,1)} %constant.24.clone.refs_10_) | copy-start | bytes 2359300
  16.3 1.6 %copy-start.6 = (f32[72,128]{1,0:T(8,128)S(1)}, f32[72,128]{1,0:T(8,128)}, u32[]{:S(2)}) copy-start(f32[72,128]{1,0:T(8,128)} %constant.23.clone.refs_6_.refs_10_.terms_ref) | copy-start | bytes 110596
  21.8 45.8 %copy-start.2 = (bf16[2,512,256]{2,1,0:T(8,128)(2,1)S(1)}, bf16[2,512,256]{2,1,0:T(8,128)(2,1)}, u32[]{:S(2)}) copy-start(bf16[2,512,256]{2,1,0:T(8,128)(2,1)} %constant.28.clone.from_grid_ref) | copy-start | bytes 1572868
  21.8 45.8 %copy-start.3 = (bf16[2,256,512]{2,1,0:T(8,128)(2,1)S(1)}, bf16[2,256,512]{2,1,0:T(8,128)(2,1)}, u32[]{:S(2)}) copy-start(bf16[2,256,512]{2,1,0:T(8,128)(2,1)} %constant.27.clone.to_grid_ref) | copy-start | bytes 1572868
  21.8 45.8 %copy-start.9 = (f32[16,256]{1,0:T(8,128)S(1)}, f32[16,256]{1,0:T(8,128)}, u32[]{:S(2)}) copy-start(f32[16,256]{1,0:T(8,128)} %constant.25.clone.lines_ref) | copy-start | bytes 49156
  21.9 45.8 %copy-start.10 = (f32[8,128]{1,0:T(8,128)S(1)}, f32[8,128]{1,0:T(8,128)}, u32[]{:S(2)}) copy-start(f32[8,128]{1,0:T(8,128)} %constant.26.clone.slope_ref) | copy-start | bytes 12292
  68.8 17.8 %all-to-all-start.1 = ((f32[16,3,4,128]{3,2,1,0:T(4,128)}), f32[16,3,4,128]{3,2,1,0:T(4,128)S(1)}, u32[]{:S(2)}, u32[]{:S(2)}) async-start(f32[16,3,4,128]{3,2,1,0:T(4,128)} %own_row.1), calls=%async_computation.1 | async-start | bytes 196608 | tf_op jit(solution)/shard_map/all_to_all | solution.py:887
  72.5 4.4 %collective-permute-start.4 = (f32[32,128]{1,0:T(8,128)S(1)}, f32[32,128]{1,0:T(8,128)S(1)}, u32[]{:S(2)}, u32[]{:S(2)}) collective-permute-start(f32[32,128]{1,0:T(8,128)S(1)} %get-tuple-element.45), channel_id=1, source_target_pairs={{0,1},{1,2},{2,3},{3,4},{4,5},{5,6},{6,7},{7,8},{8,9},{9,10},{10,1... | collective-permute-start | bytes 49160 | tf_op jit(solution)/shard_map/ppermute | solution.py:818
  73.0 15.6 %collective-permute-start.5 = (f32[96,128]{1,0:T(8,128)S(1)}, f32[96,128]{1,0:T(8,128)S(1)}, u32[]{:S(2)}, u32[]{:S(2)}) collective-permute-start(f32[96,128]{1,0:T(8,128)S(1)} %get-tuple-element.47), channel_id=1, source_target_pairs={{0,31},{1,0},{2,1},{3,2},{4,3},{5,4},{6,5},{7,6},{8,7},{9,8},{10,9... | collective-permute-start | bytes 147464 | tf_op jit(solution)/shard_map/ppermute | solution.py:818
  88.6 7.5 %copy-start.4 = (bf16[2,256,384]{2,1,0:T(8,128)(2,1)S(1)}, bf16[2,256,384]{2,1,0:T(8,128)(2,1)}, u32[]{:S(2)}) copy-start(bf16[2,256,384]{2,1,0:T(8,128)(2,1)} %constant.29.clone.refs_4_.table_ref) | copy-start | bytes 1179652
  89.0 8.6 %collective-permute-start.6 = (f32[56,128]{1,0:T(8,128)S(1)}, f32[56,128]{1,0:T(8,128)S(1)}, u32[]{:S(2)}, u32[]{:S(2)}) collective-permute-start(f32[56,128]{1,0:T(8,128)S(1)} %get-tuple-element.53), channel_id=1, source_target_pairs={{0,32},{32,64},{64,96},{96,128},{128,160},{160,192},{192,224},{224... | collective-permute-start | bytes 86024 | tf_op jit(solution)/shard_map/ppermute | solution.py:818
  94.2 7.9 %collective-permute-start.7 = (f32[56,128]{1,0:T(8,128)S(1)}, f32[56,128]{1,0:T(8,128)S(1)}, u32[]{:S(2)}, u32[]{:S(2)}) collective-permute-start(f32[56,128]{1,0:T(8,128)S(1)} %get-tuple-element.54), channel_id=1, source_target_pairs={{32,0},{64,32},{96,64},{128,96},{160,128},{192,160},{224,192},{256... | collective-permute-start | bytes 86024 | tf_op jit(solution)/shard_map/ppermute | solution.py:818

commit v6 on v5

--- a/solution.py
+++ b/solution.py
@@ -64,6 +64,11 @@
 
 def own_place():
     return lax.axis_index("band"), 2 * lax.axis_index("z") + lax.axis_index("core")
+
+
+def swap_odd(first, second):
+    even = lax.axis_index("band") % 2 == 0
+    return jnp.where(even, first, second), jnp.where(even, second, first)
 
 
 def to_col(row):
@@ -185,6 +190,8 @@
             out_ref[lines, 256:384] = edge
     west_ref[...] = west
     east_ref[...] = east
+    north, south = north_ref[...], south_ref[...]
+    north_ref[...], south_ref[...] = swap_odd(south, north)
 
 
 def third_tile(tail, left, right, f, cols):
@@ -235,10 +242,11 @@
     devices = cos_ref.shape[0]
     half = devices // 2
     band, lon = own_place()
+    below, above = swap_odd(below_ref[...], above_ref[...])
     for f in range(4):
         ext_ref[f, 0:rows, :] = fields_ref[f]
-        ext_ref[f, rows : rows + HALO, :] = below_ref[HALO * f : HALO * f + HALO, :]
-        ext_ref[f, rows + HALO : ext, :] = above_ref[HALO * f : HALO * f + HALO, :]
+        ext_ref[f, rows : rows + HALO, :] = below[HALO * f : HALO * f + HALO]
+        ext_ref[f, rows + HALO : ext, :] = above[HALO * f : HALO * f + HALO]
     edge = ext_ref[3, rows:ext, 256:384]
     marked = iota(edge.shape, 1) == WEIGHT_LANE
     mask, keep = filter_ref[0:1, :], filter_ref[1:2, :]
@@ -512,6 +520,8 @@
                     at + r : at + r + 1, 128 * t : 128 * t + 128
                 ]
         out_ref[54:56, :] = jnp.zeros((2, 128), F32)
+    north, south = north_ref[...], south_ref[...]
+    north_ref[...], south_ref[...] = swap_odd(south, north)
 
 
 EDGE = 16
@@ -593,8 +603,8 @@
     own_ref,
     inner_ref,
     depx_ref,
-    above_ref,
-    below_ref,
+    second_ref,
+    first_ref,
     terms_ref,
     cos_ref,
     sin_ref,
@@ -608,6 +618,8 @@
     h_ref,
     e_ref,
     n_ref,
+    below_ref,
+    above_ref,
     sems,
 ):
     rows, cols = h_ref.shape
@@ -645,6 +657,7 @@
             f,
             cols,
         )
+    below_ref[...], above_ref[...] = swap_odd(first_ref[...], second_ref[...])
     turn_cos, turn_sin = cos_ref[pl.ds(lon, 1), :], sin_ref[pl.ds(lon, 1), :]
     for f in range(6):
         for at, in_ref in ((8 * f, below_ref), (8 * f + 4, above_ref)):
@@ -817,6 +830,8 @@
         pairs = [(i, (i + shift) % count) for i in range(count) if closed or 0 <= i + shift < count]
         return lax.ppermute(value, axis, pairs)
 
+    even = [(i, i ^ 1) for i in range(bands)]
+    odd = [(i, ((i + 1) ^ 1) - 1) for i in range(1, bands - 1)]
     fields, west, east, north, south, kept, marks = call(
         pack_tile,
         "pack_tile",
@@ -834,7 +849,7 @@
         ),
         direct=range(9),
     )
-    below, above = send(north, "band", -1, False), send(south, "band", 1, False)
+    below, above = lax.ppermute(north, "band", even), lax.ppermute(south, "band", odd)
     right, left = send(west, LON, -1, True), send(east, LON, 1, True)
     near, far, placed = call(
         pack_observations,
@@ -902,7 +917,7 @@
         [(rows, LANES), (56, 128), (56, 128)],
         (everyone, dep, corner_right, kept),
     )
-    below, above = send(north, "band", -1, False), send(south, "band", 1, False)
+    below, above = lax.ppermute(north, "band", even), lax.ppermute(south, "band", odd)
     own, inner = call(
         lambda *refs: own_rows(cols, *refs),
         "own_rows",
@@ -947,6 +962,7 @@
             ),
             scratch=[(48, 256), (edge, LANES), (4, edge, LANES)]
             + [(rows, cols)] * 3
+            + [(56, 128)] * 2
             + [pltpu.SemaphoreType.DMA((3, 3))],
             outside=True,
         )

time: 104 us -> 101 us (0.971)
  waiting for transfers between devices: 15.9 us -> 13.9 us
    ppermute x8 -> x4, starting transfers between devices: 24.4 us -> 11.6 us  [send(): return lax.ppermute(value, axis, pairs)]
    ppermute x0 -> x4, starting transfers between devices: none -> 11.9 us  [the longest x2 8.07 us: on_device(): lax.ppermute(south, 'band', odd)]
    ppermute x8 -> x4, waiting for transfers between devices: 6.14 us -> 1.6 us  [send(): return lax.ppermute(value, axis, pairs)]
    ppermute x0 -> x4, waiting for transfers between devices: none -> 2.43 us  [the longest x2 2.42 us: on_device(): lax.ppermute(north, 'band', even)]
where the time goes in v6:
time: 101 us; the launch traced here: 100 us
  blocking collectives  49.9 us (49%)
  starting transfers between devices  27.2 us (27%)
  waiting for transfers between devices  13.9 us (14%)
  Pallas kernels  8.26 us (8%)
    all_to_all x1, blocking collectives, on_device(): owned = lax.all_to_all(joined, 'z', split_axis=0, concat_axis=0, tiled=True)  45.5 us
    ppermute x4, starting transfers between devices, send(): return lax.ppermute(value, axis, pairs)  11.6 us
    all_to_all x1, waiting for transfers between devices, on_device(): lax.all_to_all(spread, 'z', split_axis=0, concat_axis=0, tiled=True)  9.86 us
    pallas_call x9, Pallas kernels, call(): pl.pallas_call(kernel, name=name, out_shape=shapes, in_specs=specs, out_s...  8.26 us
    ppermute x2, starting transfers between devices, on_device(): lax.ppermute(south, 'band', odd)  8.07 us
    ppermute x2, starting transfers between devices, on_device(): lax.ppermute(north, 'band', even)  3.87 us
    all_to_all x1, starting transfers between devices, on_device(): lax.all_to_all(spread, 'z', split_axis=0, concat_axis=0, tiled=True)  3.62 us
    all_gather x1, blocking collectives, on_device(): swapped = lax.all_gather(other, 'core', axis=0, tiled=False)  2.46 us
  transfers between devices with their start and end apart: 9, of which 4 were waited for; matrix products, arithmetic and copies ran while one was open for 0% of the time, Pallas kernels for 3%

profile of v6, /device:TPU:24, one launch (start us, length us, event | category | flops | bytes accessed | tf_op | source)
XLA Modules:
  0.0 100.2 jit_solution(11247224855308035296)
XLA Ops:
  0.7 1.3 %pack_tile.1 = (f32[4,64,384]{2,1,0:T(8,128)S(1)}, f32[64,128]{1,0:T(8,128)S(1)}, f32[64,128]{1,0:T(8,128)S(1)}, f32[16,384]{1,0:T(8,128)S(1)}, f32[16,384]{1,0:...) custom-call(f32[64,270]{1,0:T(8,128)} %h_hbm.1, f32[64,270]{1,0:T(8,128)} %e_hbm.1, f32[64,270]{1,0:T(8,128)} %n_hbm.1, ...), custom_call_target="tpu_custom_call" | custom-call | flops 1000000000 | bytes 2000000 | tf_op jit(solution)/shard_map/pack_tile/pallas_call | solution.py:788
  2.0 3.1 %collective-permute-start.2 = (f32[16,384]{1,0:T(8,128)S(1)}, f32[16,384]{1,0:T(8,128)S(1)}, u32[]{:S(2)}, u32[]{:S(2)}) collective-permute-start(f32[16,384]{1,0:T(8,128)S(1)} %get-tuple-element.32), channel_id=1, source_target_pairs={{32,64},{64,32},{96,128},{128,96},{160,192},{192,160},{224,256},{2... | collective-permute-start | bytes 73736 | tf_op jit(solution)/shard_map/ppermute | solution.py:852
  5.1 2.0 %collective-permute-start.3 = (f32[16,384]{1,0:T(8,128)S(1)}, f32[16,384]{1,0:T(8,128)S(1)}, u32[]{:S(2)}, u32[]{:S(2)}) collective-permute-start(f32[16,384]{1,0:T(8,128)S(1)} %get-tuple-element.33), channel_id=1, source_target_pairs={{0,32},{32,0},{64,96},{96,64},{128,160},{160,128},{192,224},{224,1... | collective-permute-start | bytes 73736 | tf_op jit(solution)/shard_map/ppermute | solution.py:852
  7.1 8.6 %collective-permute-start.1 = (f32[64,128]{1,0:T(8,128)S(1)}, f32[64,128]{1,0:T(8,128)S(1)}, u32[]{:S(2)}, u32[]{:S(2)}) collective-permute-start(f32[64,128]{1,0:T(8,128)S(1)} %get-tuple-element.31), channel_id=1, source_target_pairs={{0,31},{1,0},{2,1},{3,2},{4,3},{5,4},{6,5},{7,6},{8,7},{9,8},{10,9... | collective-permute-start | bytes 98312 | tf_op jit(solution)/shard_map/ppermute | solution.py:831
  15.8 0.8 pack_observations.1
  16.6 0.7 collective-permute-done.refs_1_.refs_6_.left_ref
  17.3 0.0 collective-permute-done.1.refs_2_.refs_7_.right_ref
  17.3 1.3 %partial_sums.1 = (f32[4,72,384]{2,1,0:T(8,128)S(1)}, f32[72,128]{1,0:T(8,128)S(1)}, f32[32,128]{1,0:T(8,128)S(1)}, f32[32,128]{1,0:T(8,128)S(1)}, f32[16,56,128...) custom-call(f32[4,64,384]{2,1,0:T(8,128)S(1)} %get-tuple-element.29.refs_0_, ...), custom_call_target="tpu_custom_call" | custom-call | flops 1000000000 | bytes 2000000 | tf_op jit(solution)/shard_map/partial_sums/pallas_call | solution.py:788
  18.6 2.5 %all-gather = f32[32,56,128]{2,1,0:T(8,128)S(1)} all-gather(f32[16,56,128]{2,1,0:T(8,128)S(1)} %get-tuple-element.41), channel_id=2, replica_groups=mesh['band'=16,'z'=16,'core'=2] {'core'}, dimensions={0}, use_global_device_ids=true | all-gather | bytes 1376256 | tf_op jit(solution)/shard_map/all_gather | solution.py:883
  21.1 0.1 join.1
  21.3 45.5 %all_to_all.10.in_ref = f32[16,37,2,128]{3,2,1,0:T(2,128)S(1)} all-to-all(f32[16,37,2,128]{3,2,1,0:T(2,128)S(1)} %join.1), channel_id=1, replica_groups=mesh['band'=16,'z'=16,'core'=2] {'z'}, dimensions={0} | all-to-all | bytes 1212416 | tf_op jit(solution)/shard_map/all_to_all | solution.py:887
  66.8 1.2 %own_row.1 = f32[16,3,4,128]{3,2,1,0:T(4,128)} custom-call(f32[16,37,2,128]{3,2,1,0:T(2,128)S(1)} %all_to_all.10.in_ref, f32[8,64]{1,0:T(8,128)S(1)} %get-tuple-element.34.filter_ref.refs_5_.refs_3_.refs_1_, f32[16,256]{1,0:T(8,128)S(1)} %copy-done.9, f32[8,128]{1,0:T(8,128)S(1)} %copy-done.10, bf16[2,256,512]{2,1,0:T(8,128)(2,1)S(1)} %copy-done.3, ...), custom_call_target="tpu_custom_call" | custom-call | flops 1000000000 | bytes 2000000 | tf_op jit(solution)/shard_map/own_row/pallas_call | solution.py:788
  68.0 3.6 %all-to-all-start.1 = ((f32[16,3,4,128]{3,2,1,0:T(4,128)}), f32[16,3,4,128]{3,2,1,0:T(4,128)S(1)}, u32[]{:S(2)}, u32[]{:S(2)}) async-start(f32[16,3,4,128]{3,2,1,0:T(4,128)} %own_row.1), calls=%async_computation.1 | async-start | bytes 196608 | tf_op jit(solution)/shard_map/all_to_all | solution.py:902
  71.7 0.5 unpack_observations.1
  72.2 3.0 %collective-permute-start.5 = (f32[96,128]{1,0:T(8,128)S(1)}, f32[96,128]{1,0:T(8,128)S(1)}, u32[]{:S(2)}, u32[]{:S(2)}) collective-permute-start(f32[96,128]{1,0:T(8,128)S(1)} %get-tuple-element.47), channel_id=1, source_target_pairs={{0,31},{1,0},{2,1},{3,2},{4,3},{5,4},{6,5},{7,6},{8,7},{9,8},{10,9... | collective-permute-start | bytes 147464 | tf_op jit(solution)/shard_map/ppermute | solution.py:831
  75.2 0.9 collective-permute-done.4.corner_left_ref
  76.0 9.9 %all-to-all-done.1 = f32[16,3,4,128]{3,2,1,0:T(4,128)S(1)} async-done(((f32[16,3,4,128]{3,2,1,0:T(4,128)}), f32[16,3,4,128]{3,2,1,0:T(4,128)S(1)}, u32[]{:S(2)}, u32[]{:S(2)}) %all-to-all-start.1) | async-done | bytes 98336 | tf_op jit(solution)/shard_map/all_to_all | solution.py:902
  85.9 1.9 %all-gather.1 = f32[32,3,4,128]{3,2,1,0:T(4,128)S(1)} all-gather(f32[16,3,4,128]{3,2,1,0:T(4,128)S(1)} %all-to-all-done.1), channel_id=3, replica_groups=mesh['band'=16,'z'=16,'core'=2] {'core'}, dimensions={0}, use_global_device_ids=true | all-gather | bytes 294912 | tf_op jit(solution)/shard_map/all_gather | solution.py:903
  87.8 0.4 band_edges.1
  88.2 5.0 %collective-permute-start.6 = (f32[56,128]{1,0:T(8,128)S(1)}, f32[56,128]{1,0:T(8,128)S(1)}, u32[]{:S(2)}, u32[]{:S(2)}) collective-permute-start(f32[56,128]{1,0:T(8,128)S(1)} %get-tuple-element.53), channel_id=1, source_target_pairs={{32,64},{64,32},{96,128},{128,96},{160,192},{192,160},{224,256},{2... | collective-permute-start | bytes 86024 | tf_op jit(solution)/shard_map/ppermute | solution.py:920
  93.3 1.9 %collective-permute-start.7 = (f32[56,128]{1,0:T(8,128)S(1)}, f32[56,128]{1,0:T(8,128)S(1)}, u32[]{:S(2)}, u32[]{:S(2)}) collective-permute-start(f32[56,128]{1,0:T(8,128)S(1)} %get-tuple-element.54), channel_id=1, source_target_pairs={{0,32},{32,0},{64,96},{96,64},{128,160},{160,128},{192,224},{224,1... | collective-permute-start | bytes 86024 | tf_op jit(solution)/shard_map/ppermute | solution.py:920
  95.2 1.4 %own_rows.1 = (f32[384,384]{1,0:T(8,128)S(1)}, f32[3,48,384]{2,1,0:T(8,128)S(1)}) custom-call(f32[2,16,3,4,128]{4,3,2,1,0:T(4,128)S(1)} %bitcast.9, f32[8,64]{1,0:T(8,128)S(1)} %get-tuple-element.34.filter_ref.refs_5_.refs_3_.refs_1_, f32[32,128]{1,0:T(8,128)S(1)} %copy-done.8, f32[32,128]{1,0:T(8,128)S(1)} %copy-done.7, bf16[2,256,384]{2,1,0:T(8,128)(2,1)S(1)} %copy-done.4, ...), custom_call_target="tpu_custom_call" | custom-call | flops 1000000000 | bytes 2000000 | tf_op jit(solution)/shard_map/own_rows/pallas_call | solution.py:788
  96.6 2.4 %collective-permute-done.7.first_ref = f32[56,128]{1,0:T(8,128)S(1)} collective-permute-done((f32[56,128]{1,0:T(8,128)S(1)}, f32[56,128]{1,0:T(8,128)S(1)}, u32[]{:S(2)}, u32[]{:S(2)}) %collective-permute-start.7) | collective-permute-done | bytes 28704 | tf_op jit(solution)/shard_map/ppermute | solution.py:920
  99.0 1.2 %last_stage.1 = (f32[64,270]{1,0:T(8,128)}, f32[64,270]{1,0:T(8,128)}, f32[64,270]{1,0:T(8,128)}) custom-call(f32[4,72,384]{2,1,0:T(8,128)S(1)} %get-tuple-element.39.refs_5_.wide_ref, f32[64,128]{1,0:T(8,128)S(1)} %collective-permute-done.refs_1_.refs_6_.left_ref, f32[64,128]{1,0:T(8,128)S(1)} %collective-permute-done.1.refs_2_.refs_7_.right_ref, ...), custom_call_target="tpu_custom_call" | custom-call | flops 1000000000 | bytes 2000000 | tf_op jit(solution)/shard_map/last_stage/pallas_call | solution.py:788
  (28 shorter events, 0.1 us)
Async XLA Ops:
  0.6 15.1 %copy-start = (f32[128,256]{1,0:T(8,128)S(1)}, f32[128,256]{1,0:T(8,128)}, u32[]{:S(2)}) copy-start(f32[128,256]{1,0:T(8,128)} %values_ref.1) | copy-start | bytes 393220
  0.6 15.1 %copy-start.5 = (bf16[2,384,256]{2,1,0:T(8,128)(2,1)S(1)}, bf16[2,384,256]{2,1,0:T(8,128)(2,1)}, u32[]{:S(2)}) copy-start(bf16[2,384,256]{2,1,0:T(8,128)(2,1)} %constant.22.clone.table_ref.refs_9_) | copy-start | bytes 1179652
  0.7 15.1 %copy-start.7 = (f32[32,128]{1,0:T(8,128)S(1)}, f32[32,128]{1,0:T(8,128)}, u32[]{:S(2)}) copy-start(f32[32,128]{1,0:T(8,128)} %constant.21.clone.sin_ref.refs_8_.refs_3_) | copy-start | bytes 49156
  0.7 15.1 %copy-start.8 = (f32[32,128]{1,0:T(8,128)S(1)}, f32[32,128]{1,0:T(8,128)}, u32[]{:S(2)}) copy-start(f32[32,128]{1,0:T(8,128)} %constant.20.clone.cos_ref.refs_7_.refs_2_) | copy-start | bytes 49156
  2.0 14.6 %collective-permute-start.2 = (f32[16,384]{1,0:T(8,128)S(1)}, f32[16,384]{1,0:T(8,128)S(1)}, u32[]{:S(2)}, u32[]{:S(2)}) collective-permute-start(f32[16,384]{1,0:T(8,128)S(1)} %get-tuple-element.32), channel_id=1, source_target_pairs={{32,64},{64,32},{96,128},{128,96},{160,192},{192,160},{224,256},{2... | collective-permute-start | bytes 73736 | tf_op jit(solution)/shard_map/ppermute | solution.py:852
  5.1 11.5 %collective-permute-start.3 = (f32[16,384]{1,0:T(8,128)S(1)}, f32[16,384]{1,0:T(8,128)S(1)}, u32[]{:S(2)}, u32[]{:S(2)}) collective-permute-start(f32[16,384]{1,0:T(8,128)S(1)} %get-tuple-element.33), channel_id=1, source_target_pairs={{0,32},{32,0},{64,96},{96,64},{128,160},{160,128},{192,224},{224,1... | collective-permute-start | bytes 73736 | tf_op jit(solution)/shard_map/ppermute | solution.py:852
  7.0 10.2 %collective-permute-start = (f32[64,128]{1,0:T(8,128)S(1)}, f32[64,128]{1,0:T(8,128)S(1)}, u32[]{:S(2)}, u32[]{:S(2)}) collective-permute-start(f32[64,128]{1,0:T(8,128)S(1)} %get-tuple-element.30), channel_id=1, source_target_pairs={{0,1},{1,2},{2,3},{3,4},{4,5},{5,6},{6,7},{7,8},{8,9},{9,10},{10,1... | collective-permute-start | bytes 98312 | tf_op jit(solution)/shard_map/ppermute | solution.py:831
  7.1 10.2 %collective-permute-start.1 = (f32[64,128]{1,0:T(8,128)S(1)}, f32[64,128]{1,0:T(8,128)S(1)}, u32[]{:S(2)}, u32[]{:S(2)}) collective-permute-start(f32[64,128]{1,0:T(8,128)S(1)} %get-tuple-element.31), channel_id=1, source_target_pairs={{0,31},{1,0},{2,1},{3,2},{4,3},{5,4},{6,5},{7,6},{8,7},{9,8},{10,9... | collective-permute-start | bytes 98312 | tf_op jit(solution)/shard_map/ppermute | solution.py:831
  15.7 1.6 %copy-start.1 = (bf16[2,384,512]{2,1,0:T(8,128)(2,1)S(1)}, bf16[2,384,512]{2,1,0:T(8,128)(2,1)}, u32[]{:S(2)}) copy-start(bf16[2,384,512]{2,1,0:T(8,128)(2,1)} %constant.24.clone.refs_10_) | copy-start | bytes 2359300
  15.7 1.6 %copy-start.6 = (f32[72,128]{1,0:T(8,128)S(1)}, f32[72,128]{1,0:T(8,128)}, u32[]{:S(2)}) copy-start(f32[72,128]{1,0:T(8,128)} %constant.23.clone.refs_6_.refs_10_.terms_ref) | copy-start | bytes 110596
  21.2 45.6 %copy-start.2 = (bf16[2,512,256]{2,1,0:T(8,128)(2,1)S(1)}, bf16[2,512,256]{2,1,0:T(8,128)(2,1)}, u32[]{:S(2)}) copy-start(bf16[2,512,256]{2,1,0:T(8,128)(2,1)} %constant.28.clone.from_grid_ref) | copy-start | bytes 1572868
  21.2 45.6 %copy-start.3 = (bf16[2,256,512]{2,1,0:T(8,128)(2,1)S(1)}, bf16[2,256,512]{2,1,0:T(8,128)(2,1)}, u32[]{:S(2)}) copy-start(bf16[2,256,512]{2,1,0:T(8,128)(2,1)} %constant.27.clone.to_grid_ref) | copy-start | bytes 1572868
  21.2 45.6 %copy-start.9 = (f32[16,256]{1,0:T(8,128)S(1)}, f32[16,256]{1,0:T(8,128)}, u32[]{:S(2)}) copy-start(f32[16,256]{1,0:T(8,128)} %constant.25.clone.lines_ref) | copy-start | bytes 49156
  21.3 45.6 %copy-start.10 = (f32[8,128]{1,0:T(8,128)S(1)}, f32[8,128]{1,0:T(8,128)}, u32[]{:S(2)}) copy-start(f32[8,128]{1,0:T(8,128)} %constant.26.clone.slope_ref) | copy-start | bytes 12292
  68.0 17.9 %all-to-all-start.1 = ((f32[16,3,4,128]{3,2,1,0:T(4,128)}), f32[16,3,4,128]{3,2,1,0:T(4,128)S(1)}, u32[]{:S(2)}, u32[]{:S(2)}) async-start(f32[16,3,4,128]{3,2,1,0:T(4,128)} %own_row.1), calls=%async_computation.1 | async-start | bytes 196608 | tf_op jit(solution)/shard_map/all_to_all | solution.py:902
  71.6 4.4 %collective-permute-start.4 = (f32[32,128]{1,0:T(8,128)S(1)}, f32[32,128]{1,0:T(8,128)S(1)}, u32[]{:S(2)}, u32[]{:S(2)}) collective-permute-start(f32[32,128]{1,0:T(8,128)S(1)} %get-tuple-element.45), channel_id=1, source_target_pairs={{0,1},{1,2},{2,3},{3,4},{4,5},{5,6},{6,7},{7,8},{8,9},{9,10},{10,1... | collective-permute-start | bytes 49160 | tf_op jit(solution)/shard_map/ppermute | solution.py:831
  72.2 15.6 %collective-permute-start.5 = (f32[96,128]{1,0:T(8,128)S(1)}, f32[96,128]{1,0:T(8,128)S(1)}, u32[]{:S(2)}, u32[]{:S(2)}) collective-permute-start(f32[96,128]{1,0:T(8,128)S(1)} %get-tuple-element.47), channel_id=1, source_target_pairs={{0,31},{1,0},{2,1},{3,2},{4,3},{5,4},{6,5},{7,6},{8,7},{9,8},{10,9... | collective-permute-start | bytes 147464 | tf_op jit(solution)/shard_map/ppermute | solution.py:831
  87.8 7.4 %copy-start.4 = (bf16[2,256,384]{2,1,0:T(8,128)(2,1)S(1)}, bf16[2,256,384]{2,1,0:T(8,128)(2,1)}, u32[]{:S(2)}) copy-start(bf16[2,256,384]{2,1,0:T(8,128)(2,1)} %constant.29.clone.refs_4_.table_ref) | copy-start | bytes 1179652
  88.2 8.4 %collective-permute-start.6 = (f32[56,128]{1,0:T(8,128)S(1)}, f32[56,128]{1,0:T(8,128)S(1)}, u32[]{:S(2)}, u32[]{:S(2)}) collective-permute-start(f32[56,128]{1,0:T(8,128)S(1)} %get-tuple-element.53), channel_id=1, source_target_pairs={{32,64},{64,32},{96,128},{128,96},{160,192},{192,160},{224,256},{2... | collective-permute-start | bytes 86024 | tf_op jit(solution)/shard_map/ppermute | solution.py:920
  93.3 5.8 %collective-permute-start.7 = (f32[56,128]{1,0:T(8,128)S(1)}, f32[56,128]{1,0:T(8,128)S(1)}, u32[]{:S(2)}, u32[]{:S(2)}) collective-permute-start(f32[56,128]{1,0:T(8,128)S(1)} %get-tuple-element.54), channel_id=1, source_target_pairs={{0,32},{32,0},{64,96},{96,64},{128,160},{160,128},{192,224},{224,1... | collective-permute-start | bytes 86024 | tf_op jit(solution)/shard_map/ppermute | solution.py:920

commit v7 on v6

--- a/solution.py
+++ b/solution.py
@@ -191,7 +191,7 @@
     west_ref[...] = west
     east_ref[...] = east
     north, south = north_ref[...], south_ref[...]
-    north_ref[...], south_ref[...] = swap_odd(south, north)
+    north_ref[...], south_ref[...] = swap_odd(north, south)
 
 
 def third_tile(tail, left, right, f, cols):
@@ -521,7 +521,7 @@
                 ]
         out_ref[54:56, :] = jnp.zeros((2, 128), F32)
     north, south = north_ref[...], south_ref[...]
-    north_ref[...], south_ref[...] = swap_odd(south, north)
+    north_ref[...], south_ref[...] = swap_odd(north, south)
 
 
 EDGE = 16
@@ -849,7 +849,7 @@
         ),
         direct=range(9),
     )
-    below, above = lax.ppermute(north, "band", even), lax.ppermute(south, "band", odd)
+    above, below = lax.ppermute(north, "band", odd), lax.ppermute(south, "band", even)
     right, left = send(west, LON, -1, True), send(east, LON, 1, True)
     near, far, placed = call(
         pack_observations,
@@ -917,7 +917,7 @@
         [(rows, LANES), (56, 128), (56, 128)],
         (everyone, dep, corner_right, kept),
     )
-    below, above = lax.ppermute(north, "band", even), lax.ppermute(south, "band", odd)
+    above, below = lax.ppermute(north, "band", odd), lax.ppermute(south, "band", even)
     own, inner = call(
         lambda *refs: own_rows(cols, *refs),
         "own_rows",

time: 101 us -> 101 us (level)
  no operation moved by 1% of the time
where the time goes in v7:
time: 101 us; the launch traced here: 100 us
  blocking collectives  49.9 us (49%)
  starting transfers between devices  27.2 us (27%)
  waiting for transfers between devices  13.9 us (14%)
  Pallas kernels  8.26 us (8%)
    all_to_all x1, blocking collectives, on_device(): owned = lax.all_to_all(joined, 'z', split_axis=0, concat_axis=0, tiled=True)  45.5 us
    ppermute x4, starting transfers between devices, send(): return lax.ppermute(value, axis, pairs)  11.6 us
    all_to_all x1, waiting for transfers between devices, on_device(): lax.all_to_all(spread, 'z', split_axis=0, concat_axis=0, tiled=True)  9.86 us
    pallas_call x9, Pallas kernels, call(): pl.pallas_call(kernel, name=name, out_shape=shapes, in_specs=specs, out_s...  8.26 us
    ppermute x2, starting transfers between devices, on_device(): lax.ppermute(north, 'band', odd)  8.07 us
    ppermute x2, starting transfers between devices, on_device(): lax.ppermute(south, 'band', even)  3.87 us
    all_to_all x1, starting transfers between devices, on_device(): lax.all_to_all(spread, 'z', split_axis=0, concat_axis=0, tiled=True)  3.62 us
    all_gather x1, blocking collectives, on_device(): swapped = lax.all_gather(other, 'core', axis=0, tiled=False)  2.46 us
  transfers between devices with their start and end apart: 9, of which 4 were waited for; matrix products, arithmetic and copies ran while one was open for 0% of the time, Pallas kernels for 3%

profile of v7, /device:TPU:24, one launch (start us, length us, event | category | flops | bytes accessed | tf_op | source)
XLA Modules:
  0.0 100.2 jit_solution(12929635516548232979)
XLA Ops:
  0.7 1.3 %pack_tile.1 = (f32[4,64,384]{2,1,0:T(8,128)S(1)}, f32[64,128]{1,0:T(8,128)S(1)}, f32[64,128]{1,0:T(8,128)S(1)}, f32[16,384]{1,0:T(8,128)S(1)}, f32[16,384]{1,0:...) custom-call(f32[64,270]{1,0:T(8,128)} %h_hbm.1, f32[64,270]{1,0:T(8,128)} %e_hbm.1, f32[64,270]{1,0:T(8,128)} %n_hbm.1, ...), custom_call_target="tpu_custom_call" | custom-call | flops 1000000000 | bytes 2000000 | tf_op jit(solution)/shard_map/pack_tile/pallas_call | solution.py:788
  2.0 3.1 %collective-permute-start.2 = (f32[16,384]{1,0:T(8,128)S(1)}, f32[16,384]{1,0:T(8,128)S(1)}, u32[]{:S(2)}, u32[]{:S(2)}) collective-permute-start(f32[16,384]{1,0:T(8,128)S(1)} %get-tuple-element.32), channel_id=1, source_target_pairs={{32,64},{64,32},{96,128},{128,96},{160,192},{192,160},{224,256},{2... | collective-permute-start | bytes 73736 | tf_op jit(solution)/shard_map/ppermute | solution.py:852
  5.1 2.0 %collective-permute-start.3 = (f32[16,384]{1,0:T(8,128)S(1)}, f32[16,384]{1,0:T(8,128)S(1)}, u32[]{:S(2)}, u32[]{:S(2)}) collective-permute-start(f32[16,384]{1,0:T(8,128)S(1)} %get-tuple-element.33), channel_id=1, source_target_pairs={{0,32},{32,0},{64,96},{96,64},{128,160},{160,128},{192,224},{224,1... | collective-permute-start | bytes 73736 | tf_op jit(solution)/shard_map/ppermute | solution.py:852
  7.1 8.6 %collective-permute-start.1 = (f32[64,128]{1,0:T(8,128)S(1)}, f32[64,128]{1,0:T(8,128)S(1)}, u32[]{:S(2)}, u32[]{:S(2)}) collective-permute-start(f32[64,128]{1,0:T(8,128)S(1)} %get-tuple-element.31), channel_id=1, source_target_pairs={{0,31},{1,0},{2,1},{3,2},{4,3},{5,4},{6,5},{7,6},{8,7},{9,8},{10,9... | collective-permute-start | bytes 98312 | tf_op jit(solution)/shard_map/ppermute | solution.py:831
  15.8 0.8 pack_observations.1
  16.6 0.7 collective-permute-done.refs_1_.refs_6_.left_ref
  17.3 0.0 collective-permute-done.1.refs_2_.refs_7_.right_ref
  17.3 1.3 %partial_sums.1 = (f32[4,72,384]{2,1,0:T(8,128)S(1)}, f32[72,128]{1,0:T(8,128)S(1)}, f32[32,128]{1,0:T(8,128)S(1)}, f32[32,128]{1,0:T(8,128)S(1)}, f32[16,56,128...) custom-call(f32[4,64,384]{2,1,0:T(8,128)S(1)} %get-tuple-element.29.refs_0_, ...), custom_call_target="tpu_custom_call" | custom-call | flops 1000000000 | bytes 2000000 | tf_op jit(solution)/shard_map/partial_sums/pallas_call | solution.py:788
  18.6 2.5 %all-gather = f32[32,56,128]{2,1,0:T(8,128)S(1)} all-gather(f32[16,56,128]{2,1,0:T(8,128)S(1)} %get-tuple-element.41), channel_id=2, replica_groups=mesh['band'=16,'z'=16,'core'=2] {'core'}, dimensions={0}, use_global_device_ids=true | all-gather | bytes 1376256 | tf_op jit(solution)/shard_map/all_gather | solution.py:883
  21.1 0.1 join.1
  21.3 45.5 %all_to_all.10.in_ref = f32[16,37,2,128]{3,2,1,0:T(2,128)S(1)} all-to-all(f32[16,37,2,128]{3,2,1,0:T(2,128)S(1)} %join.1), channel_id=1, replica_groups=mesh['band'=16,'z'=16,'core'=2] {'z'}, dimensions={0} | all-to-all | bytes 1212416 | tf_op jit(solution)/shard_map/all_to_all | solution.py:887
  66.8 1.2 %own_row.1 = f32[16,3,4,128]{3,2,1,0:T(4,128)} custom-call(f32[16,37,2,128]{3,2,1,0:T(2,128)S(1)} %all_to_all.10.in_ref, f32[8,64]{1,0:T(8,128)S(1)} %get-tuple-element.34.filter_ref.refs_5_.refs_3_.refs_1_, f32[16,256]{1,0:T(8,128)S(1)} %copy-done.9, f32[8,128]{1,0:T(8,128)S(1)} %copy-done.10, bf16[2,256,512]{2,1,0:T(8,128)(2,1)S(1)} %copy-done.3, ...), custom_call_target="tpu_custom_call" | custom-call | flops 1000000000 | bytes 2000000 | tf_op jit(solution)/shard_map/own_row/pallas_call | solution.py:788
  68.0 3.6 %all-to-all-start.1 = ((f32[16,3,4,128]{3,2,1,0:T(4,128)}), f32[16,3,4,128]{3,2,1,0:T(4,128)S(1)}, u32[]{:S(2)}, u32[]{:S(2)}) async-start(f32[16,3,4,128]{3,2,1,0:T(4,128)} %own_row.1), calls=%async_computation.1 | async-start | bytes 196608 | tf_op jit(solution)/shard_map/all_to_all | solution.py:902
  71.7 0.5 unpack_observations.1
  72.2 3.0 %collective-permute-start.5 = (f32[96,128]{1,0:T(8,128)S(1)}, f32[96,128]{1,0:T(8,128)S(1)}, u32[]{:S(2)}, u32[]{:S(2)}) collective-permute-start(f32[96,128]{1,0:T(8,128)S(1)} %get-tuple-element.47), channel_id=1, source_target_pairs={{0,31},{1,0},{2,1},{3,2},{4,3},{5,4},{6,5},{7,6},{8,7},{9,8},{10,9... | collective-permute-start | bytes 147464 | tf_op jit(solution)/shard_map/ppermute | solution.py:831
  75.2 0.9 collective-permute-done.4.corner_left_ref
  76.0 9.9 %all-to-all-done.1 = f32[16,3,4,128]{3,2,1,0:T(4,128)S(1)} async-done(((f32[16,3,4,128]{3,2,1,0:T(4,128)}), f32[16,3,4,128]{3,2,1,0:T(4,128)S(1)}, u32[]{:S(2)}, u32[]{:S(2)}) %all-to-all-start.1) | async-done | bytes 98336 | tf_op jit(solution)/shard_map/all_to_all | solution.py:902
  85.9 1.9 %all-gather.1 = f32[32,3,4,128]{3,2,1,0:T(4,128)S(1)} all-gather(f32[16,3,4,128]{3,2,1,0:T(4,128)S(1)} %all-to-all-done.1), channel_id=3, replica_groups=mesh['band'=16,'z'=16,'core'=2] {'core'}, dimensions={0}, use_global_device_ids=true | all-gather | bytes 294912 | tf_op jit(solution)/shard_map/all_gather | solution.py:903
  87.8 0.4 band_edges.1
  88.2 5.0 %collective-permute-start.6 = (f32[56,128]{1,0:T(8,128)S(1)}, f32[56,128]{1,0:T(8,128)S(1)}, u32[]{:S(2)}, u32[]{:S(2)}) collective-permute-start(f32[56,128]{1,0:T(8,128)S(1)} %get-tuple-element.53), channel_id=1, source_target_pairs={{32,64},{64,32},{96,128},{128,96},{160,192},{192,160},{224,256},{2... | collective-permute-start | bytes 86024 | tf_op jit(solution)/shard_map/ppermute | solution.py:920
  93.3 1.9 %collective-permute-start.7 = (f32[56,128]{1,0:T(8,128)S(1)}, f32[56,128]{1,0:T(8,128)S(1)}, u32[]{:S(2)}, u32[]{:S(2)}) collective-permute-start(f32[56,128]{1,0:T(8,128)S(1)} %get-tuple-element.54), channel_id=1, source_target_pairs={{0,32},{32,0},{64,96},{96,64},{128,160},{160,128},{192,224},{224,1... | collective-permute-start | bytes 86024 | tf_op jit(solution)/shard_map/ppermute | solution.py:920
  95.2 1.4 %own_rows.1 = (f32[384,384]{1,0:T(8,128)S(1)}, f32[3,48,384]{2,1,0:T(8,128)S(1)}) custom-call(f32[2,16,3,4,128]{4,3,2,1,0:T(4,128)S(1)} %bitcast.9, f32[8,64]{1,0:T(8,128)S(1)} %get-tuple-element.34.filter_ref.refs_5_.refs_3_.refs_1_, f32[32,128]{1,0:T(8,128)S(1)} %copy-done.8, f32[32,128]{1,0:T(8,128)S(1)} %copy-done.7, bf16[2,256,384]{2,1,0:T(8,128)(2,1)S(1)} %copy-done.4, ...), custom_call_target="tpu_custom_call" | custom-call | flops 1000000000 | bytes 2000000 | tf_op jit(solution)/shard_map/own_rows/pallas_call | solution.py:788
  96.6 2.4 %collective-permute-done.7.first_ref = f32[56,128]{1,0:T(8,128)S(1)} collective-permute-done((f32[56,128]{1,0:T(8,128)S(1)}, f32[56,128]{1,0:T(8,128)S(1)}, u32[]{:S(2)}, u32[]{:S(2)}) %collective-permute-start.7) | collective-permute-done | bytes 28704 | tf_op jit(solution)/shard_map/ppermute | solution.py:920
  99.0 1.2 %last_stage.1 = (f32[64,270]{1,0:T(8,128)}, f32[64,270]{1,0:T(8,128)}, f32[64,270]{1,0:T(8,128)}) custom-call(f32[4,72,384]{2,1,0:T(8,128)S(1)} %get-tuple-element.39.refs_5_.wide_ref, f32[64,128]{1,0:T(8,128)S(1)} %collective-permute-done.refs_1_.refs_6_.left_ref, f32[64,128]{1,0:T(8,128)S(1)} %collective-permute-done.1.refs_2_.refs_7_.right_ref, ...), custom_call_target="tpu_custom_call" | custom-call | flops 1000000000 | bytes 2000000 | tf_op jit(solution)/shard_map/last_stage/pallas_call | solution.py:788
  (28 shorter events, 0.1 us)
Async XLA Ops:
  0.6 15.1 %copy-start = (f32[128,256]{1,0:T(8,128)S(1)}, f32[128,256]{1,0:T(8,128)}, u32[]{:S(2)}) copy-start(f32[128,256]{1,0:T(8,128)} %values_ref.1) | copy-start | bytes 393220
  0.6 15.1 %copy-start.5 = (bf16[2,384,256]{2,1,0:T(8,128)(2,1)S(1)}, bf16[2,384,256]{2,1,0:T(8,128)(2,1)}, u32[]{:S(2)}) copy-start(bf16[2,384,256]{2,1,0:T(8,128)(2,1)} %constant.22.clone.table_ref.refs_9_) | copy-start | bytes 1179652
  0.7 15.1 %copy-start.7 = (f32[32,128]{1,0:T(8,128)S(1)}, f32[32,128]{1,0:T(8,128)}, u32[]{:S(2)}) copy-start(f32[32,128]{1,0:T(8,128)} %constant.21.clone.sin_ref.refs_8_.refs_3_) | copy-start | bytes 49156
  0.7 15.1 %copy-start.8 = (f32[32,128]{1,0:T(8,128)S(1)}, f32[32,128]{1,0:T(8,128)}, u32[]{:S(2)}) copy-start(f32[32,128]{1,0:T(8,128)} %constant.20.clone.cos_ref.refs_7_.refs_2_) | copy-start | bytes 49156
  2.0 14.6 %collective-permute-start.2 = (f32[16,384]{1,0:T(8,128)S(1)}, f32[16,384]{1,0:T(8,128)S(1)}, u32[]{:S(2)}, u32[]{:S(2)}) collective-permute-start(f32[16,384]{1,0:T(8,128)S(1)} %get-tuple-element.32), channel_id=1, source_target_pairs={{32,64},{64,32},{96,128},{128,96},{160,192},{192,160},{224,256},{2... | collective-permute-start | bytes 73736 | tf_op jit(solution)/shard_map/ppermute | solution.py:852
  5.1 11.5 %collective-permute-start.3 = (f32[16,384]{1,0:T(8,128)S(1)}, f32[16,384]{1,0:T(8,128)S(1)}, u32[]{:S(2)}, u32[]{:S(2)}) collective-permute-start(f32[16,384]{1,0:T(8,128)S(1)} %get-tuple-element.33), channel_id=1, source_target_pairs={{0,32},{32,0},{64,96},{96,64},{128,160},{160,128},{192,224},{224,1... | collective-permute-start | bytes 73736 | tf_op jit(solution)/shard_map/ppermute | solution.py:852
  7.1 10.2 %collective-permute-start = (f32[64,128]{1,0:T(8,128)S(1)}, f32[64,128]{1,0:T(8,128)S(1)}, u32[]{:S(2)}, u32[]{:S(2)}) collective-permute-start(f32[64,128]{1,0:T(8,128)S(1)} %get-tuple-element.30), channel_id=1, source_target_pairs={{0,1},{1,2},{2,3},{3,4},{4,5},{5,6},{6,7},{7,8},{8,9},{9,10},{10,1... | collective-permute-start | bytes 98312 | tf_op jit(solution)/shard_map/ppermute | solution.py:831
  7.1 10.2 %collective-permute-start.1 = (f32[64,128]{1,0:T(8,128)S(1)}, f32[64,128]{1,0:T(8,128)S(1)}, u32[]{:S(2)}, u32[]{:S(2)}) collective-permute-start(f32[64,128]{1,0:T(8,128)S(1)} %get-tuple-element.31), channel_id=1, source_target_pairs={{0,31},{1,0},{2,1},{3,2},{4,3},{5,4},{6,5},{7,6},{8,7},{9,8},{10,9... | collective-permute-start | bytes 98312 | tf_op jit(solution)/shard_map/ppermute | solution.py:831
  15.7 1.6 %copy-start.1 = (bf16[2,384,512]{2,1,0:T(8,128)(2,1)S(1)}, bf16[2,384,512]{2,1,0:T(8,128)(2,1)}, u32[]{:S(2)}) copy-start(bf16[2,384,512]{2,1,0:T(8,128)(2,1)} %constant.24.clone.refs_10_) | copy-start | bytes 2359300
  15.7 1.6 %copy-start.6 = (f32[72,128]{1,0:T(8,128)S(1)}, f32[72,128]{1,0:T(8,128)}, u32[]{:S(2)}) copy-start(f32[72,128]{1,0:T(8,128)} %constant.23.clone.refs_6_.refs_10_.terms_ref) | copy-start | bytes 110596
  21.2 45.6 %copy-start.2 = (bf16[2,512,256]{2,1,0:T(8,128)(2,1)S(1)}, bf16[2,512,256]{2,1,0:T(8,128)(2,1)}, u32[]{:S(2)}) copy-start(bf16[2,512,256]{2,1,0:T(8,128)(2,1)} %constant.28.clone.from_grid_ref) | copy-start | bytes 1572868
  21.2 45.6 %copy-start.3 = (bf16[2,256,512]{2,1,0:T(8,128)(2,1)S(1)}, bf16[2,256,512]{2,1,0:T(8,128)(2,1)}, u32[]{:S(2)}) copy-start(bf16[2,256,512]{2,1,0:T(8,128)(2,1)} %constant.27.clone.to_grid_ref) | copy-start | bytes 1572868
  21.3 45.6 %copy-start.9 = (f32[16,256]{1,0:T(8,128)S(1)}, f32[16,256]{1,0:T(8,128)}, u32[]{:S(2)}) copy-start(f32[16,256]{1,0:T(8,128)} %constant.25.clone.lines_ref) | copy-start | bytes 49156
  21.3 45.6 %copy-start.10 = (f32[8,128]{1,0:T(8,128)S(1)}, f32[8,128]{1,0:T(8,128)}, u32[]{:S(2)}) copy-start(f32[8,128]{1,0:T(8,128)} %constant.26.clone.slope_ref) | copy-start | bytes 12292
  68.0 17.9 %all-to-all-start.1 = ((f32[16,3,4,128]{3,2,1,0:T(4,128)}), f32[16,3,4,128]{3,2,1,0:T(4,128)S(1)}, u32[]{:S(2)}, u32[]{:S(2)}) async-start(f32[16,3,4,128]{3,2,1,0:T(4,128)} %own_row.1), calls=%async_computation.1 | async-start | bytes 196608 | tf_op jit(solution)/shard_map/all_to_all | solution.py:902
  71.6 4.4 %collective-permute-start.4 = (f32[32,128]{1,0:T(8,128)S(1)}, f32[32,128]{1,0:T(8,128)S(1)}, u32[]{:S(2)}, u32[]{:S(2)}) collective-permute-start(f32[32,128]{1,0:T(8,128)S(1)} %get-tuple-element.45), channel_id=1, source_target_pairs={{0,1},{1,2},{2,3},{3,4},{4,5},{5,6},{6,7},{7,8},{8,9},{9,10},{10,1... | collective-permute-start | bytes 49160 | tf_op jit(solution)/shard_map/ppermute | solution.py:831
  72.2 15.6 %collective-permute-start.5 = (f32[96,128]{1,0:T(8,128)S(1)}, f32[96,128]{1,0:T(8,128)S(1)}, u32[]{:S(2)}, u32[]{:S(2)}) collective-permute-start(f32[96,128]{1,0:T(8,128)S(1)} %get-tuple-element.47), channel_id=1, source_target_pairs={{0,31},{1,0},{2,1},{3,2},{4,3},{5,4},{6,5},{7,6},{8,7},{9,8},{10,9... | collective-permute-start | bytes 147464 | tf_op jit(solution)/shard_map/ppermute | solution.py:831
  87.8 7.4 %copy-start.4 = (bf16[2,256,384]{2,1,0:T(8,128)(2,1)S(1)}, bf16[2,256,384]{2,1,0:T(8,128)(2,1)}, u32[]{:S(2)}) copy-start(bf16[2,256,384]{2,1,0:T(8,128)(2,1)} %constant.29.clone.refs_4_.table_ref) | copy-start | bytes 1179652
  88.2 8.4 %collective-permute-start.6 = (f32[56,128]{1,0:T(8,128)S(1)}, f32[56,128]{1,0:T(8,128)S(1)}, u32[]{:S(2)}, u32[]{:S(2)}) collective-permute-start(f32[56,128]{1,0:T(8,128)S(1)} %get-tuple-element.53), channel_id=1, source_target_pairs={{32,64},{64,32},{96,128},{128,96},{160,192},{192,160},{224,256},{2... | collective-permute-start | bytes 86024 | tf_op jit(solution)/shard_map/ppermute | solution.py:920
  93.3 5.8 %collective-permute-start.7 = (f32[56,128]{1,0:T(8,128)S(1)}, f32[56,128]{1,0:T(8,128)S(1)}, u32[]{:S(2)}, u32[]{:S(2)}) collective-permute-start(f32[56,128]{1,0:T(8,128)S(1)} %get-tuple-element.54), channel_id=1, source_target_pairs={{0,32},{32,0},{64,96},{96,64},{128,160},{160,128},{192,224},{224,1... | collective-permute-start | bytes 86024 | tf_op jit(solution)/shard_map/ppermute | solution.py:920

commit v8 on v6

--- a/solution.py
+++ b/solution.py
@@ -69,6 +69,11 @@
 def swap_odd(first, second):
     even = lax.axis_index("band") % 2 == 0
     return jnp.where(even, first, second), jnp.where(even, second, first)
+
+
+def swap_cores(first, second):
+    zero = lax.axis_index("core") == 0
+    return jnp.where(zero, first, second), jnp.where(zero, second, first)
 
 
 def to_col(row):
@@ -188,8 +193,7 @@
                 edge = jnp.where(iota(edge.shape, 1) == WEIGHT_LANE, weight[span, :], edge)
             out_ref[lines, 0:256] = fields_ref[f, span, 0:256]
             out_ref[lines, 256:384] = edge
-    west_ref[...] = west
-    east_ref[...] = east
+    west_ref[...], east_ref[...] = swap_cores(west, east)
     north, south = north_ref[...], south_ref[...]
     north_ref[...], south_ref[...] = swap_odd(south, north)
 
@@ -214,8 +218,8 @@
 def partial_sums(
     cols,
     fields_ref,
-    left_ref,
-    right_ref,
+    outer_ref,
+    inner_ref,
     above_ref,
     below_ref,
     filter_ref,
@@ -227,6 +231,8 @@
     placed_ref,
     near_ref,
     far_ref,
+    left_ref,
+    right_ref,
     ext_ref,
     weight_ref,
     west_ref,
@@ -242,6 +248,7 @@
     devices = cos_ref.shape[0]
     half = devices // 2
     band, lon = own_place()
+    left_ref[...], right_ref[...] = swap_cores(outer_ref[...], inner_ref[...])
     below, above = swap_odd(below_ref[...], above_ref[...])
     for f in range(4):
         ext_ref[f, 0:rows, :] = fields_ref[f]
@@ -850,7 +857,9 @@
         direct=range(9),
     )
     below, above = lax.ppermute(north, "band", even), lax.ppermute(south, "band", odd)
-    right, left = send(west, LON, -1, True), send(east, LON, 1, True)
+    across = [(i, (i + 1 if i % 2 else i - 1) % devices) for i in range(devices)]
+    within = [(i, i ^ 1) for i in range(devices)]
+    outer, inner = lax.ppermute(west, LON, across), lax.ppermute(east, LON, within)
     near, far, placed = call(
         pack_observations,
         "pack_observations",
@@ -858,14 +867,14 @@
         (obs_values, marks, kept, made["cos"], made["sin"], made["analyse"]),
         cost=3.0,
     )
-    wide, weight, corner_west, corner_east, mine, other = call(
+    left, right, wide, weight, corner_west, corner_east, mine, other = call(
         lambda *refs: partial_sums(cols, *refs),
         "partial_sums",
-        [(4, ext, LANES), (ext, 128)] + [(8 * HALO, 128)] * 2 + [(half, 56, 128)] * 2,
+        [(rows, 128)] * 2 + [(4, ext, LANES), (ext, 128)] + [(8 * HALO, 128)] * 2 + [(half, 56, 128)] * 2,
         (
             fields,
-            left,
-            right,
+            outer,
+            inner,
             above,
             below,
             kept,

time: 101 us -> 102 us (level)
  starting transfers between devices: 27.2 us -> 31 us
  blocking collectives: 49.9 us -> 47.9 us
    ppermute x0 -> x2, starting transfers between devices: none -> 12.5 us  [the longest x1 10.5 us: on_device(): lax.ppermute(west, LON, across)]
    ppermute x4 -> x2, starting transfers between devices: 11.6 us -> 2.97 us  [send(): return lax.ppermute(value, axis, pairs)]
    all_to_all x1, blocking collectives: 45.5 us -> 43.4 us  [on_device(): owned = lax.all_to_all(joined, 'z', split_axis=0, concat_axis=0, tiled=True)]
where the time goes in v8:
time: 102 us
  blocking collectives  47.9 us (47%)
  starting transfers between devices  31 us (30%)
  waiting for transfers between devices  13.4 us (13%)
  Pallas kernels  8.27 us (8%)
    all_to_all x1, blocking collectives, on_device(): owned = lax.all_to_all(joined, 'z', split_axis=0, concat_axis=0, tiled=True)  43.4 us
    ppermute x1, starting transfers between devices, on_device(): lax.ppermute(west, LON, across)  10.5 us
    all_to_all x1, waiting for transfers between devices, on_device(): lax.all_to_all(spread, 'z', split_axis=0, concat_axis=0, tiled=True)  9.81 us
    pallas_call x9, Pallas kernels, call(): pl.pallas_call(kernel, name=name, out_shape=shapes, in_specs=specs, out_s...  8.27 us
    ppermute x2, starting transfers between devices, on_device(): lax.ppermute(south, 'band', odd)  8.07 us
    ppermute x2, starting transfers between devices, on_device(): lax.ppermute(north, 'band', even)  3.87 us
    all_to_all x1, starting transfers between devices, on_device(): lax.all_to_all(spread, 'z', split_axis=0, concat_axis=0, tiled=True)  3.66 us
    ppermute x2, starting transfers between devices, send(): return lax.ppermute(value, axis, pairs)  2.97 us
  transfers between devices with their start and end apart: 9, of which 4 were waited for; matrix products, arithmetic and copies ran while one was open for 0% of the time, Pallas kernels for 3%

profile of v8, /device:TPU:24, one launch (start us, length us, event | category | flops | bytes accessed | tf_op | source)
XLA Modules:
  0.0 101.5 jit_solution(11008369275938178110)
XLA Ops:
  0.7 1.3 %pack_tile.1 = (f32[4,64,384]{2,1,0:T(8,128)S(1)}, f32[64,128]{1,0:T(8,128)S(1)}, f32[64,128]{1,0:T(8,128)S(1)}, f32[16,384]{1,0:T(8,128)S(1)}, f32[16,384]{1,0:...) custom-call(f32[64,270]{1,0:T(8,128)} %h_hbm.1, f32[64,270]{1,0:T(8,128)} %e_hbm.1, f32[64,270]{1,0:T(8,128)} %n_hbm.1, ...), custom_call_target="tpu_custom_call" | custom-call | flops 1000000000 | bytes 2000000 | tf_op jit(solution)/shard_map/pack_tile/pallas_call | solution.py:795
  2.0 3.1 %collective-permute-start.2 = (f32[16,384]{1,0:T(8,128)S(1)}, f32[16,384]{1,0:T(8,128)S(1)}, u32[]{:S(2)}, u32[]{:S(2)}) collective-permute-start(f32[16,384]{1,0:T(8,128)S(1)} %get-tuple-element.34), channel_id=1, source_target_pairs={{32,64},{64,32},{96,128},{128,96},{160,192},{192,160},{224,256},{2... | collective-permute-start | bytes 73736 | tf_op jit(solution)/shard_map/ppermute | solution.py:859
  5.1 2.0 %collective-permute-start.3 = (f32[16,384]{1,0:T(8,128)S(1)}, f32[16,384]{1,0:T(8,128)S(1)}, u32[]{:S(2)}, u32[]{:S(2)}) collective-permute-start(f32[16,384]{1,0:T(8,128)S(1)} %get-tuple-element.35), channel_id=1, source_target_pairs={{0,32},{32,0},{64,96},{96,64},{128,160},{160,128},{192,224},{224,1... | collective-permute-start | bytes 73736 | tf_op jit(solution)/shard_map/ppermute | solution.py:859
  7.1 10.5 %collective-permute-start = (f32[64,128]{1,0:T(8,128)S(1)}, f32[64,128]{1,0:T(8,128)S(1)}, u32[]{:S(2)}, u32[]{:S(2)}) collective-permute-start(f32[64,128]{1,0:T(8,128)S(1)} %get-tuple-element.32), channel_id=1, source_target_pairs={{0,31},{1,2},{2,1},{3,4},{4,3},{5,6},{6,5},{7,8},{8,7},{9,10},{10,... | collective-permute-start | bytes 98312 | tf_op jit(solution)/shard_map/ppermute | solution.py:862
  17.6 1.9 %collective-permute-start.1 = (f32[64,128]{1,0:T(8,128)S(1)}, f32[64,128]{1,0:T(8,128)S(1)}, u32[]{:S(2)}, u32[]{:S(2)}) collective-permute-start(f32[64,128]{1,0:T(8,128)S(1)} %get-tuple-element.33), channel_id=1, source_target_pairs={{0,1},{1,0},{2,3},{3,2},{4,5},{5,4},{6,7},{7,6},{8,9},{9,8},{10,11... | collective-permute-start | bytes 98312 | tf_op jit(solution)/shard_map/ppermute | solution.py:862
  19.6 0.8 pack_observations.1
  20.4 0.3 collective-permute-done.1.refs_2_
  20.7 1.3 %partial_sums.1 = (f32[64,128]{1,0:T(8,128)S(1)}, f32[64,128]{1,0:T(8,128)S(1)}, f32[4,72,384]{2,1,0:T(8,128)S(1)}, f32[72,128]{1,0:T(8,128)S(1)}, f32[32,128]{1...) custom-call(f32[4,64,384]{2,1,0:T(8,128)S(1)} %get-tuple-element.31.refs_0_, ...), custom_call_target="tpu_custom_call" | custom-call | flops 1000000000 | bytes 2000000 | tf_op jit(solution)/shard_map/partial_sums/pallas_call | solution.py:795
  22.0 2.6 %all-gather = f32[32,56,128]{2,1,0:T(8,128)S(1)} all-gather(f32[16,56,128]{2,1,0:T(8,128)S(1)} %get-tuple-element.45), channel_id=2, replica_groups=mesh['band'=16,'z'=16,'core'=2] {'core'}, dimensions={0}, use_global_device_ids=true | all-gather | bytes 1376256 | tf_op jit(solution)/shard_map/all_gather | solution.py:892
  24.6 0.1 join.1
  24.8 43.4 %all_to_all.10.in_ref = f32[16,37,2,128]{3,2,1,0:T(2,128)S(1)} all-to-all(f32[16,37,2,128]{3,2,1,0:T(2,128)S(1)} %join.1), channel_id=1, replica_groups=mesh['band'=16,'z'=16,'core'=2] {'z'}, dimensions={0} | all-to-all | bytes 1212416 | tf_op jit(solution)/shard_map/all_to_all | solution.py:896
  68.2 1.2 %own_row.1 = f32[16,3,4,128]{3,2,1,0:T(4,128)} custom-call(f32[16,37,2,128]{3,2,1,0:T(2,128)S(1)} %all_to_all.10.in_ref, f32[8,64]{1,0:T(8,128)S(1)} %get-tuple-element.36.filter_ref.refs_5_.refs_3_.refs_1_, f32[16,256]{1,0:T(8,128)S(1)} %copy-done.9, f32[8,128]{1,0:T(8,128)S(1)} %copy-done.10, bf16[2,256,512]{2,1,0:T(8,128)(2,1)S(1)} %copy-done.3, ...), custom_call_target="tpu_custom_call" | custom-call | flops 1000000000 | bytes 2000000 | tf_op jit(solution)/shard_map/own_row/pallas_call | solution.py:795
  69.3 3.7 %all-to-all-start.1 = ((f32[16,3,4,128]{3,2,1,0:T(4,128)}), f32[16,3,4,128]{3,2,1,0:T(4,128)S(1)}, u32[]{:S(2)}, u32[]{:S(2)}) async-start(f32[16,3,4,128]{3,2,1,0:T(4,128)} %own_row.1), calls=%async_computation.1 | async-start | bytes 196608 | tf_op jit(solution)/shard_map/all_to_all | solution.py:911
  73.0 0.5 unpack_observations.1
  73.5 3.0 %collective-permute-start.5 = (f32[96,128]{1,0:T(8,128)S(1)}, f32[96,128]{1,0:T(8,128)S(1)}, u32[]{:S(2)}, u32[]{:S(2)}) collective-permute-start(f32[96,128]{1,0:T(8,128)S(1)} %get-tuple-element.51), channel_id=1, source_target_pairs={{0,31},{1,0},{2,1},{3,2},{4,3},{5,4},{6,5},{7,6},{8,7},{9,8},{10,9... | collective-permute-start | bytes 147464 | tf_op jit(solution)/shard_map/ppermute | solution.py:838
  76.5 0.9 collective-permute-done.4.corner_left_ref
  77.4 9.8 %all-to-all-done.1 = f32[16,3,4,128]{3,2,1,0:T(4,128)S(1)} async-done(((f32[16,3,4,128]{3,2,1,0:T(4,128)}), f32[16,3,4,128]{3,2,1,0:T(4,128)S(1)}, u32[]{:S(2)}, u32[]{:S(2)}) %all-to-all-start.1) | async-done | bytes 98336 | tf_op jit(solution)/shard_map/all_to_all | solution.py:911
  87.2 1.9 %all-gather.1 = f32[32,3,4,128]{3,2,1,0:T(4,128)S(1)} all-gather(f32[16,3,4,128]{3,2,1,0:T(4,128)S(1)} %all-to-all-done.1), channel_id=3, replica_groups=mesh['band'=16,'z'=16,'core'=2] {'core'}, dimensions={0}, use_global_device_ids=true | all-gather | bytes 294912 | tf_op jit(solution)/shard_map/all_gather | solution.py:912
  89.1 0.4 band_edges.1
  89.5 5.0 %collective-permute-start.6 = (f32[56,128]{1,0:T(8,128)S(1)}, f32[56,128]{1,0:T(8,128)S(1)}, u32[]{:S(2)}, u32[]{:S(2)}) collective-permute-start(f32[56,128]{1,0:T(8,128)S(1)} %get-tuple-element.57), channel_id=1, source_target_pairs={{32,64},{64,32},{96,128},{128,96},{160,192},{192,160},{224,256},{2... | collective-permute-start | bytes 86024 | tf_op jit(solution)/shard_map/ppermute | solution.py:929
  94.6 1.9 %collective-permute-start.7 = (f32[56,128]{1,0:T(8,128)S(1)}, f32[56,128]{1,0:T(8,128)S(1)}, u32[]{:S(2)}, u32[]{:S(2)}) collective-permute-start(f32[56,128]{1,0:T(8,128)S(1)} %get-tuple-element.58), channel_id=1, source_target_pairs={{0,32},{32,0},{64,96},{96,64},{128,160},{160,128},{192,224},{224,1... | collective-permute-start | bytes 86024 | tf_op jit(solution)/shard_map/ppermute | solution.py:929
  96.5 1.4 %own_rows.1 = (f32[384,384]{1,0:T(8,128)S(1)}, f32[3,48,384]{2,1,0:T(8,128)S(1)}) custom-call(f32[2,16,3,4,128]{4,3,2,1,0:T(4,128)S(1)} %bitcast.9, f32[8,64]{1,0:T(8,128)S(1)} %get-tuple-element.36.filter_ref.refs_5_.refs_3_.refs_1_, f32[32,128]{1,0:T(8,128)S(1)} %copy-done.8, f32[32,128]{1,0:T(8,128)S(1)} %copy-done.7, bf16[2,256,384]{2,1,0:T(8,128)(2,1)S(1)} %copy-done.4, ...), custom_call_target="tpu_custom_call" | custom-call | flops 1000000000 | bytes 2000000 | tf_op jit(solution)/shard_map/own_rows/pallas_call | solution.py:795
  97.9 2.4 %collective-permute-done.7.first_ref = f32[56,128]{1,0:T(8,128)S(1)} collective-permute-done((f32[56,128]{1,0:T(8,128)S(1)}, f32[56,128]{1,0:T(8,128)S(1)}, u32[]{:S(2)}, u32[]{:S(2)}) %collective-permute-start.7) | collective-permute-done | bytes 28704 | tf_op jit(solution)/shard_map/ppermute | solution.py:929
  100.3 1.2 %last_stage.1 = (f32[64,270]{1,0:T(8,128)}, f32[64,270]{1,0:T(8,128)}, f32[64,270]{1,0:T(8,128)}) custom-call(f32[4,72,384]{2,1,0:T(8,128)S(1)} %get-tuple-element.41.refs_5_.wide_ref, f32[64,128]{1,0:T(8,128)S(1)} %get-tuple-element.42.refs_6_.left_ref, f32[64,128]{1,0:T(8,128)S(1)} %get-tuple-element.43.refs_7_.right_ref, ...), custom_call_target="tpu_custom_call" | custom-call | flops 1000000000 | bytes 2000000 | tf_op jit(solution)/shard_map/last_stage/pallas_call | solution.py:795
  (28 shorter events, 0.1 us)
Async XLA Ops:
  0.6 18.9 %copy-start = (f32[128,256]{1,0:T(8,128)S(1)}, f32[128,256]{1,0:T(8,128)}, u32[]{:S(2)}) copy-start(f32[128,256]{1,0:T(8,128)} %values_ref.1) | copy-start | bytes 393220
  0.6 18.9 %copy-start.5 = (bf16[2,384,256]{2,1,0:T(8,128)(2,1)S(1)}, bf16[2,384,256]{2,1,0:T(8,128)(2,1)}, u32[]{:S(2)}) copy-start(bf16[2,384,256]{2,1,0:T(8,128)(2,1)} %constant.22.clone.table_ref.refs_9_) | copy-start | bytes 1179652
  0.7 18.9 %copy-start.7 = (f32[32,128]{1,0:T(8,128)S(1)}, f32[32,128]{1,0:T(8,128)}, u32[]{:S(2)}) copy-start(f32[32,128]{1,0:T(8,128)} %constant.21.clone.sin_ref.refs_8_.refs_3_) | copy-start | bytes 49156
  0.7 18.9 %copy-start.8 = (f32[32,128]{1,0:T(8,128)S(1)}, f32[32,128]{1,0:T(8,128)}, u32[]{:S(2)}) copy-start(f32[32,128]{1,0:T(8,128)} %constant.20.clone.cos_ref.refs_7_.refs_2_) | copy-start | bytes 49156
  2.0 18.4 %collective-permute-start.2 = (f32[16,384]{1,0:T(8,128)S(1)}, f32[16,384]{1,0:T(8,128)S(1)}, u32[]{:S(2)}, u32[]{:S(2)}) collective-permute-start(f32[16,384]{1,0:T(8,128)S(1)} %get-tuple-element.34), channel_id=1, source_target_pairs={{32,64},{64,32},{96,128},{128,96},{160,192},{192,160},{224,256},{2... | collective-permute-start | bytes 73736 | tf_op jit(solution)/shard_map/ppermute | solution.py:859
  5.1 15.3 %collective-permute-start.3 = (f32[16,384]{1,0:T(8,128)S(1)}, f32[16,384]{1,0:T(8,128)S(1)}, u32[]{:S(2)}, u32[]{:S(2)}) collective-permute-start(f32[16,384]{1,0:T(8,128)S(1)} %get-tuple-element.35), channel_id=1, source_target_pairs={{0,32},{32,0},{64,96},{96,64},{128,160},{160,128},{192,224},{224,1... | collective-permute-start | bytes 73736 | tf_op jit(solution)/shard_map/ppermute | solution.py:859
  7.1 13.4 %collective-permute-start = (f32[64,128]{1,0:T(8,128)S(1)}, f32[64,128]{1,0:T(8,128)S(1)}, u32[]{:S(2)}, u32[]{:S(2)}) collective-permute-start(f32[64,128]{1,0:T(8,128)S(1)} %get-tuple-element.32), channel_id=1, source_target_pairs={{0,31},{1,2},{2,1},{3,4},{4,3},{5,6},{6,5},{7,8},{8,7},{9,10},{10,... | collective-permute-start | bytes 98312 | tf_op jit(solution)/shard_map/ppermute | solution.py:862
  17.6 3.1 %collective-permute-start.1 = (f32[64,128]{1,0:T(8,128)S(1)}, f32[64,128]{1,0:T(8,128)S(1)}, u32[]{:S(2)}, u32[]{:S(2)}) collective-permute-start(f32[64,128]{1,0:T(8,128)S(1)} %get-tuple-element.33), channel_id=1, source_target_pairs={{0,1},{1,0},{2,3},{3,2},{4,5},{5,4},{6,7},{7,6},{8,9},{9,8},{10,11... | collective-permute-start | bytes 98312 | tf_op jit(solution)/shard_map/ppermute | solution.py:862
  19.6 1.1 %copy-start.1 = (bf16[2,384,512]{2,1,0:T(8,128)(2,1)S(1)}, bf16[2,384,512]{2,1,0:T(8,128)(2,1)}, u32[]{:S(2)}) copy-start(bf16[2,384,512]{2,1,0:T(8,128)(2,1)} %constant.24.clone.refs_10_) | copy-start | bytes 2359300
  19.6 1.1 %copy-start.6 = (f32[72,128]{1,0:T(8,128)S(1)}, f32[72,128]{1,0:T(8,128)}, u32[]{:S(2)}) copy-start(f32[72,128]{1,0:T(8,128)} %constant.23.clone.refs_6_.refs_10_.terms_ref) | copy-start | bytes 110596
  24.7 43.4 %copy-start.2 = (bf16[2,512,256]{2,1,0:T(8,128)(2,1)S(1)}, bf16[2,512,256]{2,1,0:T(8,128)(2,1)}, u32[]{:S(2)}) copy-start(bf16[2,512,256]{2,1,0:T(8,128)(2,1)} %constant.28.clone.from_grid_ref) | copy-start | bytes 1572868
  24.7 43.4 %copy-start.3 = (bf16[2,256,512]{2,1,0:T(8,128)(2,1)S(1)}, bf16[2,256,512]{2,1,0:T(8,128)(2,1)}, u32[]{:S(2)}) copy-start(bf16[2,256,512]{2,1,0:T(8,128)(2,1)} %constant.27.clone.to_grid_ref) | copy-start | bytes 1572868
  24.8 43.4 %copy-start.9 = (f32[16,256]{1,0:T(8,128)S(1)}, f32[16,256]{1,0:T(8,128)}, u32[]{:S(2)}) copy-start(f32[16,256]{1,0:T(8,128)} %constant.25.clone.lines_ref) | copy-start | bytes 49156
  24.8 43.4 %copy-start.10 = (f32[8,128]{1,0:T(8,128)S(1)}, f32[8,128]{1,0:T(8,128)}, u32[]{:S(2)}) copy-start(f32[8,128]{1,0:T(8,128)} %constant.26.clone.slope_ref) | copy-start | bytes 12292
  69.3 17.9 %all-to-all-start.1 = ((f32[16,3,4,128]{3,2,1,0:T(4,128)}), f32[16,3,4,128]{3,2,1,0:T(4,128)S(1)}, u32[]{:S(2)}, u32[]{:S(2)}) async-start(f32[16,3,4,128]{3,2,1,0:T(4,128)} %own_row.1), calls=%async_computation.1 | async-start | bytes 196608 | tf_op jit(solution)/shard_map/all_to_all | solution.py:911
  73.0 4.4 %collective-permute-start.4 = (f32[32,128]{1,0:T(8,128)S(1)}, f32[32,128]{1,0:T(8,128)S(1)}, u32[]{:S(2)}, u32[]{:S(2)}) collective-permute-start(f32[32,128]{1,0:T(8,128)S(1)} %get-tuple-element.49), channel_id=1, source_target_pairs={{0,1},{1,2},{2,3},{3,4},{4,5},{5,6},{6,7},{7,8},{8,9},{9,10},{10,1... | collective-permute-start | bytes 49160 | tf_op jit(solution)/shard_map/ppermute | solution.py:838
  73.5 15.6 %collective-permute-start.5 = (f32[96,128]{1,0:T(8,128)S(1)}, f32[96,128]{1,0:T(8,128)S(1)}, u32[]{:S(2)}, u32[]{:S(2)}) collective-permute-start(f32[96,128]{1,0:T(8,128)S(1)} %get-tuple-element.51), channel_id=1, source_target_pairs={{0,31},{1,0},{2,1},{3,2},{4,3},{5,4},{6,5},{7,6},{8,7},{9,8},{10,9... | collective-permute-start | bytes 147464 | tf_op jit(solution)/shard_map/ppermute | solution.py:838
  89.1 7.4 %copy-start.4 = (bf16[2,256,384]{2,1,0:T(8,128)(2,1)S(1)}, bf16[2,256,384]{2,1,0:T(8,128)(2,1)}, u32[]{:S(2)}) copy-start(bf16[2,256,384]{2,1,0:T(8,128)(2,1)} %constant.29.clone.refs_4_.table_ref) | copy-start | bytes 1179652
  89.5 8.4 %collective-permute-start.6 = (f32[56,128]{1,0:T(8,128)S(1)}, f32[56,128]{1,0:T(8,128)S(1)}, u32[]{:S(2)}, u32[]{:S(2)}) collective-permute-start(f32[56,128]{1,0:T(8,128)S(1)} %get-tuple-element.57), channel_id=1, source_target_pairs={{32,64},{64,32},{96,128},{128,96},{160,192},{192,160},{224,256},{2... | collective-permute-start | bytes 86024 | tf_op jit(solution)/shard_map/ppermute | solution.py:929
  94.6 5.8 %collective-permute-start.7 = (f32[56,128]{1,0:T(8,128)S(1)}, f32[56,128]{1,0:T(8,128)S(1)}, u32[]{:S(2)}, u32[]{:S(2)}) collective-permute-start(f32[56,128]{1,0:T(8,128)S(1)} %get-tuple-element.58), channel_id=1, source_target_pairs={{0,32},{32,0},{64,96},{96,64},{128,160},{160,128},{192,224},{224,1... | collective-permute-start | bytes 86024 | tf_op jit(solution)/shard_map/ppermute | solution.py:929
